TPU v7x, 128 devices: a whole 4x4x4 slice. The times are simulated.
128 devices in a mesh: tile: 4 (over z), lev: 32 (over y, x, core).
Axes of the slice: x: 4, y: 4, z: 4, core: 2. Of those that a mesh axis runs over, the one named last changes fastest.
Arguments:
- fields: float32 [224, 524288], P('lev', 'tile'), may hold values from -15 to 15
- chan_mean: float32 [224], replicated, may hold values from -6 to 6
- chan_scale: float32 [224], replicated, may hold values from 0.2 to 1
- w_embed_in: bfloat16 [224, 512], replicated, may hold values from -0.375 to 0.375
- b_embed: float32 [512], replicated, may hold values from -6 to 6
- w_embed_out: bfloat16 [512, 512], replicated, may hold values from -0.25 to 0.25
- halo_index: int32 [128, 2, 256], P(('tile', 'lev')), may hold values from 0 to 4095
- local_src: int32 [128, 4096], P(('tile', 'lev')), may hold values from 0 to 4607
- local_dst: int32 [128, 4096], P(('tile', 'lev')), may hold values from -1 to 319, as said below
- remote_src: int32 [128, 32, 16], P(('tile', 'lev')), may hold values from 0 to 4607
- remote_dst: int32 [128, 32, 16], P(('tile', 'lev')), may hold values from -1 to 319, as said below
- w_msg_in: bfloat16 [512, 512], replicated, may hold values from -0.25 to 0.25
- b_msg: float32 [512], replicated, may hold values from -6 to 6
- w_msg_out: bfloat16 [512, 512], replicated, may hold values from -0.25 to 0.25
- mesh_nodes: bfloat16 [40960, 512], P(('tile', 'lev')), may hold values from -6 to 6
- w_node_in: bfloat16 [1024, 512], replicated, may hold values from -0.1875 to 0.1875
- b_node: float32 [512], replicated, may hold values from -6 to 6
- w_node_out: bfloat16 [512, 512], replicated, may hold values from -0.25 to 0.25
Outputs:
- grid_latent: bfloat16 [524288, 512], P(('tile', 'lev'))
- mesh_out: bfloat16 [40960, 512], P(('tile', 'lev'))
Inputs may be any that keep to these rules, and one draw needn't show every extreme that they name: `local_dst`: -1 marks a padding slot; other entries name node n of the block itself. `remote_dst`: -1 marks a padding slot; entry [b, o, s] otherwise names node n of block o of the same tile.
All inputs are finite; a program needn't handle non-finite values.
Results may differ from a plain program's by a relative error of at most 0.0075.
Values may be sent and summed in bfloat16 or wider, within the bound.
No kernel may reach another device: no remote copies, remote signals or barrier semaphores. Data moves between devices by JAX's collectives and lax.ppermute only.
A program may use at most 128 MiB of HBM per device.

v0:
```python
import jax
import jax.numpy as jnp
from jax import lax
from jax.sharding import PartitionSpec as P


def extended(block, sides, width):
    for axis, dim in sides:
        count = lax.axis_size(axis)
        forward = [(i, i + 1) for i in range(count - 1)]
        forward.append((count - 1, 0))
        backward = [(target, source) for source, target in forward]
        low = lax.ppermute(
            lax.slice_in_dim(block, block.shape[dim] - width, None, axis=dim), axis, forward
        )
        high = lax.ppermute(lax.slice_in_dim(block, 0, width, axis=dim), axis, backward)
        block = jnp.concatenate([low, block, high], axis=dim)
    return block


def message(table, sources, w_msg_in, b_msg, w_msg_out):
    rows = jnp.take(table, sources, axis=0)
    pre = jnp.dot(rows, w_msg_in, preferred_element_type=jnp.float32) + b_msg
    act = jax.nn.silu(pre).astype(jnp.bfloat16)
    return jnp.dot(act, w_msg_out, preferred_element_type=jnp.float32)


def node_table(ids, count):
    nodes = jnp.arange(count, dtype=jnp.int32)
    return (ids[..., None] == nodes).astype(jnp.float32)


def shards(
    fields,
    chan_mean,
    chan_scale,
    w_embed_in,
    b_embed,
    w_embed_out,
    halo_index,
    local_src,
    local_dst,
    remote_src,
    remote_dst,
    w_msg_in,
    b_msg,
    w_msg_out,
    mesh_nodes,
    w_node_in,
    b_node,
    w_node_out,
):
    levels = lax.axis_size("lev")
    width = mesh_nodes.shape[1]
    node_count = mesh_nodes.shape[0]
    local_count = local_src.shape[1]
    slot_count = remote_src.shape[2]
    gathered = lax.all_to_all(fields, "lev", split_axis=1, concat_axis=0, tiled=True)
    normed = ((gathered - chan_mean[:, None]) * chan_scale[:, None]).astype(jnp.bfloat16)
    pre = (
        lax.dot_general(
            normed, w_embed_in, (((0,), (0,)), ((), ())), preferred_element_type=jnp.float32
        )
        + b_embed
    )
    hidden = jax.nn.silu(pre).astype(jnp.bfloat16)
    latent = jnp.dot(hidden, w_embed_out, preferred_element_type=jnp.float32).astype(jnp.bfloat16)
    outgoing = jnp.take(latent, halo_index[0], axis=0)
    padded = extended(outgoing, (("tile", 0),), 1)
    table = jnp.concatenate([latent, padded[0], padded[3]], axis=0)
    sources = jnp.concatenate([local_src[0], remote_src[0].reshape(-1)])
    msgs = message(table, sources, w_msg_in, b_msg, w_msg_out)
    near_dst = local_dst[0]
    far_dst = remote_dst[0]
    near_valid = near_dst >= 0
    near_msgs = jnp.where(near_valid[:, None], msgs[:local_count], 0.0)
    far_msgs = msgs[local_count:].reshape(levels, slot_count, width)
    far_valid = far_dst >= 0
    far_msgs = jnp.where(far_valid[:, :, None], far_msgs, 0.0)
    near_onehot = node_table(near_dst, node_count)
    near_sum = lax.dot_general(
        near_onehot,
        near_msgs,
        (((0,), (0,)), ((), ())),
        precision=lax.Precision.HIGHEST,
        preferred_element_type=jnp.float32,
    )
    own_level = lax.axis_index("lev")
    far_onehot = node_table(far_dst, node_count)
    far_sum = jnp.einsum(
        "osn,osw->onw",
        far_onehot,
        far_msgs,
        precision=lax.Precision.HIGHEST,
        preferred_element_type=jnp.float32,
    )
    own_mask = (jnp.arange(levels, dtype=jnp.int32) == own_level).astype(jnp.float32)
    partial_value = far_sum + own_mask[:, None, None] * near_sum[None, :, :]
    summed = lax.psum_scatter(
        partial_value.reshape(levels * node_count, width), "lev", scatter_dimension=0, tiled=True
    )
    summed_b = summed.astype(jnp.bfloat16)
    node_pre = jnp.dot(mesh_nodes, w_node_in[:width], preferred_element_type=jnp.float32)
    node_pre = (
        node_pre + jnp.dot(summed_b, w_node_in[width:], preferred_element_type=jnp.float32) + b_node
    )
    node_act = jax.nn.silu(node_pre).astype(jnp.bfloat16)
    mesh_out = (
        mesh_nodes.astype(jnp.float32)
        + jnp.dot(node_act, w_node_out, preferred_element_type=jnp.float32)
    ).astype(jnp.bfloat16)
    return (latent, mesh_out)


def solution(mesh):
    return jax.shard_map(
        shards,
        mesh=mesh,
        in_specs=(
            P("lev", "tile"),
            P(),
            P(),
            P(),
            P(),
            P(),
            P(("tile", "lev"), None, None),
            P(("tile", "lev"), None),
            P(("tile", "lev"), None),
            P(("tile", "lev"), None, None),
            P(("tile", "lev"), None, None),
            P(),
            P(),
            P(),
            P(("tile", "lev"), None),
            P(),
            P(),
            P(),
        ),
        out_specs=(P(("tile", "lev"), None), P(("tile", "lev"), None)),
        check_vma=False,
    )
```

profile of v0, /device:TPU:1, one launch (start us, length us, event | category | flops | bytes accessed | tf_op | source)
XLA Modules:
  0.0 287.7 jit_solution(15444443365396451290)
XLA Ops:
  7.2 0.0 copy-start
  7.2 0.0 copy-start.6
  7.2 0.0 copy-start.7
  7.2 0.0 copy-start.3
  7.2 0.0 copy-start.4
  7.2 0.0 copy-start.8
  7.2 0.0 copy-start.11
  7.2 0.0 copy-start.12
  7.3 0.0 copy-start.15
  7.3 0.0 copy-start.16
  7.3 8.8 %all-to-all-start = ((f32[7,32,4096]{2,0,1:T(8,128)}), f32[7,32,4096]{2,0,1:T(8,128)}, u32[]{:S(2)}, u32[]{:S(2)}) async-start(f32[7,32,4096]{2,0,1:T(8,128)} %bitcast.28), calls=%async_computation | async-start | bytes 8388608 | tf_op jit(solution)/shard_map/all_to_all | solution.py:58
  16.1 0.0 reduce-scatter.2.cloned.1.call-start
  16.1 0.0 copy-done.6
  16.1 0.1 copy.25
  16.2 0.1 concatenate.42
  16.3 0.1 concatenate.38
  16.4 0.0 copy-done.7
  16.4 0.0 copy-done.3
  16.4 0.1 fusion.26
  16.5 0.0 copy-done.4
  16.5 50.2 %all-to-all-done = f32[7,32,4096]{2,0,1:T(8,128)} async-done(((f32[7,32,4096]{2,0,1:T(8,128)}), f32[7,32,4096]{2,0,1:T(8,128)}, u32[]{:S(2)}, u32[]{:S(2)}) %all-to-all-start) | async-done | bytes 3670048 | tf_op jit(solution)/shard_map/all_to_all | solution.py:58
  66.7 3.7 %all_to_all.17 = f32[224,4096]{1,0:T(8,128)} reshape(f32[32,7,4096]{2,1,0:T(8,128)} %bitcast.1) | data formatting | bytes 7340032 | tf_op jit(solution)/shard_map/all_to_all | solution.py:58
  70.5 0.0 copy-done.8
  70.5 0.0 copy-done.11
  70.5 0.0 copy-done.12
  70.5 0.0 copy-done.15
  70.5 0.0 copy-done.16
  70.5 7.7 %convolution_convert_fusion = bf16[4096,512]{1,0:T(8,128)(2,1)} fusion(bf16[512,512]{1,0:T(8,128)(2,1)S(1)} %copy-done.8, bf16[224,512]{1,0:T(8,128)(2,1)S(1)} %copy-done.11, f32[512]{0:T(512)S(1)} %copy-done.12, f32[224,4096]{1,0:T(8,128)} %all_to_all.17, f32[224]{0:T(256)S(1)} %copy-done.15, f32[224]{0:T(256)S(1)} %copy-done.16), kind=kOutput, calls=%fused_computation.8 | convolution fusion | flops 3104440320 | bytes 8621824 | tf_op jit(solution)/shard_map/dot_general | solution.py:67
  78.2 0.0 copy-start.5
  78.2 4.7 %gather_fusion = bf16[512,512]{1,0:T(8,128)(2,1)S(1)} fusion(bf16[4096,512]{1,0:T(8,128)(2,1)} %convolution_convert_fusion, s32[1024]{0:T(1024)S(1)} %pad_clamp_fusion.1), kind=kCustom, calls=%fused_computation | custom fusion | bytes 1050624 | tf_op jit(solution)/shard_map/jit(_take)/gather | solution.py:68
  83.0 0.1 broadcast_select_fusion
  83.1 1.7 collective-permute-start
  84.8 2.4 collective-permute-start.1
  87.2 0.1 copy.23
  87.3 0.1 copy.24
  87.4 0.0 copy-done.5
  87.4 3.3 %collective-permute-done = bf16[1,256,512]{2,1,0:T(8,128)(2,1)S(1)} collective-permute-done((bf16[1,256,512]{2,1,0:T(8,128)(2,1)S(1)}, bf16[1,256,512]{2,1,0:T(8,128)(2,1)S(1)}, u32[]{:S(2)}, u32[]{:S(2)}) %collective-permute-start) | collective-permute-done | bytes 262176 | tf_op jit(solution)/shard_map/ppermute | solution.py:13
  90.7 0.0 collective-permute-done.1
  90.7 3.9 %pad_maximum_fusion = bf16[4608,512]{1,0:T(8,128)(2,1)} fusion(bf16[256,512]{1,0:T(8,128)(2,1)S(1)} %bitcast.31, bf16[256,512]{1,0:T(8,128)(2,1)S(1)} %bitcast.30, bf16[4096,512]{1,0:T(8,128)(2,1)} %convolution_convert_fusion), kind=kLoop, calls=%fused_computation.9 | loop fusion | flops 14155776 | bytes 9437184 | tf_op jit(solution)/shard_map/concatenate | solution.py:70
  94.6 0.0 copy-start.9
  94.6 0.0 copy-start.13
  94.6 17.0 %gather_fusion.1 = bf16[4608,512]{1,0:T(8,128)(2,1)} fusion(bf16[4608,512]{1,0:T(8,128)(2,1)} %pad_maximum_fusion, s32[5120]{0:T(1024)S(1)} %pad_clamp_fusion), kind=kCustom, calls=%fused_computation.1 | custom fusion | bytes 9455616 | tf_op jit(solution)/shard_map/jit(_take)/gather | solution.py:22
  111.6 0.0 copy-done
  111.6 0.0 copy-done.9
  111.6 0.0 copy-done.13
  111.7 10.6 %fusion.8 = f32[4608,512]{1,0:T(8,128)} fusion(bf16[512,512]{1,0:T(8,128)(2,1)S(1)} %copy-done, bf16[512,512]{1,0:T(8,128)(2,1)S(1)} %copy-done.9, f32[512]{0:T(512)S(1)} %copy-done.13, bf16[4608,512]{1,0:T(8,128)(2,1)} %gather_fusion.1, pred[4608]{0:T(1024)(128)(4,1)S(1)} %compare_and_fusion), kind=kOutput, calls=%fused_computation.17 | convolution fusion | flops 4848353280 | bytes 15211008 | tf_op jit(solution)/shard_map/dot_general | solution.py:25
  122.3 0.0 slice-start
  122.3 10.7 %fusion = f32[320,512]{1,0:T(8,128)S(1)} fusion(f32[4608,512]{1,0:T(8,128)} %fusion.8, pred[4096]{0:T(1024)(128)(4,1)S(1)} %broadcast_compare_fusion, s32[4096]{0:T(1024)S(1)} %bitcast.36), kind=kOutput, calls=%fused_computation.5 | convolution fusion | flops 8056471552 | bytes 9064448 | tf_op jit(solution)/shard_map/dot_general | solution.py:81
  133.0 0.0 slice-done
  133.0 15.2 %multiply_add_fusion = f32[32,320,512]{2,1,0:T(8,128)} fusion(f32[320,512]{1,0:T(8,128)S(1)} %fusion, f32[32]{0:T(128)S(1)} %compare_convert_fusion, f32[32,16,512]{2,1,0:T(8,128)S(1)} %bitcast.27, pred[32,16]{1,0:T(8,128)(4,1)S(1)} %copy.24, s32[32,16]{1,0:T(8,128)S(1)} %copy.23), kind=kOutput, calls=%fused_computation.2 | convolution fusion | flops 1017544704 | bytes 22678144 | tf_op jit(solution)/shard_map/osn,osw->onw/dot_general | solution.py:90
  148.2 0.0 copy-start.1
  148.2 0.0 copy-start.2
  148.2 0.0 copy-start.10
  148.2 0.0 copy-start.14
  148.2 0.0 reduce-scatter.2.cloned.1.call-update
  148.2 0.9 copy-done.1
  149.1 0.4 copy-done.2
  149.5 0.3 fusion.18
  149.8 128.5 %reduce-scatter.2.cloned.1.call-done = f32[320,512]{1,0:T(8,128)} async-done(((f32[10240,512]{1,0:T(8,128)}), f32[320,512]{1,0:T(8,128)}) %reduce-scatter.2.cloned.1.call-update) | async-done | bytes 655376 | tf_op jit(solution)/shard_map/reduce_scatter | solution.py:99
  278.4 0.0 copy-done.10
  278.4 0.0 copy-done.14
  278.4 2.5 fusion.13
  (10 shorter events, 0.1 us)
Async XLA Ops:
  7.2 104.5 %copy-start = (bf16[512,512]{1,0:T(8,128)(2,1)S(1)}, bf16[512,512]{1,0:T(8,128)(2,1)}, u32[]{:S(2)}) copy-start(bf16[512,512]{1,0:T(8,128)(2,1)} %param.31) | copy-start | bytes 1572868
  7.2 8.9 %copy-start.6 = (s32[1,32,16]{1,2,0:T(8,128)S(1)}, s32[1,32,16]{1,2,0:T(8,128)}, u32[]{:S(2)}) copy-start(s32[1,32,16]{1,2,0:T(8,128)} %param.27) | copy-start | bytes 6148
  7.2 9.2 %copy-start.7 = (s32[1,2,256]{2,1,0:T(2,128)S(1)}, s32[1,2,256]{2,1,0:T(2,128)}, u32[]{:S(2)}) copy-start(s32[1,2,256]{2,1,0:T(2,128)} %param.24) | copy-start | bytes 6148
  7.2 9.2 %copy-start.3 = (s32[1,4096]{1,0:T(1,128)S(1)}, s32[1,4096]{1,0:T(1,128)}, u32[]{:S(2)}) copy-start(s32[1,4096]{1,0:T(1,128)} %param.25) | copy-start | bytes 49156
  7.2 9.3 %copy-start.4 = (s32[1,32,16]{1,2,0:T(8,128)S(1)}, s32[1,32,16]{1,2,0:T(8,128)}, u32[]{:S(2)}) copy-start(s32[1,32,16]{1,2,0:T(8,128)} %param.28) | copy-start | bytes 6148
  7.2 63.2 %copy-start.8 = (bf16[512,512]{1,0:T(8,128)(2,1)S(1)}, bf16[512,512]{1,0:T(8,128)(2,1)}, u32[]{:S(2)}) copy-start(bf16[512,512]{1,0:T(8,128)(2,1)} %param.23) | copy-start | bytes 1572868
  7.2 63.2 %copy-start.11 = (bf16[224,512]{1,0:T(8,128)(2,1)S(1)}, bf16[224,512]{1,0:T(8,128)(2,1)}, u32[]{:S(2)}) copy-start(bf16[224,512]{1,0:T(8,128)(2,1)} %param.21) | copy-start | bytes 688132
  7.2 63.2 %copy-start.12 = (f32[512]{0:T(512)S(1)}, f32[512]{0:T(512)}, u32[]{:S(2)}) copy-start(f32[512]{0:T(512)} %param.22) | copy-start | bytes 6148
  7.3 63.2 %copy-start.15 = (f32[224]{0:T(256)S(1)}, f32[224]{0:T(256)}, u32[]{:S(2)}) copy-start(f32[224]{0:T(256)} %param.20) | copy-start | bytes 2692
  7.3 63.2 %copy-start.16 = (f32[224]{0:T(256)S(1)}, f32[224]{0:T(256)}, u32[]{:S(2)}) copy-start(f32[224]{0:T(256)} %param.19) | copy-start | bytes 2692
  7.3 59.5 %all-to-all-start = ((f32[7,32,4096]{2,0,1:T(8,128)}), f32[7,32,4096]{2,0,1:T(8,128)}, u32[]{:S(2)}, u32[]{:S(2)}) async-start(f32[7,32,4096]{2,0,1:T(8,128)} %bitcast.28), calls=%async_computation | async-start | bytes 8388608 | tf_op jit(solution)/shard_map/all_to_all | solution.py:58
  16.1 262.3 %reduce-scatter.2.cloned.1.call-start = ((), (), s32[]{:S(2)}) async-start(), calls=%async_computation.2 | async-start | bytes 21626880 | tf_op jit(solution)/shard_map/reduce_scatter | solution.py:99
  78.2 9.2 %copy-start.5 = (s32[1,4096]{1,0:T(1,128)S(1)}, s32[1,4096]{1,0:T(1,128)}, u32[]{:S(2)}) copy-start(s32[1,4096]{1,0:T(1,128)} %param.26) | copy-start | bytes 49156
  83.1 7.6 %collective-permute-start = (bf16[1,256,512]{2,1,0:T(8,128)(2,1)S(1)}, bf16[1,256,512]{2,1,0:T(8,128)(2,1)S(1)}, u32[]{:S(2)}, u32[]{:S(2)}) collective-permute-start(bf16[1,256,512]{2,1,0:T(8,128)(2,1)S(1)} %get-tuple-element.2), channel_id=1, source_target_pairs={{0,32},{32,64},{64,96},{96,0},{1,33},{33,65},{65,97},{97,1},{2,34}... | collective-permute-start | bytes 786440 | tf_op jit(solution)/shard_map/ppermute | solution.py:13
  84.8 5.9 %collective-permute-start.1 = (bf16[1,256,512]{2,1,0:T(8,128)(2,1)S(1)}, bf16[1,256,512]{2,1,0:T(8,128)(2,1)S(1)}, u32[]{:S(2)}, u32[]{:S(2)}) collective-permute-start(bf16[1,256,512]{2,1,0:T(8,128)(2,1)S(1)} %get-tuple-element.3), channel_id=1, source_target_pairs={{32,0},{64,32},{96,64},{0,96},{33,1},{65,33},{97,65},{1,97},{34,2}... | collective-permute-start | bytes 786440 | tf_op jit(solution)/shard_map/ppermute | solution.py:16
  94.6 17.0 %copy-start.9 = (bf16[512,512]{1,0:T(8,128)(2,1)S(1)}, bf16[512,512]{1,0:T(8,128)(2,1)}, u32[]{:S(2)}) copy-start(bf16[512,512]{1,0:T(8,128)(2,1)} %param.29) | copy-start | bytes 1572868
  94.6 17.0 %copy-start.13 = (f32[512]{0:T(512)S(1)}, f32[512]{0:T(512)}, u32[]{:S(2)}) copy-start(f32[512]{0:T(512)} %param.30) | copy-start | bytes 6148
  122.3 10.7 %slice-start = ((f32[4608,512]{1,0:T(8,128)}), f32[512,512]{1,0:T(8,128)S(1)}, s32[]{:S(2)}) async-start(f32[4608,512]{1,0:T(8,128)} %fusion.8), calls=%async_computation.3 | async-start | bytes 2097152 | tf_op jit(solution)/shard_map/slice | solution.py:77
  148.2 1.0 copy-start.1
  148.2 1.3 copy-start.2
  148.2 130.2 %copy-start.10 = (bf16[512,512]{1,0:T(8,128)(2,1)S(1)}, bf16[512,512]{1,0:T(8,128)(2,1)}, u32[]{:S(2)}) copy-start(bf16[512,512]{1,0:T(8,128)(2,1)} %param.35) | copy-start | bytes 1572868
  148.2 130.2 %copy-start.14 = (f32[512]{0:T(512)S(1)}, f32[512]{0:T(512)}, u32[]{:S(2)}) copy-start(f32[512]{0:T(512)} %param.34) | copy-start | bytes 6148
Sparse Core Ops, SparseCore 0:
  148.3 129.9 reduce-scatter.1
where the time goes:
time: 288 us
  waiting for transfers between devices  182 us (63%)
  matrix products  47 us (16%)
  local copies, waits for them, and re-layouts  27.3 us (9%)
  between operations  14.3 us (5%)
  starting transfers between devices  12.9 us (4%)
  other arithmetic  4.16 us (1%)
    reduce_scatter x1, waiting for transfers between devices, shards(): lax.psum_scatter(partial_value.reshape(levels * node_count, width), 'lev'...  129 us
    all_to_all x1, waiting for transfers between devices, shards(): lax.all_to_all(fields, 'lev', split_axis=1, concat_axis=0, tiled=True)  50.2 us
    gather x1, local copies, waits for them, and re-layouts, message(): rows = jnp.take(table, sources, axis=0)  17 us
    dot_general x1, matrix products, shards(): jnp.einsum('osn,osw->onw', far_onehot, far_msgs, precision=lax.Precision....  15.2 us
    dot_general x1, matrix products, shards(): lax.dot_general(near_onehot, near_msgs, (((0,), (0,)), ((), ())), precisi...  10.7 us
    dot_general x1, matrix products, message(): return jnp.dot(act, w_msg_out, preferred_element_type=jnp.float32)  10.6 us
    all_to_all x1, starting transfers between devices, shards(): lax.all_to_all(fields, 'lev', split_axis=1, concat_axis=0, tiled=True)  8.78 us
    dot_general x1, matrix products, shards(): jnp.dot(hidden, w_embed_out, preferred_element_type=jnp.float32)  7.73 us
  transfers between devices with their start and end apart: 4, of which 3 were waited for; matrix products, arithmetic and copies ran while one was open for 0% of the time, Pallas kernels for 0%

commit v1 on v0

v1 whole, which is shorter than its diff:
```python
import functools

import jax
import jax.numpy as jnp
from jax import lax
from jax.experimental import pallas as pl
from jax.experimental.pallas import tpu as pltpu
from jax.sharding import PartitionSpec as P

BF = jnp.bfloat16
F32 = jnp.float32
NT = (((1,), (1,)), ((), ()))
TN = (((0,), (0,)), ((), ()))
LIMIT = 56 * 1024 * 1024


def params(**kw):
    return pltpu.CompilerParams(vmem_limit_bytes=LIMIT, **kw)


def whole(shape):
    return pl.BlockSpec(shape, lambda *_: (0,) * len(shape))


def cost(flops, nbytes):
    return pl.CostEstimate(flops=int(flops), bytes_accessed=int(nbytes), transcendentals=0)


def dot(a, b, dims=(((1,), (0,)), ((), ()))):
    return lax.dot_general(a, b, dims, preferred_element_type=F32)


def gate(h):
    return h + h * jnp.tanh(h)


def split(v):
    hi = v.astype(BF)
    return hi, (v - hi.astype(F32)).astype(BF)


def pack_kernel(me_ref, mean_ref, scale_ref, x_ref, code_ref, o_ref):
    chans = x_ref.shape[0]
    count, _, pts = o_ref.shape
    base = me_ref[0] * chans
    row = lax.broadcasted_iota(jnp.int32, (chans, 1), 0)
    mean = jnp.zeros((chans, 1), F32)
    scale = jnp.zeros((chans, 1), F32)
    for c in range(chans):
        mean = jnp.where(row == c, mean_ref[base + c], mean)
        scale = jnp.where(row == c, scale_ref[base + c], scale)
    for j in range(count):
        val = (x_ref[:, j * pts : (j + 1) * pts] - mean) * scale
        tail = jnp.concatenate(
            [code_ref[j], jnp.zeros((1, pts - code_ref.shape[2]), F32)], axis=1
        )
        o_ref[j] = jnp.concatenate([val, tail], axis=0).astype(BF)


def pack(me, mean, scale, fields, code, levels):
    chans, points = fields.shape
    pts = points // levels
    per = 4
    smem = pl.BlockSpec(memory_space=pltpu.SMEM)
    return pl.pallas_call(
        pack_kernel,
        grid=(levels // per,),
        in_specs=[
            smem,
            smem,
            smem,
            pl.BlockSpec((chans, per * pts), lambda i: (0, i)),
            pl.BlockSpec((per, 1, code.shape[2]), lambda i: (i, 0, 0)),
        ],
        out_specs=pl.BlockSpec((per, chans + 1, pts), lambda i: (i, 0, 0)),
        out_shape=jax.ShapeDtypeStruct((levels, chans + 1, pts), BF),
        compiler_params=params(),
        cost_estimate=cost(points * 16, points * 48),
        name="pack",
    )(me, mean, scale, fields, code)


def count_kernel(src_ref, dst_ref, o_ref, hot_ref):
    nodes, edges = hot_ref.shape
    tile = o_ref.shape[1]
    chunk = 1024

    @pl.when(pl.program_id(0) == 0)
    def _():
        ids = lax.broadcasted_iota(jnp.int32, (nodes, edges), 0)
        hot_ref[...] = jnp.where(ids == dst_ref[...], 1.0, 0.0).astype(BF)

    rows = lax.broadcasted_iota(jnp.int32, (tile, chunk), 0) + pl.program_id(0) * tile
    acc = jnp.zeros((nodes, tile), F32)
    for c in range(edges // chunk):
        at = slice(c * chunk, (c + 1) * chunk)
        hot = jnp.where(rows == src_ref[:, at], 1.0, 0.0).astype(BF)
        acc = acc + dot(hot_ref[:, at], hot, NT)
    o_ref[...] = acc.astype(BF)


def count_edges(src, dst, nodes, table):
    edges = src.shape[1]
    tile = 512
    return pl.pallas_call(
        count_kernel,
        grid=(table // tile,),
        in_specs=[whole((1, edges)), whole((1, edges))],
        out_specs=pl.BlockSpec((nodes, tile), lambda i: (0, i)),
        out_shape=jax.ShapeDtypeStruct((nodes, table), BF),
        scratch_shapes=[pltpu.VMEM((nodes, edges), BF)],
        compiler_params=params(),
        cost_estimate=cost(2 * nodes * edges * table, nodes * table * 2),
        name="count",
    )(src, dst)


def halo_kernel(x_ref, idx_ref, low_ref, high_ref):
    pts = x_ref.shape[1]
    half = low_ref.shape[1]
    chunk = 1024
    acc = jnp.zeros((x_ref.shape[0], 2 * half), F32)
    for c in range(pts // chunk):
        rows = lax.broadcasted_iota(jnp.int32, (chunk, 2 * half), 0) + c * chunk
        hot = jnp.where(rows == idx_ref[...], 1.0, 0.0).astype(BF)
        acc = acc + dot(x_ref[:, c * chunk : (c + 1) * chunk], hot)
    low_ref[...] = acc[:, :half].astype(BF)
    high_ref[...] = acc[:, half:].astype(BF)


def halo_select(x, idx):
    rows, pts = x.shape
    half = idx.shape[1] // 2
    out = jax.ShapeDtypeStruct((rows, half), BF)
    return pl.pallas_call(
        halo_kernel,
        out_shape=(out, out),
        compiler_params=params(),
        cost_estimate=cost(2 * rows * pts * 2 * half, rows * pts * 2),
        name="halo",
    )(x, idx)


def slots_kernel(x_ref, src_ref, o_ref):
    slots = o_ref.shape[0]
    pts = x_ref.shape[1]
    chunk = 1024
    acc = jnp.zeros(o_ref.shape, F32)
    for c in range(pts // chunk):
        ids = lax.broadcasted_iota(jnp.int32, (slots, chunk), 1) + c * chunk
        hot = jnp.where(ids == src_ref[...], 1.0, 0.0).astype(BF)
        acc = acc + dot(hot, x_ref[:, c * chunk : (c + 1) * chunk], NT)
    o_ref[...] = acc.astype(BF)


def slots_select(x, src):
    rows, pts = x.shape
    slots = src.shape[0]
    return pl.pallas_call(
        slots_kernel,
        out_shape=jax.ShapeDtypeStruct((slots, rows), BF),
        compiler_params=params(),
        cost_estimate=cost(2 * rows * pts * slots, rows * pts * 2),
        name="slots",
    )(x, src)


def slots_halo_kernel(own_ref, low_ref, up_ref, src_ref, o_ref, *, start):
    slots = o_ref.shape[0]
    half = low_ref.shape[1]
    ids = lax.broadcasted_iota(jnp.int32, (slots, half), 1) + start
    low = jnp.where(ids == src_ref[...], 1.0, 0.0).astype(BF)
    up = jnp.where(ids + half == src_ref[...], 1.0, 0.0).astype(BF)
    acc = own_ref[...].astype(F32) + dot(low, low_ref[...], NT) + dot(up, up_ref[...], NT)
    o_ref[...] = acc.astype(BF)


def slots_halo(own, low, up, src, start):
    slots, rows = own.shape
    return pl.pallas_call(
        functools.partial(slots_halo_kernel, start=start),
        out_shape=jax.ShapeDtypeStruct((slots, rows), BF),
        compiler_params=params(),
        cost_estimate=cost(4 * rows * low.shape[1] * slots, slots * rows * 4),
        name="slots_halo",
    )(own, low, up, src)


def latent_of(x, dims, w_in, b_in, w_out):
    hidden = gate(dot(x, w_in, dims) + b_in).astype(BF)
    return dot(hidden, w_out).astype(BF)


def act_of(latent, w_msg, b_msg):
    return gate(dot(latent, w_msg) + b_msg).astype(BF)


def embed_kernel(x_ref, s_ref, w_in, b_in, w_out, w_msg, b_msg, *rest):
    lat_ref, sum_ref = rest[-2:]

    @pl.when(pl.program_id(0) == 0)
    def _():
        if len(rest) == 4:
            sum_ref[...] = rest[1][...]
        else:
            sum_ref[...] = jnp.zeros_like(sum_ref)

    latent = latent_of(x_ref[...], TN, w_in[...], b_in[...], w_out[...])
    lat_ref[...] = latent
    act = act_of(latent, w_msg[...], b_msg[...])
    sum_ref[...] += dot(s_ref[...], act)


def embed(x, counts, weights, first, steps, tile, before=None):
    rows, pts = x.shape
    nodes = counts.shape[0]
    lat = weights[0].shape[1]
    specs = [
        pl.BlockSpec((rows, tile), lambda i: (0, i + first)),
        pl.BlockSpec((nodes, tile), lambda i: (0, i + first)),
    ] + [whole(w.shape) for w in weights]
    args = [x, counts, *weights]
    alias = {}
    if before is not None:
        alias = {len(args): 0}
        args += list(before)
        specs += [pl.BlockSpec(memory_space=pl.ANY), whole((nodes, lat))]
    return pl.pallas_call(
        embed_kernel,
        grid=(steps,),
        in_specs=specs,
        out_specs=[
            pl.BlockSpec((tile, lat), lambda i: (i + first, 0)),
            whole((nodes, lat)),
        ],
        out_shape=(
            jax.ShapeDtypeStruct((pts, lat), BF),
            jax.ShapeDtypeStruct((nodes, lat), F32),
        ),
        input_output_aliases=alias,
        compiler_params=params(),
        cost_estimate=cost(
            2 * steps * tile * lat * (rows + 2 * lat + nodes), steps * tile * (rows + lat) * 2
        ),
        name="embed",
    )(*args)


def halo_act_kernel(low_ref, up_ref, s_ref, w_in, b_in, w_out, w_msg, b_msg, sum_ref, o_ref):
    half = low_ref.shape[1]
    total = sum_ref[...]
    for k, ref in enumerate((low_ref, up_ref)):
        latent = latent_of(ref[...], TN, w_in[...], b_in[...], w_out[...])
        act = act_of(latent, w_msg[...], b_msg[...])
        total = total + dot(s_ref[:, k * half : (k + 1) * half], act)
    o_ref[...] = total


def halo_act(low, up, counts, weights, total, start):
    rows, half = low.shape
    nodes, lat = total.shape
    at = start // (2 * half)
    return pl.pallas_call(
        halo_act_kernel,
        grid=(1,),
        in_specs=[
            whole(low.shape),
            whole(up.shape),
            pl.BlockSpec((nodes, 2 * half), lambda i: (0, at)),
            *[whole(w.shape) for w in weights],
            whole(total.shape),
        ],
        out_specs=whole(total.shape),
        out_shape=jax.ShapeDtypeStruct(total.shape, F32),
        compiler_params=params(),
        cost_estimate=cost(4 * half * lat * (rows + 2 * lat + nodes), 2 * lat * lat * 2),
        name="halo_act",
    )(low, up, counts, *weights, total)


def node_kernel(
    r_ref, dst_ref, w_in, b_in, w_out, w_msg, b_msg, sum_ref, w_mo, mesh_ref, w_na, w_nb, b_n, w_no, o_ref
):
    nodes = sum_ref.shape[0]
    latent = latent_of(r_ref[...], (((1,), (0,)), ((), ())), w_in[...], b_in[...], w_out[...])
    act = act_of(latent, w_msg[...], b_msg[...])
    ids = lax.broadcasted_iota(jnp.int32, (nodes, dst_ref.shape[1]), 0)
    hot = jnp.where(ids == dst_ref[...], 1.0, 0.0).astype(BF)
    hi, lo = split(sum_ref[...] + dot(hot, act))
    summed = (dot(hi, w_mo[...]) + dot(lo, w_mo[...])).astype(BF)
    mesh = mesh_ref[...]
    pre = dot(mesh, w_na[...]) + dot(summed, w_nb[...]) + b_n[...]
    node = gate(pre).astype(BF)
    o_ref[...] = (mesh.astype(F32) + dot(node, w_no[...])).astype(BF)


def node_update(rows, dst, weights, total, w_mo, mesh, w_na, w_nb, b_n, w_no):
    slots = rows.shape[0]
    lat = total.shape[1]
    return pl.pallas_call(
        node_kernel,
        out_shape=jax.ShapeDtypeStruct(mesh.shape, BF),
        compiler_params=params(),
        cost_estimate=cost(6 * slots * lat * lat, 6 * lat * lat * 2),
        name="node",
    )(rows, dst, *weights, total, w_mo, mesh, w_na, w_nb, b_n, w_no)


def shards(
    fields,
    chan_mean,
    chan_scale,
    w_embed_in,
    b_embed,
    w_embed_out,
    halo_index,
    local_src,
    local_dst,
    remote_src,
    remote_dst,
    w_msg_in,
    b_msg,
    w_msg_out,
    mesh_nodes,
    w_node_in,
    b_node,
    w_node_out,
):
    levels = lax.axis_size("lev")
    tiles = lax.axis_size("tile")
    chans, points = fields.shape
    pts = points // levels
    nodes, lat = mesh_nodes.shape
    slot_count = remote_src.shape[2]
    halo = halo_index.shape[2]
    table = pts + 2 * halo
    wide = (chans + 1) * levels

    me = lax.axis_index("lev").astype(jnp.int32).reshape(1)
    code = remote_dst[0] + 1
    code = jnp.concatenate([code // 16, code % 16], axis=1).astype(F32)
    code = jnp.pad(code, ((0, 0), (0, 128 - code.shape[1])))[:, None, :]
    sent = pack(me, chan_mean, chan_scale, fields, code, levels)
    got = lax.all_to_all(sent, "lev", split_axis=0, concat_axis=0, tiled=True)
    x = got.reshape(wide, pts)

    counts = count_edges(local_src, local_dst, nodes, table)
    w_in = jnp.pad((w_embed_in * 0.5).reshape(levels, chans, lat), ((0, 0), (0, 1), (0, 0)))
    weights = (
        w_in.reshape(wide, lat),
        (b_embed * 0.5)[None, :],
        w_embed_out,
        w_msg_in * 0.5,
        (b_msg * 0.5)[None, :],
    )

    low, high = halo_select(x, halo_index.reshape(1, 2 * halo))
    ahead = [(i, (i + 1) % tiles) for i in range(tiles)]
    back = [(t, s) for s, t in ahead]
    from_low = lax.ppermute(high, "tile", ahead)
    from_up = lax.ppermute(low, "tile", back)
    src = remote_src.reshape(-1, 1)
    own = slots_select(x, src)
    rows = slots_halo(own, from_low, from_up, src, pts)
    rows = lax.all_to_all(
        rows.reshape(levels, slot_count, wide), "lev", split_axis=0, concat_axis=0, tiled=True
    ).reshape(levels * slot_count, wide)

    tile = 512
    steps = pts // tile
    part = embed(x, counts, weights, 0, steps // 2, tile)
    latent, total = embed(x, counts, weights, steps // 2, steps - steps // 2, tile, part)
    total = halo_act(from_low, from_up, counts, weights, total, pts)

    back_code = got[:, chans, : 2 * slot_count].astype(jnp.int32)
    dst = back_code[:, :slot_count] * 16 + back_code[:, slot_count:] - 1
    mesh_out = node_update(
        rows,
        dst.reshape(1, -1),
        weights,
        total,
        w_msg_out,
        mesh_nodes,
        w_node_in[:lat] * 0.5,
        w_node_in[lat:] * 0.5,
        (b_node * 0.5)[None, :],
        w_node_out,
    )
    return (latent, mesh_out)


def solution(mesh):
    return jax.shard_map(
        shards,
        mesh=mesh,
        in_specs=(
            P("lev", "tile"),
            P(),
            P(),
            P(),
            P(),
            P(),
            P(("tile", "lev"), None, None),
            P(("tile", "lev"), None),
            P(("tile", "lev"), None),
            P(("tile", "lev"), None, None),
            P(("tile", "lev"), None, None),
            P(),
            P(),
            P(),
            P(("tile", "lev"), None),
            P(),
            P(),
            P(),
        ),
        out_specs=(P(("tile", "lev"), None), P(("tile", "lev"), None)),
        check_vma=False,
    )
```

time: 288 us -> 94.2 us (0.33)
  waiting for transfers between devices: 182 us -> 3.73 us
  Pallas kernels: 0 us -> 55.7 us
  matrix products: 47 us -> 0 us
  local copies, waits for them, and re-layouts: 27.3 us -> 9.6 us
  between operations: 14.3 us -> 0.72 us
  starting transfers between devices: 12.9 us -> 18 us
    reduce_scatter x1 -> x0, waiting for transfers between devices: 129 us -> none  [shards(): lax.psum_scatter(partial_value.reshape(levels * node_count, width), 'lev'...]
    pallas_call x0 -> x9, Pallas kernels: none -> 55.7 us  [the longest x1 16.1 us: count_edges(): pl.pallas_call(count_kernel, grid=(table // tile,), in_specs=[whole((1, e...]
    dot_general x6 -> x0, matrix products: 47 us -> none  [the longest x1 15.2 us: shards(): jnp.einsum('osn,osw->onw', far_onehot, far_msgs, precision=lax.Precision....]
    all_to_all x1 -> x2, waiting for transfers between devices: 50.2 us -> 3.72 us  [the longest x1 3.72 us: shards(): got = lax.all_to_all(sent, 'lev', split_axis=0, concat_axis=0, tiled=True)]
    gather x2 -> x0, local copies, waits for them, and re-layouts: 21.7 us -> none  [the longest x1 17 us: message(): rows = jnp.take(table, sources, axis=0)]
    all_to_all x1 -> x2, starting transfers between devices: 8.78 us -> 14.2 us  [the longest x1 8.72 us: shards(): got = lax.all_to_all(sent, 'lev', split_axis=0, concat_axis=0, tiled=True)]
    mul x0 -> x6, other arithmetic: none -> 5.42 us  [the longest x1 1.89 us: shards(): w_msg_in * 0.5]
    concatenate x1 -> x0, other arithmetic: 3.91 us -> none  [shards(): table = jnp.concatenate([latent, padded[0], padded[3]], axis=0)]
  transfers between devices with their start and end apart: 4 -> 4, of which waited for: 3 -> 1; matrix products, arithmetic and copies ran while one was open for 0% -> 11% of each run, Pallas kernels for 0% -> 41%
where the time goes in v1:
time: 94.2 us; the launch traced here: 93.4 us
  Pallas kernels  55.7 us (59%)
  starting transfers between devices  18 us (19%)
  local copies, waits for them, and re-layouts  9.6 us (10%)
  other arithmetic  5.61 us (6%)
  waiting for transfers between devices  3.73 us (4%)
    pallas_call x1, Pallas kernels, count_edges(): pl.pallas_call(count_kernel, grid=(table // tile,), in_specs=[whole((1, e...  16.1 us
    pallas_call x2, Pallas kernels, embed(): pl.pallas_call(embed_kernel, grid=(steps,), in_specs=specs, out_specs=[pl...  14.4 us
    all_to_all x1, starting transfers between devices, shards(): got = lax.all_to_all(sent, 'lev', split_axis=0, concat_axis=0, tiled=True)  8.72 us
    pallas_call x1, Pallas kernels, pack(): pl.pallas_call(pack_kernel, grid=(levels // per,), in_specs=[smem, smem,...  6.41 us
    all_to_all x1, starting transfers between devices, shards(): lax.all_to_all(rows.reshape(levels, slot_count, wide), 'lev', split_axis=...  5.51 us
    pallas_call x1, Pallas kernels, node_update(): pl.pallas_call(node_kernel, out_shape=jax.ShapeDtypeStruct(mesh.shape, BF...  5.22 us
    unnamed x25, local copies, waits for them, and re-layouts  4.78 us
    pallas_call x1, Pallas kernels, halo_act(): pl.pallas_call(halo_act_kernel, grid=(1,), in_specs=[whole(low.shape), wh...  4.19 us
  transfers between devices with their start and end apart: 4, of which 1 were waited for; matrix products, arithmetic and copies ran while one was open for 11% of the time, Pallas kernels for 41%

profile of v1, /device:TPU:1, one launch (start us, length us, event | category | flops | bytes accessed | tf_op | source)
XLA Modules:
  0.0 93.4 jit_solution(7527294800301948346)
XLA Ops:
  0.6 0.8 copy.31
  1.4 0.1 add_convert_fusion
  1.5 0.6 pad.8
  2.1 0.0 copy-start.5
  2.1 0.0 copy-start.7
  2.1 0.0 copy-start.8
  2.1 0.0 copy-start.9
  2.1 0.0 copy-start.6
  2.1 6.4 %pack.1 = bf16[32,8,4096]{2,1,0:T(8,128)(2,1)} custom-call(s32[1]{0:T(128)} %bitcast.me_ref, f32[224]{0:T(256)} %mean_ref.1, f32[224]{0:T(256)} %scale_ref.1, f32[7,131072]{1,0:T(8,128)} %x_ref.1, f32[32,1,128]{2,1,0:T(1,128)} %bitcast.49), custom_call_target="tpu_custom_call" | custom-call | flops 2097152 | bytes 6291456 | tf_op jit(solution)/shard_map/pack/pallas_call | solution.py:65
  8.6 0.0 copy-start.10
  8.6 0.0 copy-start.2
  8.6 8.7 %all-to-all-start = ((bf16[32,8,4096]{2,1,0:T(8,128)(2,1)}), bf16[32,8,4096]{2,1,0:T(8,128)(2,1)S(1)}, u32[]{:S(2)}, u32[]{:S(2)}) async-start(bf16[32,8,4096]{2,1,0:T(8,128)(2,1)} %pack.1), calls=%async_computation | async-start | bytes 4194304 | tf_op jit(solution)/shard_map/all_to_all | solution.py:344
  17.3 0.0 copy-done.5
  17.3 0.7 broadcast_multiply_fusion.1
  18.0 0.0 copy-done.7
  18.0 0.6 broadcast_multiply_fusion.4
  18.6 0.0 copy-done.8
  18.6 0.6 broadcast_multiply_fusion.3
  19.2 1.0 %reshape.37 = bf16[32,7,512]{2,1,0:T(8,128)(2,1)S(1)} reshape(bf16[224,512]{1,0:T(8,128)(2,1)} %broadcast_multiply_fusion.1) | data formatting | bytes 458752 | tf_op jit(solution)/shard_map/reshape | solution.py:348
  20.2 0.0 copy-done.9
  20.2 0.6 copy.37
  20.8 0.0 copy-done.6
  20.8 0.1 copy.32
  20.9 0.9 reshape.45.src_ref
  21.7 0.8 pad_bitcast_fusion.w_in
  22.5 0.0 copy-done.10
  22.5 0.6 broadcast_multiply_fusion.2
  23.1 1.9 %broadcast_multiply_fusion.w_msg = bf16[512,512]{1,0:T(8,128)(2,1)} fusion(bf16[512,512]{1,0:T(8,128)(2,1)} %param.29), kind=kLoop, calls=%fused_computation.2 | loop fusion | flops 262144 | bytes 1048576 | tf_op jit(solution)/shard_map/mul | solution.py:353
  25.0 0.0 copy-done.2
  25.0 1.1 %slice_multiply_fusion = (bf16[512,512]{1,0:T(8,128)(2,1)}, bf16[512,512]{1,0:T(8,128)(2,1)}) fusion(bf16[1024,512]{1,0:T(8,128)(2,1)S(1)} %copy-done.2), kind=kLoop, calls=%fused_computation | loop fusion | flops 524288 | bytes 2097152 | tf_op jit(solution)/shard_map/mul | solution.py:385
  26.1 16.1 %count.1.s_ref = bf16[320,4608]{1,0:T(8,128)(2,1)} custom-call(s32[1,4096]{1,0:T(1,128)} %src_ref.1, s32[1,4096]{1,0:T(1,128)} %dst_ref.1), custom_call_target="tpu_custom_call" | custom-call | flops 12079595520 | bytes 2949120 | tf_op jit(solution)/shard_map/count/pallas_call | solution.py:105
  42.2 3.7 %all-to-all-done = bf16[32,8,4096]{2,1,0:T(8,128)(2,1)S(1)} async-done(((bf16[32,8,4096]{2,1,0:T(8,128)(2,1)}), bf16[32,8,4096]{2,1,0:T(8,128)(2,1)S(1)}, u32[]{:S(2)}, u32[]{:S(2)}) %all-to-all-start) | async-done | bytes 2097184 | tf_op jit(solution)/shard_map/all_to_all | solution.py:344
  45.9 0.0 copy-start
  45.9 1.3 %copy-done = bf16[32,8,4096]{2,1,0:T(8,128)(2,1)} copy-done((bf16[32,8,4096]{2,1,0:T(8,128)(2,1)}, bf16[32,8,4096]{2,1,0:T(8,128)(2,1)S(1)}, u32[]{:S(2)}) %copy-start) | copy-done | bytes 2097176
  47.2 3.6 %halo.1 = (bf16[256,256]{1,0:T(8,128)(2,1)}, bf16[256,256]{1,0:T(8,128)(2,1)}) custom-call(bf16[256,4096]{1,0:T(8,128)(2,1)} %bitcast.43, s32[1,512]{1,0:T(1,128)} %bitcast.60), custom_call_target="tpu_custom_call" | custom-call | flops 1073741824 | bytes 2097152 | tf_op jit(solution)/shard_map/halo/pallas_call | solution.py:135
  50.8 1.6 %collective-permute-start = (bf16[256,256]{1,0:T(8,128)(2,1)}, bf16[256,256]{1,0:T(8,128)(2,1)S(1)}, u32[]{:S(2)}, u32[]{:S(2)}) collective-permute-start(bf16[256,256]{1,0:T(8,128)(2,1)} %get-tuple-element.11), channel_id=1, source_target_pairs={{0,32},{32,64},{64,96},{96,0},{1,33},{33,65},{65,97},{97,1},{2,34}... | collective-permute-start | bytes 393224 | tf_op jit(solution)/shard_map/ppermute | solution.py:360
  52.4 2.1 %collective-permute-start.1 = (bf16[256,256]{1,0:T(8,128)(2,1)}, bf16[256,256]{1,0:T(8,128)(2,1)S(1)}, u32[]{:S(2)}, u32[]{:S(2)}) collective-permute-start(bf16[256,256]{1,0:T(8,128)(2,1)} %get-tuple-element.12), channel_id=1, source_target_pairs={{32,0},{64,32},{96,64},{0,96},{33,1},{65,33},{97,65},{1,97},{34,2}... | collective-permute-start | bytes 393224 | tf_op jit(solution)/shard_map/ppermute | solution.py:361
  54.6 0.9 slice.20
  55.4 7.1 %embed.2 = (bf16[4096,512]{1,0:T(8,128)(2,1)}, f32[320,512]{1,0:T(8,128)}) custom-call(bf16[256,4096]{1,0:T(8,128)(2,1)} %bitcast.44, bf16[320,4608]{1,0:T(8,128)(2,1)} %count.1.s_ref, bf16[256,512]{1,0:T(8,128)(2,1)} %pad_bitcast_fusion.w_in, f32[1,512]{1,0:T(1,128)} %bitcast.50, bf16[512,512]{1,0:T(8,128)(2,1)} %w_out.7, ...), custom_call_target="tpu_custom_call" | custom-call | flops 3355443200 | bytes 3145728 | tf_op jit(solution)/shard_map/embed/pallas_call | solution.py:228
  62.5 0.1 fusion
  62.6 0.7 reshape.43.dst_ref
  63.3 3.6 %slots.1.own_ref = bf16[512,256]{1,0:T(8,128)(2,1)} custom-call(bf16[256,4096]{1,0:T(8,128)(2,1)} %bitcast.45, s32[512,1]{1,0:T(8,128)} %reshape.45.src_ref), custom_call_target="tpu_custom_call" | custom-call | flops 1073741824 | bytes 2097152 | tf_op jit(solution)/shard_map/slots/pallas_call | solution.py:159
  66.9 0.0 collective-permute-done.low_ref
  66.9 0.0 copy-start.3
  66.9 0.0 collective-permute-done.1.up_ref
  66.9 0.6 copy-done.3
  67.5 0.0 copy-start.4
  67.5 0.6 copy-done.4
  68.2 2.2 %slots_halo.1 = bf16[512,256]{1,0:T(8,128)(2,1)} custom-call(bf16[512,256]{1,0:T(8,128)(2,1)} %slots.1.own_ref, bf16[256,256]{1,0:T(8,128)(2,1)} %copy-done.3, bf16[256,256]{1,0:T(8,128)(2,1)} %copy-done.4, s32[512,1]{1,0:T(8,128)} %reshape.45.src_ref), custom_call_target="tpu_custom_call" | custom-call | flops 134217728 | bytes 524288 | tf_op jit(solution)/shard_map/slots_halo/pallas_call | solution.py:180
  70.4 5.5 %all-to-all-start.1 = ((bf16[32,16,256]{2,1,0:T(8,128)(2,1)}), bf16[32,16,256]{2,1,0:T(8,128)(2,1)S(1)}, u32[]{:S(2)}, u32[]{:S(2)}) async-start(bf16[32,16,256]{2,1,0:T(8,128)(2,1)} %bitcast.48), calls=%async_computation.1 | async-start | bytes 524288 | tf_op jit(solution)/shard_map/all_to_all | solution.py:365
  76.0 7.3 %embed.3 = (bf16[4096,512]{1,0:T(8,128)(2,1)}, f32[320,512]{1,0:T(8,128)}) custom-call(bf16[256,4096]{1,0:T(8,128)(2,1)} %bitcast.46, bf16[320,4608]{1,0:T(8,128)(2,1)} %count.1.s_ref, bf16[256,512]{1,0:T(8,128)(2,1)} %pad_bitcast_fusion.w_in, f32[1,512]{1,0:T(1,128)} %bitcast.51, bf16[512,512]{1,0:T(8,128)(2,1)} %w_out.7, ...), custom_call_target="tpu_custom_call", output_to_operand_aliasing={{0}: (7, {})} | custom-call | flops 3355443200 | bytes 3145728 | tf_op jit(solution)/shard_map/embed/pallas_call | solution.py:228
  83.3 4.2 %halo_act.1.sum_ref = f32[320,512]{1,0:T(8,128)} custom-call(bf16[256,256]{1,0:T(8,128)(2,1)} %copy-done.3, bf16[256,256]{1,0:T(8,128)(2,1)} %copy-done.4, bf16[320,4608]{1,0:T(8,128)(2,1)} %count.1.s_ref, bf16[256,512]{1,0:T(8,128)(2,1)} %pad_bitcast_fusion.w_in, f32[1,512]{1,0:T(1,128)} %bitcast.52, bf16[512,512]{1,0:T(8,128)(2,1)} %w_out.7, ...), custom_call_target="tpu_custom_call" | custom-call | flops 838860800 | bytes 1048576 | tf_op jit(solution)/shard_map/halo_act/pallas_call | solution.py:263
  87.4 0.0 all-to-all-done.1
  87.5 0.0 copy-start.1
  87.5 0.7 copy-done.1
  88.2 5.2 %node.1 = bf16[320,512]{1,0:T(8,128)(2,1)} custom-call(bf16[512,256]{1,0:T(8,128)(2,1)} %bitcast.47, s32[1,512]{1,0:T(1,128)} %reshape.43.dst_ref, bf16[256,512]{1,0:T(8,128)(2,1)} %pad_bitcast_fusion.w_in, f32[1,512]{1,0:T(1,128)} %bitcast.53, bf16[512,512]{1,0:T(8,128)(2,1)} %w_out.7, bf16[512,512]{1,0:T(8,128)(2,1)} %broadcast_multiply_fusion.w_msg, ...), custom_call_target="tpu_custom_call" | custom-call | flops 805306368 | bytes 3145728 | tf_op jit(solution)/shard_map/node/pallas_call | solution.py:300
  (2 shorter events, 0.0 us)
Async XLA Ops:
  2.1 15.2 %copy-start.5 = (bf16[224,512]{1,0:T(8,128)(2,1)S(1)}, bf16[224,512]{1,0:T(8,128)(2,1)}, u32[]{:S(2)}) copy-start(bf16[224,512]{1,0:T(8,128)(2,1)} %param.21) | copy-start | bytes 688132
  2.1 15.9 %copy-start.7 = (f32[512]{0:T(512)S(1)}, f32[512]{0:T(512)}, u32[]{:S(2)}) copy-start(f32[512]{0:T(512)} %param.22) | copy-start | bytes 6148
  2.1 16.5 %copy-start.8 = (f32[512]{0:T(512)S(1)}, f32[512]{0:T(512)}, u32[]{:S(2)}) copy-start(f32[512]{0:T(512)} %param.30) | copy-start | bytes 6148
  2.1 18.1 %copy-start.9 = (s32[1,2,256]{2,1,0:T(2,128)S(1)}, s32[1,2,256]{2,1,0:T(2,128)}, u32[]{:S(2)}) copy-start(s32[1,2,256]{2,1,0:T(2,128)} %param.24) | copy-start | bytes 6148
  2.1 18.7 %copy-start.6 = (s32[1,32,16]{1,2,0:T(8,128)S(1)}, s32[1,32,16]{1,2,0:T(8,128)}, u32[]{:S(2)}) copy-start(s32[1,32,16]{1,2,0:T(8,128)} %param.27) | copy-start | bytes 6148
  8.6 14.0 %copy-start.10 = (f32[512]{0:T(512)S(1)}, f32[512]{0:T(512)}, u32[]{:S(2)}) copy-start(f32[512]{0:T(512)} %param.34) | copy-start | bytes 6148
  8.6 16.5 %copy-start.2 = (bf16[1024,512]{1,0:T(8,128)(2,1)S(1)}, bf16[1024,512]{1,0:T(8,128)(2,1)}, u32[]{:S(2)}) copy-start(bf16[1024,512]{1,0:T(8,128)(2,1)} %param.33) | copy-start | bytes 3145732
  8.6 37.3 %all-to-all-start = ((bf16[32,8,4096]{2,1,0:T(8,128)(2,1)}), bf16[32,8,4096]{2,1,0:T(8,128)(2,1)S(1)}, u32[]{:S(2)}, u32[]{:S(2)}) async-start(bf16[32,8,4096]{2,1,0:T(8,128)(2,1)} %pack.1), calls=%async_computation | async-start | bytes 4194304 | tf_op jit(solution)/shard_map/all_to_all | solution.py:344
  45.9 1.3 %copy-start = (bf16[32,8,4096]{2,1,0:T(8,128)(2,1)}, bf16[32,8,4096]{2,1,0:T(8,128)(2,1)S(1)}, u32[]{:S(2)}) copy-start(bf16[32,8,4096]{2,1,0:T(8,128)(2,1)S(1)} %all-to-all-done) | copy-start | bytes 6291460
  50.8 16.1 %collective-permute-start = (bf16[256,256]{1,0:T(8,128)(2,1)}, bf16[256,256]{1,0:T(8,128)(2,1)S(1)}, u32[]{:S(2)}, u32[]{:S(2)}) collective-permute-start(bf16[256,256]{1,0:T(8,128)(2,1)} %get-tuple-element.11), channel_id=1, source_target_pairs={{0,32},{32,64},{64,96},{96,0},{1,33},{33,65},{65,97},{97,1},{2,34}... | collective-permute-start | bytes 393224 | tf_op jit(solution)/shard_map/ppermute | solution.py:360
  52.4 14.5 %collective-permute-start.1 = (bf16[256,256]{1,0:T(8,128)(2,1)}, bf16[256,256]{1,0:T(8,128)(2,1)S(1)}, u32[]{:S(2)}, u32[]{:S(2)}) collective-permute-start(bf16[256,256]{1,0:T(8,128)(2,1)} %get-tuple-element.12), channel_id=1, source_target_pairs={{32,0},{64,32},{96,64},{0,96},{33,1},{65,33},{97,65},{1,97},{34,2}... | collective-permute-start | bytes 393224 | tf_op jit(solution)/shard_map/ppermute | solution.py:361
  66.9 0.6 copy-start.3
  67.5 0.6 copy-start.4
  70.4 17.0 %all-to-all-start.1 = ((bf16[32,16,256]{2,1,0:T(8,128)(2,1)}), bf16[32,16,256]{2,1,0:T(8,128)(2,1)S(1)}, u32[]{:S(2)}, u32[]{:S(2)}) async-start(bf16[32,16,256]{2,1,0:T(8,128)(2,1)} %bitcast.48), calls=%async_computation.1 | async-start | bytes 524288 | tf_op jit(solution)/shard_map/all_to_all | solution.py:365
  87.5 0.7 copy-start.1

commit v2 on v0

v2 whole, which is shorter than its diff:
```python
import functools

import jax
import jax.numpy as jnp
from jax import lax
from jax.experimental import pallas as pl
from jax.experimental.pallas import tpu as pltpu
from jax.sharding import PartitionSpec as P

BF = jnp.bfloat16
F32 = jnp.float32
NT = (((1,), (1,)), ((), ()))
TN = (((0,), (0,)), ((), ()))
MIB = 1024 * 1024


def params(mib, **kw):
    return pltpu.CompilerParams(vmem_limit_bytes=mib * MIB, **kw)


def whole(shape):
    return pl.BlockSpec(shape, lambda *_: (0,) * len(shape))


def cost(flops, nbytes):
    return pl.CostEstimate(flops=int(flops), bytes_accessed=int(nbytes), transcendentals=0)


def dot(a, b, dims=(((1,), (0,)), ((), ()))):
    return lax.dot_general(a, b, dims, preferred_element_type=F32)


def silu(v):
    h = 0.5 * v
    return (h + h * jnp.tanh(h)).astype(BF)


def hot(ids, index):
    return jnp.where(ids == index, 1.0, 0.0).astype(BF)


def pack_kernel(me_ref, mean_ref, scale_ref, x_ref, o_ref, in_buf, out_buf, in_sem, out_sem, *, parts):
    chans, points = in_buf.shape
    levels, _, pts = out_buf.shape
    per = levels // parts
    width = per * pts

    def load(k):
        at = pl.ds(k * width, width)
        return pltpu.make_async_copy(x_ref.at[:, at], in_buf.at[:, at], in_sem.at[k])

    def store(k):
        at = pl.ds(k * per, per)
        return pltpu.make_async_copy(out_buf.at[at], o_ref.at[at], out_sem.at[k])

    for k in range(parts):
        load(k).start()
    base = me_ref[0] * chans
    row = lax.broadcasted_iota(jnp.int32, (chans, 1), 0)
    mean = jnp.zeros((chans, 1), F32)
    scale = jnp.zeros((chans, 1), F32)
    for c in range(chans):
        mean = jnp.where(row == c, mean_ref[base + c], mean)
        scale = jnp.where(row == c, scale_ref[base + c], scale)
    pad = jnp.zeros((1, pts), F32)
    for k in range(parts):
        load(k).wait()
        for j in range(k * per, (k + 1) * per):
            val = (in_buf[:, j * pts : (j + 1) * pts] - mean) * scale
            out_buf[j] = jnp.concatenate([val, pad], axis=0).astype(BF)
        store(k).start()
    for k in range(parts):
        store(k).wait()


def pack(me, mean, scale, fields, levels):
    chans, points = fields.shape
    pts = points // levels
    parts = 8
    smem = pl.BlockSpec(memory_space=pltpu.SMEM)
    shape = (levels, chans + 1, pts)
    return pl.pallas_call(
        functools.partial(pack_kernel, parts=parts),
        in_specs=[smem, smem, smem, pl.BlockSpec(memory_space=pl.ANY)],
        out_specs=pl.BlockSpec(memory_space=pl.ANY),
        out_shape=jax.ShapeDtypeStruct(shape, BF),
        scratch_shapes=[
            pltpu.VMEM(fields.shape, F32),
            pltpu.VMEM(shape, BF),
            pltpu.SemaphoreType.DMA((parts,)),
            pltpu.SemaphoreType.DMA((parts,)),
        ],
        compiler_params=params(60),
        cost_estimate=cost(points * 16, points * 48),
        name="pack",
    )(me, mean, scale, fields)


def count_kernel(src_ref, dst_ref, w_ref, mesh_ref, w_na, b_n, o_ref, w_in_ref, pre_ref, hot_ref, *, chans):
    nodes, edges = hot_ref.shape
    tile = o_ref.shape[1]
    chunk = 1024

    @pl.when(pl.program_id(0) == 0)
    def _():
        ids = lax.broadcasted_iota(jnp.int32, (nodes, edges), 0)
        hot_ref[...] = hot(ids, dst_ref[...])
        shape = (w_in_ref.shape[0], w_ref.shape[0])
        row = lax.broadcasted_iota(jnp.int32, shape, 0)
        col = lax.broadcasted_iota(jnp.int32, shape, 1)
        lane = row % (chans + 1)
        place = jnp.where(lane < chans, row // (chans + 1) * chans + lane, -1)
        w_in_ref[...] = dot(hot(col, place), w_ref[...]).astype(BF)
        pre_ref[...] = dot(mesh_ref[...], w_na[...]) + b_n[...]

    rows = lax.broadcasted_iota(jnp.int32, (tile, chunk), 0) + pl.program_id(0) * tile
    acc = jnp.zeros((nodes, tile), F32)
    for c in range(edges // chunk):
        at = slice(c * chunk, (c + 1) * chunk)
        acc = acc + dot(hot_ref[:, at], hot(rows, src_ref[:, at]), NT)
    o_ref[...] = acc.astype(BF)


def count_edges(src, dst, w_in, mesh, w_node, b_node, table, wide, chans):
    edges = src.shape[1]
    nodes, lat = mesh.shape
    tile = 512
    return pl.pallas_call(
        functools.partial(count_kernel, chans=chans),
        grid=(table // tile,),
        in_specs=[
            whole((1, edges)),
            whole((1, edges)),
            whole(w_in.shape),
            whole(mesh.shape),
            whole((lat, lat)),
            whole((1, lat)),
        ],
        out_specs=[
            pl.BlockSpec((nodes, tile), lambda i: (0, i)),
            whole((wide, lat)),
            whole((nodes, lat)),
        ],
        out_shape=(
            jax.ShapeDtypeStruct((nodes, table), BF),
            jax.ShapeDtypeStruct((wide, lat), BF),
            jax.ShapeDtypeStruct((nodes, lat), F32),
        ),
        scratch_shapes=[pltpu.VMEM((nodes, edges), BF)],
        compiler_params=params(28),
        cost_estimate=cost(2 * nodes * edges * table, nodes * table * 2),
        name="count",
    )(src, dst, w_in, mesh, w_node, b_node)


def select_kernel(x_ref, idx_ref, src_ref, low_ref, high_ref, own_ref):
    pts = x_ref.shape[1]
    half = low_ref.shape[1]
    chunk = 1024
    near = jnp.zeros((x_ref.shape[0], 2 * half), F32)
    far = jnp.zeros(own_ref.shape, F32)
    for c in range(pts // chunk):
        x = x_ref[:, c * chunk : (c + 1) * chunk]
        rows = lax.broadcasted_iota(jnp.int32, (chunk, 2 * half), 0) + c * chunk
        near = near + dot(x, hot(rows, idx_ref[...]))
        rows = lax.broadcasted_iota(jnp.int32, (chunk, far.shape[1]), 0) + c * chunk
        far = far + dot(x, hot(rows, src_ref[...]))
    low_ref[...] = near[:, :half].astype(BF)
    high_ref[...] = near[:, half:].astype(BF)
    own_ref[...] = far.astype(BF)


def select(x, idx, src):
    rows, pts = x.shape
    half = idx.shape[1] // 2
    slots = src.shape[1]
    out = jax.ShapeDtypeStruct((rows, half), BF)
    return pl.pallas_call(
        select_kernel,
        out_shape=(out, out, jax.ShapeDtypeStruct((rows, slots), BF)),
        compiler_params=params(24),
        cost_estimate=cost(2 * rows * pts * (2 * half + slots), rows * pts * 2),
        name="select",
    )(x, idx, src)


def slots_kernel(own_ref, low_ref, up_ref, src_ref, dst_ref, o_ref, *, start, pad):
    half = low_ref.shape[1]
    shape = (half, own_ref.shape[1])
    ids = lax.broadcasted_iota(jnp.int32, shape, 0) + start
    acc = own_ref[...].astype(F32)
    acc = acc + dot(low_ref[...], hot(ids, src_ref[...]))
    acc = acc + dot(up_ref[...], hot(ids + half, src_ref[...]))
    code = dst_ref[...] + 1
    row = lax.broadcasted_iota(jnp.int32, acc.shape, 0)
    acc = jnp.where(row == pad, (code // 16).astype(F32), acc)
    acc = jnp.where(row == 2 * pad + 1, (code % 16).astype(F32), acc)
    o_ref[...] = acc.T.astype(BF)


def slots_rows(own, low, up, src, dst, start, pad):
    rows, slots = own.shape
    return pl.pallas_call(
        functools.partial(slots_kernel, start=start, pad=pad),
        out_shape=jax.ShapeDtypeStruct((slots, rows), BF),
        compiler_params=params(16),
        cost_estimate=cost(4 * rows * low.shape[1] * slots, slots * rows * 4),
        name="slots",
    )(own, low, up, src, dst)


def act_of(x, dims, w_in, b_in, w_out, w_msg, b_msg):
    hidden = silu(dot(x, w_in[...], dims) + b_in[...])
    latent = dot(hidden, w_out[...]).astype(BF)
    return latent, silu(dot(latent, w_msg[...]) + b_msg[...])


def first_kernel(x_ref, s_ref, *rest):
    lat_ref, sum_ref = rest[-2:]
    latent, act = act_of(x_ref[...], TN, *rest[:5])
    lat_ref[...] = latent

    @pl.when(pl.program_id(0) == 0)
    def _():
        sum_ref[...] = jnp.zeros_like(sum_ref)

    sum_ref[...] += dot(s_ref[...], act)


def second_kernel(x_ref, s_ref, low_ref, up_ref, s_halo, *rest):
    lat_ref, sum_ref = rest[-2:]
    half = low_ref.shape[1]

    @pl.when(pl.program_id(0) == 0)
    def _():
        total = rest[6][...]
        for k, ref in enumerate((low_ref, up_ref)):
            _, act = act_of(ref[...], TN, *rest[:5])
            total = total + dot(s_halo[:, k * half : (k + 1) * half], act)
        sum_ref[...] = total

    latent, act = act_of(x_ref[...], TN, *rest[:5])
    lat_ref[...] = latent
    sum_ref[...] += dot(s_ref[...], act)


def embed(x, counts, weights, first, steps, tile, before=None):
    rows, pts = x.shape
    nodes = counts.shape[0]
    lat = weights[0].shape[1]
    specs = [
        pl.BlockSpec((rows, tile), lambda i: (0, i + first)),
        pl.BlockSpec((nodes, tile), lambda i: (0, i + first)),
    ]
    args = [x, counts]
    alias = {}
    if before is not None:
        latent, total, low, up = before
        both = 2 * low.shape[1]
        specs += [whole(low.shape), whole(up.shape)]
        specs += [pl.BlockSpec((nodes, both), lambda i: (0, pts // both))]
        args += [low, up, counts]
    specs += [whole(w.shape) for w in weights]
    args += weights
    if before is not None:
        alias = {len(args): 0}
        args += [latent, total]
        specs += [pl.BlockSpec(memory_space=pl.ANY), whole((nodes, lat))]
    return pl.pallas_call(
        first_kernel if before is None else second_kernel,
        grid=(steps,),
        in_specs=specs,
        out_specs=[
            pl.BlockSpec((tile, lat), lambda i: (i + first, 0)),
            whole((nodes, lat)),
        ],
        out_shape=(
            jax.ShapeDtypeStruct((pts, lat), BF),
            jax.ShapeDtypeStruct((nodes, lat), F32),
        ),
        input_output_aliases=alias,
        compiler_params=params(28),
        cost_estimate=cost(
            2 * steps * tile * lat * (rows + 2 * lat + nodes), steps * tile * (rows + lat) * 2
        ),
        name="embed",
    )(*args)


def node_kernel(r_ref, w_in, b_in, w_out, w_msg, b_msg, sum_ref, w_mo, mesh_ref, pre_ref, w_nb, w_no, o_ref, *, pad):
    nodes = sum_ref.shape[0]
    rows = r_ref[...]
    _, act = act_of(rows, (((1,), (0,)), ((), ())), w_in, b_in, w_out, w_msg, b_msg)
    lane = lax.broadcasted_iota(jnp.int32, (8, rows.shape[1]), 1)
    pick = jnp.where(lane == pad, 16.0, jnp.where(lane == 2 * pad + 1, 1.0, 0.0)).astype(BF)
    dst = dot(pick, rows, NT)[:1].astype(jnp.int32) - 1
    ids = lax.broadcasted_iota(jnp.int32, (nodes, rows.shape[0]), 0)
    total = sum_ref[...] + dot(hot(ids, dst), act)
    high = total.astype(BF)
    rest = (total - high.astype(F32)).astype(BF)
    summed = (dot(high, w_mo[...]) + dot(rest, w_mo[...])).astype(BF)
    node = silu(pre_ref[...] + dot(summed, w_nb[...]))
    o_ref[...] = (mesh_ref[...].astype(F32) + dot(node, w_no[...])).astype(BF)


def node_update(rows, weights, total, w_mo, mesh, pre, w_node, w_no, pad):
    nodes, lat = mesh.shape
    slots = rows.shape[0]
    args = [rows, *weights, total, w_mo, mesh, pre]
    return pl.pallas_call(
        functools.partial(node_kernel, pad=pad),
        grid=(1,),
        in_specs=[whole(a.shape) for a in args]
        + [pl.BlockSpec((lat, lat), lambda i: (1, 0)), whole(w_no.shape)],
        out_specs=whole(mesh.shape),
        out_shape=jax.ShapeDtypeStruct(mesh.shape, BF),
        compiler_params=params(24),
        cost_estimate=cost(6 * slots * lat * lat, 6 * lat * lat * 2),
        name="node",
    )(*args, w_node, w_no)


def shards(
    fields,
    chan_mean,
    chan_scale,
    w_embed_in,
    b_embed,
    w_embed_out,
    halo_index,
    local_src,
    local_dst,
    remote_src,
    remote_dst,
    w_msg_in,
    b_msg,
    w_msg_out,
    mesh_nodes,
    w_node_in,
    b_node,
    w_node_out,
):
    levels = lax.axis_size("lev")
    tiles = lax.axis_size("tile")
    chans, points = fields.shape
    pts = points // levels
    slot_count = remote_src.shape[2]
    halo = halo_index.shape[2]
    table = pts + 2 * halo
    wide = (chans + 1) * levels

    me = lax.axis_index("lev").astype(jnp.int32).reshape(1)
    sent = pack(me, chan_mean, chan_scale, fields, levels)
    got = lax.all_to_all(sent, "lev", split_axis=0, concat_axis=0, tiled=True)
    x = got.reshape(wide, pts)

    counts, w_in, pre = count_edges(
        local_src, local_dst, w_embed_in, mesh_nodes, w_node_in, b_node[None, :], table, wide, chans
    )
    weights = [w_in, b_embed[None, :], w_embed_out, w_msg_in, b_msg[None, :]]

    src = remote_src.reshape(1, -1)
    dst = remote_dst.reshape(1, -1)
    low, high, own = select(x, halo_index.reshape(1, 2 * halo), src)
    ahead = [(i, (i + 1) % tiles) for i in range(tiles)]
    back = [(t, s) for s, t in ahead]
    from_low = lax.ppermute(high, "tile", ahead)
    from_up = lax.ppermute(low, "tile", back)

    tile = 512
    steps = pts // tile
    latent, total = embed(x, counts, weights, 0, steps // 2, tile)

    rows = slots_rows(own, from_low, from_up, src, dst, pts, chans)
    rows = lax.all_to_all(
        rows.reshape(levels, slot_count, wide), "lev", split_axis=0, concat_axis=0, tiled=True
    ).reshape(levels * slot_count, wide)

    latent, total = embed(
        x, counts, weights, steps // 2, steps - steps // 2, tile, (latent, total, from_low, from_up)
    )
    mesh_out = node_update(
        rows, weights, total, w_msg_out, mesh_nodes, pre, w_node_in, w_node_out, chans
    )
    return (latent, mesh_out)


def solution(mesh):
    return jax.shard_map(
        shards,
        mesh=mesh,
        in_specs=(
            P("lev", "tile"),
            P(),
            P(),
            P(),
            P(),
            P(),
            P(("tile", "lev"), None, None),
            P(("tile", "lev"), None),
            P(("tile", "lev"), None),
            P(("tile", "lev"), None, None),
            P(("tile", "lev"), None, None),
            P(),
            P(),
            P(),
            P(("tile", "lev"), None),
            P(),
            P(),
            P(),
        ),
        out_specs=(P(("tile", "lev"), None), P(("tile", "lev"), None)),
        check_vma=False,
    )
```

time: 288 us -> 93.4 us (0.32)
  waiting for transfers between devices: 182 us -> 9.17 us
  matrix products: 47 us -> 0 us
  Pallas kernels: 0 us -> 43.7 us
  between operations: 14.3 us -> 0.87 us
  local copies, waits for them, and re-layouts: 27.3 us -> 20.1 us
  starting transfers between devices: 12.9 us -> 18.6 us
  other arithmetic: 4.16 us -> 0 us
    reduce_scatter x1 -> x0, waiting for transfers between devices: 129 us -> none  [shards(): lax.psum_scatter(partial_value.reshape(levels * node_count, width), 'lev'...]
    dot_general x6 -> x0, matrix products: 47 us -> none  [the longest x1 15.2 us: shards(): jnp.einsum('osn,osw->onw', far_onehot, far_msgs, precision=lax.Precision....]
    pallas_call x0 -> x7, Pallas kernels: none -> 43.7 us  [the longest x2 15.8 us: embed(): pl.pallas_call(first_kernel if before is None else second_kernel, grid=(s...]
    all_to_all x1 -> x2, waiting for transfers between devices: 50.2 us -> 9.17 us  [the longest x1 9.16 us: shards(): got = lax.all_to_all(sent, 'lev', split_axis=0, concat_axis=0, tiled=True)]
    gather x2 -> x0, local copies, waits for them, and re-layouts: 21.7 us -> none  [the longest x1 17 us: message(): rows = jnp.take(table, sources, axis=0)]
    unnamed x36 -> x71, local copies, waits for them, and re-layouts: 1.44 us -> 19.9 us
    all_to_all x1 -> x2, starting transfers between devices: 8.78 us -> 14.7 us  [the longest x1 8.64 us: shards(): got = lax.all_to_all(sent, 'lev', split_axis=0, concat_axis=0, tiled=True)]
    concatenate x1 -> x0, other arithmetic: 3.91 us -> none  [shards(): table = jnp.concatenate([latent, padded[0], padded[3]], axis=0)]
  transfers between devices with their start and end apart: 4 -> 4, of which waited for: 3 -> 1; matrix products, arithmetic and copies ran while one was open for 0% -> 0% of each run, Pallas kernels for 0% -> 34%
where the time goes in v2:
time: 93.4 us; the launch traced here: 92.4 us
  Pallas kernels  43.7 us (47%)
  local copies, waits for them, and re-layouts  20.1 us (22%)
  starting transfers between devices  18.6 us (20%)
  waiting for transfers between devices  9.17 us (10%)
    unnamed x71, local copies, waits for them, and re-layouts  19.9 us
    pallas_call x2, Pallas kernels, embed(): pl.pallas_call(first_kernel if before is None else second_kernel, grid=(s...  15.8 us
    pallas_call x1, Pallas kernels, count_edges(): pl.pallas_call(functools.partial(count_kernel, chans=chans), grid=(table...  15.5 us
    all_to_all x1, waiting for transfers between devices, shards(): got = lax.all_to_all(sent, 'lev', split_axis=0, concat_axis=0, tiled=True)  9.16 us
    all_to_all x1, starting transfers between devices, shards(): got = lax.all_to_all(sent, 'lev', split_axis=0, concat_axis=0, tiled=True)  8.64 us
    all_to_all x1, starting transfers between devices, shards(): lax.all_to_all(rows.reshape(levels, slot_count, wide), 'lev', split_axis=...  6.09 us
    pallas_call x1, Pallas kernels, pack(): pl.pallas_call(functools.partial(pack_kernel, parts=parts), in_specs=[sme...  4.1 us
    pallas_call x1, Pallas kernels, select(): pl.pallas_call(select_kernel, out_shape=(out, out, jax.ShapeDtypeStruct((...  4.02 us
  transfers between devices with their start and end apart: 4, of which 1 were waited for; matrix products, arithmetic and copies ran while one was open for 0% of the time, Pallas kernels for 34%

profile of v2, /device:TPU:1, one launch (start us, length us, event | category | flops | bytes accessed | tf_op | source)
XLA Modules:
  0.0 92.4 jit_solution(8140417650937887357)
XLA Ops:
  0.6 0.0 copy-start.33
  0.6 0.0 copy-start.31
  0.7 0.0 copy-start.32
  0.7 0.0 copy-start.23
  0.7 0.0 copy-start.28
  0.7 0.0 copy-start.29
  0.7 0.0 copy-start.30
  0.7 4.1 %pack.1 = bf16[32,8,4096]{2,1,0:T(8,128)(2,1)} custom-call(s32[1]{0:T(128)} %bitcast.me_ref, f32[224]{0:T(256)} %mean_ref.1, f32[224]{0:T(256)} %scale_ref.1, f32[7,131072]{1,0:T(8,128)} %x_ref.1), custom_call_target="tpu_custom_call" | custom-call | flops 2097152 | bytes 6291456 | tf_op jit(solution)/shard_map/pack/pallas_call | solution.py:82
  4.8 8.6 %all-to-all-start = ((bf16[32,8,4096]{2,1,0:T(8,128)(2,1)}), bf16[32,8,4096]{2,1,0:T(8,128)(2,1)}, u32[]{:S(2)}, u32[]{:S(2)}) async-start(bf16[32,8,4096]{2,1,0:T(8,128)(2,1)} %pack.1), calls=%async_computation | async-start | bytes 4194304 | tf_op jit(solution)/shard_map/all_to_all | solution.py:354
  13.5 0.0 copy-done.33
  13.5 0.0 copy-done.31
  13.5 0.1 copy.23
  13.6 0.1 reshape.28.src_ref
  13.7 0.0 copy-done.32
  13.7 0.1 copy.24
  13.7 0.1 reshape.29.dst_ref
  13.8 0.0 copy-done.23
  13.8 0.0 copy-done.28
  13.8 0.0 copy-done.29
  13.8 0.0 copy-done.30
  13.9 0.0 copy-start.8
  13.9 1.2 %copy-done.8 = bf16[1024,512]{1,0:T(8,128)(2,1)S(1)} copy-done((bf16[1024,512]{1,0:T(8,128)(2,1)S(1)}, bf16[1024,512]{1,0:T(8,128)(2,1)}, u32[]{:S(2)}) %copy-start.8) | copy-done | bytes 1048600
  15.1 0.9 %copy-done.27 = bf16[224,512]{1,0:T(8,128)(2,1)S(1)} copy-done((bf16[224,512]{1,0:T(8,128)(2,1)S(1)}, bf16[224,512]{1,0:T(8,128)(2,1)}, u32[]{:S(2)}) %copy-start.27) | copy-done | bytes 229400
  16.0 15.5 %count.1 = (bf16[320,4608]{1,0:T(8,128)(2,1)S(1)}, bf16[256,512]{1,0:T(8,128)(2,1)S(1)}, f32[320,512]{1,0:T(8,128)S(1)}) custom-call(s32[1,4096]{1,0:T(1,128)S(1)} %copy-done.28, s32[1,4096]{1,0:T(1,128)S(1)} %copy-done.29, bf16[224,512]{1,0:T(8,128)(2,1)S(1)} %copy-done.27, bf16[320,512]{1,0:T(8,128)(2,1)S(1)} %copy-done.23, ...), custom_call_target="tpu_custom_call" | custom-call | flops 12079595520 | bytes 2949120 | tf_op jit(solution)/shard_map/count/pallas_call | solution.py:128
  31.5 0.0 copy-start.4
  31.5 0.7 copy-done.4
  32.2 0.0 copy-start.11
  32.2 0.8 copy-done.11
  33.0 9.2 %all-to-all-done = bf16[32,8,4096]{2,1,0:T(8,128)(2,1)} async-done(((bf16[32,8,4096]{2,1,0:T(8,128)(2,1)}), bf16[32,8,4096]{2,1,0:T(8,128)(2,1)}, u32[]{:S(2)}, u32[]{:S(2)}) %all-to-all-start) | async-done | bytes 2097184 | tf_op jit(solution)/shard_map/all_to_all | solution.py:354
  42.2 4.0 %select.1 = (bf16[256,256]{1,0:T(8,128)(2,1)S(1)}, bf16[256,256]{1,0:T(8,128)(2,1)S(1)}, bf16[256,512]{1,0:T(8,128)(2,1)S(1)}) custom-call(bf16[256,4096]{1,0:T(8,128)(2,1)} %bitcast.1.x_ref, s32[1,512]{1,0:T(1,128)S(1)} %bitcast.16, s32[1,512]{1,0:T(1,128)S(1)} %reshape.28.src_ref), custom_call_target="tpu_custom_call" | custom-call | flops 2147483648 | bytes 2097152 | tf_op jit(solution)/shard_map/select/pallas_call | solution.py:178
  46.2 1.7 %collective-permute-start = (bf16[256,256]{1,0:T(8,128)(2,1)S(1)}, bf16[256,256]{1,0:T(8,128)(2,1)S(1)}, u32[]{:S(2)}, u32[]{:S(2)}) collective-permute-start(bf16[256,256]{1,0:T(8,128)(2,1)S(1)} %get-tuple-element.13), channel_id=1, source_target_pairs={{0,32},{32,64},{64,96},{96,0},{1,33},{33,65},{65,97},{97,1},{2,34}... | collective-permute-start | bytes 393224 | tf_op jit(solution)/shard_map/ppermute | solution.py:367
  47.9 2.2 %collective-permute-start.1 = (bf16[256,256]{1,0:T(8,128)(2,1)S(1)}, bf16[256,256]{1,0:T(8,128)(2,1)S(1)}, u32[]{:S(2)}, u32[]{:S(2)}) collective-permute-start(bf16[256,256]{1,0:T(8,128)(2,1)S(1)} %get-tuple-element.14), channel_id=1, source_target_pairs={{32,0},{64,32},{96,64},{0,96},{33,1},{65,33},{97,65},{1,97},{34,2}... | collective-permute-start | bytes 393224 | tf_op jit(solution)/shard_map/ppermute | solution.py:368
  50.1 0.0 copy-done
  50.1 0.0 copy-done.25
  50.1 0.0 copy-done.26
  50.1 0.0 copy-done.1
  50.1 0.0 copy-done.5
  50.2 7.2 %embed.2 = (bf16[4096,512]{1,0:T(8,128)(2,1)}, f32[320,512]{1,0:T(8,128)S(1)}) custom-call(bf16[256,4096]{1,0:T(8,128)(2,1)} %bitcast.1.x_ref, bf16[320,4608]{1,0:T(8,128)(2,1)S(1)} %get-tuple-element.12.s_ref.s_halo, bf16[256,512]{1,0:T(8,128)(2,1)S(1)} %copy-done.5, f32[1,512]{1,0:T(1,128)S(1)} %bitcast.10, bf16[512,512]{1,0:T(8,128)(2,1)S(1)} %copy-done, ...), custom_call_target="tpu_custom_call" | custom-call | flops 3355443200 | bytes 3145728 | tf_op jit(solution)/shard_map/embed/pallas_call | solution.py:269
  57.3 0.0 collective-permute-done.low_ref
  57.4 0.0 collective-permute-done.1.up_ref
  57.4 0.4 slots.1
  57.8 0.4 copy-done.15
  58.2 0.1 copy-done.17
  58.3 0.7 copy-done.10
  59.0 0.6 copy-done.19
  59.6 6.1 %all-to-all-start.1 = ((bf16[32,16,256]{2,1,0:T(8,128)(2,1)}), bf16[32,16,256]{2,1,0:T(8,128)(2,1)}, u32[]{:S(2)}, u32[]{:S(2)}) async-start(bf16[32,16,256]{2,1,0:T(8,128)(2,1)} %bitcast.9), calls=%async_computation.1 | async-start | bytes 524288 | tf_op jit(solution)/shard_map/all_to_all | solution.py:375
  65.7 0.0 copy-start.2
  65.7 1.0 %copy-done.2 = bf16[512,512]{1,0:T(8,128)(2,1)S(1)} copy-done((bf16[512,512]{1,0:T(8,128)(2,1)S(1)}, bf16[512,512]{1,0:T(8,128)(2,1)}, u32[]{:S(2)}) %copy-start.2) | copy-done | bytes 524312
  66.7 0.9 %copy-done.6 = bf16[256,512]{1,0:T(8,128)(2,1)S(1)} copy-done((bf16[256,512]{1,0:T(8,128)(2,1)S(1)}, bf16[256,512]{1,0:T(8,128)(2,1)}, u32[]{:S(2)}) %copy-start.6) | copy-done | bytes 262168
  67.7 1.1 %copy-done.16 = f32[320,512]{1,0:T(8,128)S(1)} copy-done((f32[320,512]{1,0:T(8,128)S(1)}, f32[320,512]{1,0:T(8,128)}, u32[]{:S(2)}) %copy-start.16) | copy-done | bytes 655384
  68.8 0.9 copy-done.18
  69.7 0.9 copy-done.20
  70.6 8.6 %embed.3 = (bf16[4096,512]{1,0:T(8,128)(2,1)}, f32[320,512]{1,0:T(8,128)S(1)}) custom-call(bf16[256,4096]{1,0:T(8,128)(2,1)} %bitcast.1.x_ref, bf16[320,4608]{1,0:T(8,128)(2,1)S(1)} %get-tuple-element.12.s_ref.s_halo, bf16[256,256]{1,0:T(8,128)(2,1)S(1)} %copy-done.18, bf16[256,256]{1,0:T(8,128)(2,1)S(1)} %copy-done.20, ...), custom_call_target="tpu_custom_call", output_to_operand_aliasing={{0}: (10, {})} | custom-call | flops 3355443200 | bytes 3145728 | tf_op jit(solution)/shard_map/embed/pallas_call | solution.py:269
  79.2 0.8 copy-done.13
  80.0 0.0 all-to-all-done.1
  80.1 1.0 %copy-done.3 = bf16[512,512]{1,0:T(8,128)(2,1)S(1)} copy-done((bf16[512,512]{1,0:T(8,128)(2,1)S(1)}, bf16[512,512]{1,0:T(8,128)(2,1)}, u32[]{:S(2)}) %copy-start.3) | copy-done | bytes 524312
  81.1 0.9 %copy-done.7 = bf16[256,512]{1,0:T(8,128)(2,1)S(1)} copy-done((bf16[256,512]{1,0:T(8,128)(2,1)S(1)}, bf16[256,512]{1,0:T(8,128)(2,1)}, u32[]{:S(2)}) %copy-start.7) | copy-done | bytes 262168
  82.0 1.2 %copy-done.9 = bf16[1024,512]{1,0:T(8,128)(2,1)S(1)} copy-done((bf16[1024,512]{1,0:T(8,128)(2,1)S(1)}, bf16[1024,512]{1,0:T(8,128)(2,1)}, u32[]{:S(2)}) %copy-start.9) | copy-done | bytes 1048600
  83.3 1.1 %copy-done.12 = f32[320,512]{1,0:T(8,128)S(1)} copy-done((f32[320,512]{1,0:T(8,128)S(1)}, f32[320,512]{1,0:T(8,128)}, u32[]{:S(2)}) %copy-start.12) | copy-done | bytes 655384
  84.4 1.1 %copy-done.14 = f32[320,512]{1,0:T(8,128)S(1)} copy-done((f32[320,512]{1,0:T(8,128)S(1)}, f32[320,512]{1,0:T(8,128)}, u32[]{:S(2)}) %copy-start.14) | copy-done | bytes 655384
  85.4 1.0 %copy-done.21 = bf16[512,512]{1,0:T(8,128)(2,1)S(1)} copy-done((bf16[512,512]{1,0:T(8,128)(2,1)S(1)}, bf16[512,512]{1,0:T(8,128)(2,1)}, u32[]{:S(2)}) %copy-start.21) | copy-done | bytes 524312
  86.5 1.0 %copy-done.22 = bf16[512,512]{1,0:T(8,128)(2,1)S(1)} copy-done((bf16[512,512]{1,0:T(8,128)(2,1)S(1)}, bf16[512,512]{1,0:T(8,128)(2,1)}, u32[]{:S(2)}) %copy-start.22) | copy-done | bytes 524312
  87.5 1.0 %copy-done.24 = bf16[320,512]{1,0:T(8,128)(2,1)S(1)} copy-done((bf16[320,512]{1,0:T(8,128)(2,1)S(1)}, bf16[320,512]{1,0:T(8,128)(2,1)}, u32[]{:S(2)}) %copy-start.24) | copy-done | bytes 327704
  88.5 3.9 %node.1 = bf16[320,512]{1,0:T(8,128)(2,1)} custom-call(bf16[512,256]{1,0:T(8,128)(2,1)} %bitcast.6.r_ref, bf16[256,512]{1,0:T(8,128)(2,1)S(1)} %copy-done.7, f32[1,512]{1,0:T(1,128)S(1)} %bitcast.12, bf16[512,512]{1,0:T(8,128)(2,1)S(1)} %copy-done, bf16[512,512]{1,0:T(8,128)(2,1)S(1)} %copy-done.3, f32[1,512]{1,0:T(1,128)S(1)} %bitcast.15, ...), custom_call_target="tpu_custom_call" | custom-call | flops 805306368 | bytes 3145728 | tf_op jit(solution)/shard_map/node/pallas_call | solution.py:310
  (24 shorter events, 0.0 us)
Async XLA Ops:
  0.6 12.8 %copy-start.33 = (s32[1,2,256]{2,1,0:T(2,128)S(1)}, s32[1,2,256]{2,1,0:T(2,128)}, u32[]{:S(2)}) copy-start(s32[1,2,256]{2,1,0:T(2,128)} %param.24) | copy-start | bytes 6148
  0.6 12.8 %copy-start.31 = (s32[1,32,16]{1,2,0:T(8,128)S(1)}, s32[1,32,16]{1,2,0:T(8,128)}, u32[]{:S(2)}) copy-start(s32[1,32,16]{1,2,0:T(8,128)} %param.27) | copy-start | bytes 6148
  0.7 13.0 %copy-start.32 = (s32[1,32,16]{1,2,0:T(8,128)S(1)}, s32[1,32,16]{1,2,0:T(8,128)}, u32[]{:S(2)}) copy-start(s32[1,32,16]{1,2,0:T(8,128)} %param.28) | copy-start | bytes 6148
  0.7 13.2 %copy-start.23 = (bf16[320,512]{1,0:T(8,128)(2,1)S(1)}, bf16[320,512]{1,0:T(8,128)(2,1)}, u32[]{:S(2)}) copy-start(bf16[320,512]{1,0:T(8,128)(2,1)} %mesh_ref.3) | copy-start | bytes 983044
  0.7 13.1 %copy-start.28 = (s32[1,4096]{1,0:T(1,128)S(1)}, s32[1,4096]{1,0:T(1,128)}, u32[]{:S(2)}) copy-start(s32[1,4096]{1,0:T(1,128)} %src_ref.1) | copy-start | bytes 49156
  0.7 13.1 %copy-start.29 = (s32[1,4096]{1,0:T(1,128)S(1)}, s32[1,4096]{1,0:T(1,128)}, u32[]{:S(2)}) copy-start(s32[1,4096]{1,0:T(1,128)} %dst_ref.1) | copy-start | bytes 49156
  0.7 13.1 %copy-start.30 = (f32[512]{0:T(512)S(1)}, f32[512]{0:T(512)}, u32[]{:S(2)}) copy-start(f32[512]{0:T(512)} %param.34) | copy-start | bytes 6148
  4.8 37.4 %all-to-all-start = ((bf16[32,8,4096]{2,1,0:T(8,128)(2,1)}), bf16[32,8,4096]{2,1,0:T(8,128)(2,1)}, u32[]{:S(2)}, u32[]{:S(2)}) async-start(bf16[32,8,4096]{2,1,0:T(8,128)(2,1)} %pack.1), calls=%async_computation | async-start | bytes 4194304 | tf_op jit(solution)/shard_map/all_to_all | solution.py:354
  13.9 1.2 %copy-start.8 = (bf16[1024,512]{1,0:T(8,128)(2,1)S(1)}, bf16[1024,512]{1,0:T(8,128)(2,1)}, u32[]{:S(2)}) copy-start(bf16[1024,512]{1,0:T(8,128)(2,1)} %w_nb.1) | copy-start | bytes 3145732
  15.1 0.9 %copy-start.27 = (bf16[224,512]{1,0:T(8,128)(2,1)S(1)}, bf16[224,512]{1,0:T(8,128)(2,1)}, u32[]{:S(2)}) copy-start(bf16[224,512]{1,0:T(8,128)(2,1)} %w_ref.1) | copy-start | bytes 688132
  31.5 0.7 copy-start.4
  32.2 0.8 copy-start.11
  33.0 17.1 %copy-start = (bf16[512,512]{1,0:T(8,128)(2,1)S(1)}, bf16[512,512]{1,0:T(8,128)(2,1)}, u32[]{:S(2)}) copy-start(bf16[512,512]{1,0:T(8,128)(2,1)} %w_out.1) | copy-start | bytes 1572868
  33.0 17.1 %copy-start.25 = (f32[512]{0:T(512)S(1)}, f32[512]{0:T(512)}, u32[]{:S(2)}) copy-start(f32[512]{0:T(512)} %param.22) | copy-start | bytes 6148
  33.0 17.1 %copy-start.26 = (f32[512]{0:T(512)S(1)}, f32[512]{0:T(512)}, u32[]{:S(2)}) copy-start(f32[512]{0:T(512)} %param.30) | copy-start | bytes 6148
  42.2 7.9 %copy-start.1 = (bf16[512,512]{1,0:T(8,128)(2,1)S(1)}, bf16[512,512]{1,0:T(8,128)(2,1)}, u32[]{:S(2)}) copy-start(bf16[512,512]{1,0:T(8,128)(2,1)} %w_msg.1) | copy-start | bytes 1572868
  42.2 8.0 %copy-start.5 = (bf16[256,512]{1,0:T(8,128)(2,1)S(1)}, bf16[256,512]{1,0:T(8,128)(2,1)}, u32[]{:S(2)}) copy-start(bf16[256,512]{1,0:T(8,128)(2,1)} %copy-done.4) | copy-start | bytes 786436
  46.2 11.1 %collective-permute-start = (bf16[256,256]{1,0:T(8,128)(2,1)S(1)}, bf16[256,256]{1,0:T(8,128)(2,1)S(1)}, u32[]{:S(2)}, u32[]{:S(2)}) collective-permute-start(bf16[256,256]{1,0:T(8,128)(2,1)S(1)} %get-tuple-element.13), channel_id=1, source_target_pairs={{0,32},{32,64},{64,96},{96,0},{1,33},{33,65},{65,97},{97,1},{2,34}... | collective-permute-start | bytes 393224 | tf_op jit(solution)/shard_map/ppermute | solution.py:367
  47.9 9.4 %collective-permute-start.1 = (bf16[256,256]{1,0:T(8,128)(2,1)S(1)}, bf16[256,256]{1,0:T(8,128)(2,1)S(1)}, u32[]{:S(2)}, u32[]{:S(2)}) collective-permute-start(bf16[256,256]{1,0:T(8,128)(2,1)S(1)} %get-tuple-element.14), channel_id=1, source_target_pairs={{32,0},{64,32},{96,64},{0,96},{33,1},{65,33},{97,65},{1,97},{34,2}... | collective-permute-start | bytes 393224 | tf_op jit(solution)/shard_map/ppermute | solution.py:368
  57.3 0.8 copy-start.15
  57.4 0.9 copy-start.17
  58.2 0.7 copy-start.10
  59.0 0.6 copy-start.19
  59.6 20.5 %all-to-all-start.1 = ((bf16[32,16,256]{2,1,0:T(8,128)(2,1)}), bf16[32,16,256]{2,1,0:T(8,128)(2,1)}, u32[]{:S(2)}, u32[]{:S(2)}) async-start(bf16[32,16,256]{2,1,0:T(8,128)(2,1)} %bitcast.9), calls=%async_computation.1 | async-start | bytes 524288 | tf_op jit(solution)/shard_map/all_to_all | solution.py:375
  65.7 1.0 %copy-start.2 = (bf16[512,512]{1,0:T(8,128)(2,1)S(1)}, bf16[512,512]{1,0:T(8,128)(2,1)}, u32[]{:S(2)}) copy-start(bf16[512,512]{1,0:T(8,128)(2,1)} %w_msg.1) | copy-start | bytes 1572868
  66.7 0.9 %copy-start.6 = (bf16[256,512]{1,0:T(8,128)(2,1)S(1)}, bf16[256,512]{1,0:T(8,128)(2,1)}, u32[]{:S(2)}) copy-start(bf16[256,512]{1,0:T(8,128)(2,1)} %copy-done.4) | copy-start | bytes 786436
  67.7 1.1 %copy-start.16 = (f32[320,512]{1,0:T(8,128)S(1)}, f32[320,512]{1,0:T(8,128)}, u32[]{:S(2)}) copy-start(f32[320,512]{1,0:T(8,128)} %copy-done.15) | copy-start | bytes 1966084
  68.8 0.9 copy-start.18
  69.7 0.9 copy-start.20
  79.2 0.8 copy-start.13
  80.1 1.0 %copy-start.3 = (bf16[512,512]{1,0:T(8,128)(2,1)S(1)}, bf16[512,512]{1,0:T(8,128)(2,1)}, u32[]{:S(2)}) copy-start(bf16[512,512]{1,0:T(8,128)(2,1)} %w_msg.1) | copy-start | bytes 1572868
  81.1 0.9 %copy-start.7 = (bf16[256,512]{1,0:T(8,128)(2,1)S(1)}, bf16[256,512]{1,0:T(8,128)(2,1)}, u32[]{:S(2)}) copy-start(bf16[256,512]{1,0:T(8,128)(2,1)} %copy-done.4) | copy-start | bytes 786436
  82.0 1.2 %copy-start.9 = (bf16[1024,512]{1,0:T(8,128)(2,1)S(1)}, bf16[1024,512]{1,0:T(8,128)(2,1)}, u32[]{:S(2)}) copy-start(bf16[1024,512]{1,0:T(8,128)(2,1)} %w_nb.1) | copy-start | bytes 3145732
  83.3 1.1 %copy-start.12 = (f32[320,512]{1,0:T(8,128)S(1)}, f32[320,512]{1,0:T(8,128)}, u32[]{:S(2)}) copy-start(f32[320,512]{1,0:T(8,128)} %copy-done.11) | copy-start | bytes 1966084
  84.4 1.1 %copy-start.14 = (f32[320,512]{1,0:T(8,128)S(1)}, f32[320,512]{1,0:T(8,128)}, u32[]{:S(2)}) copy-start(f32[320,512]{1,0:T(8,128)} %copy-done.13) | copy-start | bytes 1966084
  85.4 1.0 %copy-start.21 = (bf16[512,512]{1,0:T(8,128)(2,1)S(1)}, bf16[512,512]{1,0:T(8,128)(2,1)}, u32[]{:S(2)}) copy-start(bf16[512,512]{1,0:T(8,128)(2,1)} %w_mo.1) | copy-start | bytes 1572868
  86.5 1.0 %copy-start.22 = (bf16[512,512]{1,0:T(8,128)(2,1)S(1)}, bf16[512,512]{1,0:T(8,128)(2,1)}, u32[]{:S(2)}) copy-start(bf16[512,512]{1,0:T(8,128)(2,1)} %w_no.1) | copy-start | bytes 1572868
  87.5 1.0 %copy-start.24 = (bf16[320,512]{1,0:T(8,128)(2,1)S(1)}, bf16[320,512]{1,0:T(8,128)(2,1)}, u32[]{:S(2)}) copy-start(bf16[320,512]{1,0:T(8,128)(2,1)} %mesh_ref.3) | copy-start | bytes 983044

commit v3 on v2

v3 whole, which is shorter than its diff:
```python
import functools

import jax
import jax.numpy as jnp
from jax import lax
from jax.experimental import pallas as pl
from jax.experimental.pallas import tpu as pltpu
from jax.sharding import PartitionSpec as P

BF = jnp.bfloat16
F32 = jnp.float32
NT = (((1,), (1,)), ((), ()))
TN = (((0,), (0,)), ((), ()))
MIB = 1024 * 1024


def params(mib, **kw):
    return pltpu.CompilerParams(vmem_limit_bytes=mib * MIB, **kw)


def whole(shape):
    return pl.BlockSpec(shape, lambda *_: (0,) * len(shape))


def cost(flops, nbytes):
    return pl.CostEstimate(flops=int(flops), bytes_accessed=int(nbytes), transcendentals=0)


def dot(a, b, dims=(((1,), (0,)), ((), ()))):
    return lax.dot_general(a, b, dims, preferred_element_type=F32)


def silu2(h):
    return (h + h * jnp.tanh(h)).astype(BF)


def hot(ids, index, value=1.0):
    return jnp.where(ids == index, jnp.asarray(value, BF), jnp.asarray(0.0, BF))


def at_vmem(*arrays):
    return [pltpu.with_memory_space_constraint(a, pltpu.VMEM) for a in arrays]


def at_hbm(array):
    return pltpu.with_memory_space_constraint(array, pltpu.HBM)


VM = pl.BlockSpec(memory_space=pltpu.VMEM)
ANY = pl.BlockSpec(memory_space=pl.ANY)


def pack_kernel(me_ref, mean_ref, scale_ref, x_ref, o_ref, in_buf, out_buf, in_sem, out_sem, *, parts):
    chans, points = in_buf.shape
    levels, _, pts = out_buf.shape
    per = levels // parts
    width = per * pts

    def load(k):
        at = pl.ds(k * width, width)
        return pltpu.make_async_copy(x_ref.at[:, at], in_buf.at[:, at], in_sem.at[k])

    def store(k):
        at = pl.ds(k * per, per)
        return pltpu.make_async_copy(out_buf.at[at], o_ref.at[at], out_sem.at[k])

    for k in range(parts):
        load(k).start()
    base = me_ref[0] * chans
    row = lax.broadcasted_iota(jnp.int32, (chans, 1), 0)
    mean = jnp.zeros((chans, 1), F32)
    scale = jnp.zeros((chans, 1), F32)
    for c in range(chans):
        mean = jnp.where(row == c, mean_ref[base + c], mean)
        scale = jnp.where(row == c, scale_ref[base + c], scale)
    pad = jnp.ones((1, pts), F32)
    for k in range(parts):
        load(k).wait()
        for j in range(k * per, (k + 1) * per):
            val = (in_buf[:, j * pts : (j + 1) * pts] - mean) * scale
            out_buf[j] = jnp.concatenate([val, pad], axis=0).astype(BF)
        store(k).start()
    for k in range(parts):
        store(k).wait()


def pack(me, mean, scale, fields, levels):
    chans, points = fields.shape
    pts = points // levels
    parts = 8
    smem = pl.BlockSpec(memory_space=pltpu.SMEM)
    shape = (levels, chans + 1, pts)
    return pl.pallas_call(
        functools.partial(pack_kernel, parts=parts),
        in_specs=[smem, smem, smem, pl.BlockSpec(memory_space=pl.ANY)],
        out_specs=pl.BlockSpec(memory_space=pl.ANY),
        out_shape=jax.ShapeDtypeStruct(shape, BF),
        scratch_shapes=[
            pltpu.VMEM(fields.shape, F32),
            pltpu.VMEM(shape, BF),
            pltpu.SemaphoreType.DMA((parts,)),
            pltpu.SemaphoreType.DMA((parts,)),
        ],
        compiler_params=params(60),
        cost_estimate=cost(points * 16, points * 48),
        name="pack",
    )(me, mean, scale, fields)


def count_kernel(
    src_ref, dst_ref, w_ref, b_ref, mesh_ref, b_n, b_m, w_node, w_out, w_msg,
    o_ref, w_in_ref, pre_ref, out_ref, msg_ref, bm_ref, nb_ref, hot_ref, na_ref, sem, *, chans,
):
    nodes, edges = hot_ref.shape
    lat = w_out.shape[0]
    tile = 512
    chunk = 1024
    pairs = (
        (w_node.at[pl.ds(0, lat)], na_ref),
        (w_node.at[pl.ds(lat, lat)], nb_ref),
        (w_out, out_ref),
        (w_msg, msg_ref),
    )
    copies = [pltpu.make_async_copy(f, t, sem.at[k]) for k, (f, t) in enumerate(pairs)]
    for c in copies:
        c.start()
    ids = lax.broadcasted_iota(jnp.int32, (nodes, edges), 0).astype(jnp.int16)
    hot_ref[...] = hot(ids, dst_ref[...].astype(jnp.int16))
    shape = (w_in_ref.shape[0], w_ref.shape[0])
    row = lax.broadcasted_iota(jnp.int32, shape, 0)
    col = lax.broadcasted_iota(jnp.int32, shape, 1)
    lane = row % (chans + 1)
    place = jnp.where(lane < chans, row // (chans + 1) * chans + lane, -1)
    w_in = dot(hot(col, place, 0.5), w_ref[...])
    rest = 0.5 * b_ref[...]
    row = lax.broadcasted_iota(jnp.int32, w_in.shape, 0)
    for k in range(3):
        part = rest.astype(BF).astype(F32)
        rest = rest - part
        w_in = jnp.where(row == (k + 3) * (chans + 1) - 1, part, w_in)
    w_in_ref[...] = w_in.astype(BF)
    bm_ref[...] = 0.5 * b_m[...]

    @pl.loop(0, o_ref.shape[1] // tile)
    def _(i):
        start = pl.multiple_of(i * tile, tile)
        rows = lax.broadcasted_iota(jnp.int32, (tile, chunk), 0).astype(jnp.int16)
        acc = jnp.zeros((nodes, tile), F32)
        for c in range(edges // chunk):
            at = slice(c * chunk, (c + 1) * chunk)
            acc = acc + dot(hot_ref[:, at], hot(rows, (src_ref[:, at] - start).astype(jnp.int16)), NT)
        o_ref[:, pl.ds(start, tile)] = acc.astype(BF)

    for c in copies:
        c.wait()
    msg_ref[...] = msg_ref[...] * 0.5
    nb_ref[...] = nb_ref[...] * 0.5
    pre_ref[...] = 0.5 * (dot(mesh_ref[...], na_ref[...]) + b_n[...])


def count_edges(src, dst, w_in, b_in, mesh, b_node, b_msg, w_node, w_out, w_msg, table, wide, chans):
    edges = src.shape[1]
    nodes, lat = mesh.shape
    square = pltpu.VMEM((lat, lat), BF)
    return pl.pallas_call(
        functools.partial(count_kernel, chans=chans),
        in_specs=[VM] * 7 + [ANY] * 3,
        out_specs=[VM] * 7,
        out_shape=(
            pltpu.HBM((nodes, table), BF),
            pltpu.VMEM((wide, lat), BF),
            pltpu.HBM((nodes, lat), F32),
            square,
            square,
            pltpu.VMEM((1, lat), F32),
            pltpu.HBM((lat, lat), BF),
        ),
        scratch_shapes=[
            pltpu.VMEM((nodes, edges), BF),
            pltpu.VMEM((lat, lat), BF),
            pltpu.SemaphoreType.DMA((4,)),
        ],
        compiler_params=params(24),
        cost_estimate=cost(2 * nodes * edges * table, nodes * table * 2),
        name="count",
    )(src, dst, w_in, b_in, mesh, b_node, b_msg, *map(at_hbm, (w_node, w_out, w_msg)))


def select_kernel(x_ref, idx_ref, src_ref, low_ref, high_ref, own_ref, keep_ref, near_hot, far_hot, sem):
    pts = x_ref.shape[1]
    half = low_ref.shape[1]
    parts = sem.shape[0]
    chunk = pts // parts

    def load(c):
        at = pl.ds(c * chunk, chunk)
        return pltpu.make_async_copy(x_ref.at[:, at], keep_ref.at[:, at], sem.at[c])

    for c in range(parts):
        load(c).start()
    rows = lax.broadcasted_iota(jnp.int32, (chunk, 2 * half), 0).astype(jnp.int16)
    for c in range(parts):
        at = pl.ds(c * chunk, chunk)
        near_hot[at] = hot(rows, (idx_ref[...] - c * chunk).astype(jnp.int16))
        far_hot[at] = hot(rows, (src_ref[...] - c * chunk).astype(jnp.int16))
    for c in range(parts):
        load(c).wait()
    near = dot(keep_ref[...], near_hot[...])
    low_ref[...] = near[:, :half].astype(BF)
    high_ref[...] = near[:, half:].astype(BF)
    own_ref[...] = dot(keep_ref[...], far_hot[...]).astype(BF)


def select(x, idx, src):
    rows, pts = x.shape
    half = idx.shape[1] // 2
    slots = src.shape[1]
    out = jax.ShapeDtypeStruct((rows, half), BF)
    return pl.pallas_call(
        select_kernel,
        in_specs=[ANY, VM, VM],
        out_specs=[VM] * 4,
        out_shape=(out, out, pltpu.VMEM((rows, slots), BF), pltpu.VMEM(x.shape, BF)),
        scratch_shapes=[
            pltpu.VMEM((pts, 2 * half), BF),
            pltpu.VMEM((pts, slots), BF),
            pltpu.SemaphoreType.DMA((4,)),
        ],
        compiler_params=params(24),
        cost_estimate=cost(2 * rows * pts * (2 * half + slots), rows * pts * 2),
        name="select",
    )(at_hbm(x), idx, src)


def slots_kernel(own_ref, low_ref, up_ref, src_ref, dst_ref, o_ref, *, start, pad):
    half = low_ref.shape[1]
    shape = (half, own_ref.shape[1])
    ids = lax.broadcasted_iota(jnp.int32, shape, 0) + start
    acc = own_ref[...].astype(F32)
    acc = acc + dot(low_ref[...], hot(ids, src_ref[...]))
    acc = acc + dot(up_ref[...], hot(ids + half, src_ref[...]))
    code = dst_ref[...] + 1
    row = lax.broadcasted_iota(jnp.int32, acc.shape, 0)
    acc = jnp.where(row == pad, (code // 16).astype(F32), acc)
    acc = jnp.where(row == 2 * pad + 1, (code % 16).astype(F32), acc)
    o_ref[...] = acc.T.astype(BF)


def slots_rows(own, low, up, src, dst, start, pad):
    rows, slots = own.shape
    return pl.pallas_call(
        functools.partial(slots_kernel, start=start, pad=pad),
        in_specs=[VM] * 5,
        out_shape=jax.ShapeDtypeStruct((slots, rows), BF),
        compiler_params=params(16),
        cost_estimate=cost(4 * rows * low.shape[1] * slots, slots * rows * 4),
        name="slots",
    )(*at_vmem(own, low, up), src, dst)


def act_of(x, dims, w_in, w_out, w_msg, b_msg):
    hidden = silu2(dot(x, w_in[...], dims))
    latent = dot(hidden, w_out[...]).astype(BF)
    return latent, silu2(dot(latent, w_msg[...]) + b_msg[...])


def embed_tiles(x_ref, s_ref, weights, lat_hbm, sum_ref, buf, sem, first, steps, ready):
    tile = buf.shape[1]

    def store(i, slot):
        at = pl.ds(pl.multiple_of((i + first) * tile, tile), tile)
        return pltpu.make_async_copy(buf.at[slot], lat_hbm.at[at], sem.at[slot])

    @pl.loop(0, steps)
    def _(i):
        slot = lax.rem(i, 2)

        @pl.when(i >= 2)
        def _():
            store(i - 2, slot).wait()

        ready(i)
        at = pl.ds(pl.multiple_of(i * tile, tile), tile)
        latent, act = act_of(x_ref[:, at], TN, *weights)
        buf[slot] = latent
        store(i, slot).start()
        sum_ref[...] += dot(s_ref[:, at], act)

    for i in range(max(steps - 2, 0), steps):
        store(i, i % 2).wait()


def columns(src, dst, sem, start):
    width = dst.shape[1]
    return pltpu.make_async_copy(src.at[:, pl.ds(start, width)], dst, sem)


def first_kernel(
    x_ref, w_in, w_out, w_msg, b_msg, s_hbm, lat_ref, sum_ref, s_buf, buf, sem, in_sem, *, first, steps
):
    load = columns(s_hbm, s_buf, in_sem.at[0], 0)
    load.start()
    sum_ref[...] = jnp.zeros_like(sum_ref)

    def ready(i):
        @pl.when(i == 0)
        def _():
            load.wait()

    embed_tiles(
        x_ref, s_buf, (w_in, w_out, w_msg, b_msg), lat_ref, sum_ref, buf, sem, first, steps, ready
    )


def second_kernel(
    low_ref, up_ref, before, w_in, w_out, w_msg, b_msg, s_hbm, x_hbm, _, lat_ref, sum_ref,
    s_buf, x_buf, h_buf, buf, sem, in_sem, *, first, steps,
):
    weights = (w_in, w_out, w_msg, b_msg)
    half = low_ref.shape[1]
    start = first * buf.shape[1]
    loads = (
        columns(s_hbm, h_buf, in_sem.at[0], x_hbm.shape[1]),
        columns(x_hbm, x_buf, in_sem.at[1], start),
        columns(s_hbm, s_buf, in_sem.at[2], start),
    )
    for c in loads:
        c.start()
    acts = [act_of(ref[...], TN, *weights)[1] for ref in (low_ref, up_ref)]
    loads[0].wait()
    total = before[...]
    for k, act in enumerate(acts):
        total = total + dot(h_buf[:, k * half : (k + 1) * half], act)
    sum_ref[...] = total
    loads[1].wait()
    loads[2].wait()
    embed_tiles(x_buf, s_buf, weights, lat_ref, sum_ref, buf, sem, first, steps, lambda i: None)


def embed(x, counts, weights, first, steps, tile, before=None):
    rows, pts = x.shape
    nodes = counts.shape[0]
    lat = weights[0].shape[1]
    span = steps * tile
    inner = [pltpu.VMEM((nodes, span), BF)]
    if before is None:
        args = [*at_vmem(x, *weights), at_hbm(counts)]
        specs = [VM] * 5 + [ANY]
        alias = {}
    else:
        latent, total, low, up = before
        args = [*at_vmem(low, up, total, *weights), at_hbm(counts), at_hbm(x), at_hbm(latent)]
        specs = [VM] * 7 + [ANY] * 3
        alias = {9: 0}
        inner += [pltpu.VMEM((rows, span), BF), pltpu.VMEM((nodes, 2 * low.shape[1]), BF)]
    return pl.pallas_call(
        functools.partial(first_kernel if before is None else second_kernel, first=first, steps=steps),
        in_specs=specs,
        out_specs=[ANY, VM],
        out_shape=(pltpu.HBM((pts, lat), BF), pltpu.VMEM((nodes, lat), F32)),
        scratch_shapes=inner
        + [
            pltpu.VMEM((2, tile, lat), BF),
            pltpu.SemaphoreType.DMA((2,)),
            pltpu.SemaphoreType.DMA((3,)),
        ],
        input_output_aliases=alias,
        compiler_params=params(24),
        cost_estimate=cost(2 * span * lat * (rows + 2 * lat + nodes), span * (rows + lat) * 2),
        name="embed",
    )(*args)


def node_kernel(r_ref, w_in, w_out, w_msg, b_msg, sum_ref, *rest, pad):
    sources, o_ref, buffers, sem = rest[:5], rest[5], rest[6:11], rest[11]
    loads = [pltpu.make_async_copy(f, t, sem.at[k]) for k, (f, t) in enumerate(zip(sources, buffers))]
    for c in loads:
        c.start()
    w_mo, w_nb, pre_ref, w_no, mesh_ref = buffers
    nodes = sum_ref.shape[0]
    rows = r_ref[...]
    _, act = act_of(rows, (((1,), (0,)), ((), ())), w_in, w_out, w_msg, b_msg)
    lane = lax.broadcasted_iota(jnp.int32, (8, rows.shape[1]), 1)
    pick = jnp.where(lane == pad, 16.0, jnp.where(lane == 2 * pad + 1, 1.0, 0.0)).astype(BF)
    dst = dot(pick, rows, NT)[:1].astype(jnp.int32) - 1
    ids = lax.broadcasted_iota(jnp.int32, (nodes, rows.shape[0]), 0)
    total = sum_ref[...] + dot(hot(ids, dst), act)
    high = total.astype(BF)
    low = (total - high.astype(F32)).astype(BF)
    for c in loads:
        c.wait()
    summed = (dot(high, w_mo[...]) + dot(low, w_mo[...])).astype(BF)
    node = silu2(pre_ref[...] + dot(summed, w_nb[...]))
    o_ref[...] = (mesh_ref[...].astype(F32) + dot(node, w_no[...])).astype(BF)


def node_update(rows, weights, total, w_mo, mesh, pre, w_nb, w_no, pad):
    args = at_vmem(rows, *weights, total)
    later = [at_hbm(a) for a in (w_mo, w_nb, pre, w_no, mesh)]
    slots = rows.shape[0]
    lat = mesh.shape[1]
    return pl.pallas_call(
        functools.partial(node_kernel, pad=pad),
        in_specs=[VM] * len(args) + [ANY] * len(later),
        out_specs=VM,
        out_shape=jax.ShapeDtypeStruct(mesh.shape, BF),
        scratch_shapes=[pltpu.VMEM(a.shape, a.dtype) for a in later]
        + [pltpu.SemaphoreType.DMA((len(later),))],
        compiler_params=params(20),
        cost_estimate=cost(6 * slots * lat * lat, 6 * lat * lat * 2),
        name="node",
    )(*args, *later)


def shards(
    fields,
    chan_mean,
    chan_scale,
    w_embed_in,
    b_embed,
    w_embed_out,
    halo_index,
    local_src,
    local_dst,
    remote_src,
    remote_dst,
    w_msg_in,
    b_msg,
    w_msg_out,
    mesh_nodes,
    w_node_in,
    b_node,
    w_node_out,
):
    levels = lax.axis_size("lev")
    tiles = lax.axis_size("tile")
    chans, points = fields.shape
    pts = points // levels
    slot_count = remote_src.shape[2]
    halo = halo_index.shape[2]
    table = pts + 2 * halo
    wide = (chans + 1) * levels

    me = lax.axis_index("lev").astype(jnp.int32).reshape(1)
    sent = pack(me, chan_mean, chan_scale, fields, levels)
    got = lax.all_to_all(sent, "lev", split_axis=0, concat_axis=0, tiled=True)
    x = got.reshape(wide, pts)

    counts, w_in, pre, w_out, w_msg, b_half, w_nb = count_edges(
        local_src,
        local_dst,
        w_embed_in,
        b_embed[None, :],
        mesh_nodes,
        b_node[None, :],
        b_msg[None, :],
        w_node_in,
        w_embed_out,
        w_msg_in,
        table,
        wide,
        chans,
    )
    weights = [w_in, w_out, w_msg, b_half]

    src = remote_src.reshape(1, -1)
    dst = remote_dst.reshape(1, -1)
    low, high, own, kept = select(x, halo_index.reshape(1, 2 * halo), src)
    ahead = [(i, (i + 1) % tiles) for i in range(tiles)]
    back = [(t, s) for s, t in ahead]
    from_low = lax.ppermute(high, "tile", ahead)
    from_up = lax.ppermute(low, "tile", back)

    tile = 512
    steps = pts // tile
    latent, total = embed(kept, counts, weights, 0, steps // 2, tile)

    rows = slots_rows(own, from_low, from_up, src, dst, pts, chans)
    rows = lax.all_to_all(
        rows.reshape(levels, slot_count, wide), "lev", split_axis=0, concat_axis=0, tiled=True
    ).reshape(levels * slot_count, wide)

    latent, total = embed(
        x, counts, weights, steps // 2, steps - steps // 2, tile, (latent, total, from_low, from_up)
    )
    mesh_out = node_update(
        rows, weights, total, w_msg_out, mesh_nodes, pre, w_nb, w_node_out, chans
    )
    return (latent, mesh_out)


def solution(mesh):
    return jax.shard_map(
        shards,
        mesh=mesh,
        in_specs=(
            P("lev", "tile"),
            P(),
            P(),
            P(),
            P(),
            P(),
            P(("tile", "lev"), None, None),
            P(("tile", "lev"), None),
            P(("tile", "lev"), None),
            P(("tile", "lev"), None, None),
            P(("tile", "lev"), None, None),
            P(),
            P(),
            P(),
            P(("tile", "lev"), None),
            P(),
            P(),
            P(),
        ),
        out_specs=(P(("tile", "lev"), None), P(("tile", "lev"), None)),
        check_vma=False,
    )
```

time: 93.4 us -> 76 us (0.81)
  local copies, waits for them, and re-layouts: 20.1 us -> 0.38 us
  waiting for transfers between devices: 9.17 us -> 13.4 us
    unnamed x71 -> x23, local copies, waits for them, and re-layouts: 19.9 us -> 0.22 us
    all_to_all x1, waiting for transfers between devices: 9.16 us -> 11.6 us  [shards(): got = lax.all_to_all(sent, 'lev', split_axis=0, concat_axis=0, tiled=True)]
    all_to_all x1, waiting for transfers between devices: 0.01 us -> 1.79 us  [shards(): lax.all_to_all(rows.reshape(levels, slot_count, wide), 'lev', split_axis=...]
  transfers between devices with their start and end apart: 4 -> 4, of which waited for: 1 -> 2; matrix products, arithmetic and copies ran while one was open for 0% -> 0% of each run, Pallas kernels for 34% -> 40%
where the time goes in v3:
time: 76 us; the launch traced here: 75.6 us
  Pallas kernels  42.8 us (56%)
  starting transfers between devices  18.1 us (24%)
  waiting for transfers between devices  13.4 us (18%)
  between operations  0.87 us (1%)
    pallas_call x1, Pallas kernels, count_edges(): pl.pallas_call(functools.partial(count_kernel, chans=chans), in_specs=[VM...  16.7 us
    pallas_call x2, Pallas kernels, embed(): pl.pallas_call(functools.partial(first_kernel if before is None else seco...  13.5 us
    all_to_all x1, waiting for transfers between devices, shards(): got = lax.all_to_all(sent, 'lev', split_axis=0, concat_axis=0, tiled=True)  11.6 us
    all_to_all x1, starting transfers between devices, shards(): got = lax.all_to_all(sent, 'lev', split_axis=0, concat_axis=0, tiled=True)  8.78 us
    all_to_all x1, starting transfers between devices, shards(): lax.all_to_all(rows.reshape(levels, slot_count, wide), 'lev', split_axis=...  5.43 us
    pallas_call x1, Pallas kernels, pack(): pl.pallas_call(functools.partial(pack_kernel, parts=parts), in_specs=[sme...  3.97 us
    pallas_call x1, Pallas kernels, select(): pl.pallas_call(select_kernel, in_specs=[ANY, VM, VM], out_specs=[VM] * 4,...  3.89 us
    pallas_call x1, Pallas kernels, node_update(): pl.pallas_call(functools.partial(node_kernel, pad=pad), in_specs=[VM] * l...  3.66 us
  transfers between devices with their start and end apart: 4, of which 2 were waited for; matrix products, arithmetic and copies ran while one was open for 0% of the time, Pallas kernels for 40%

profile of v3, /device:TPU:1, one launch (start us, length us, event | category | flops | bytes accessed | tf_op | source)
XLA Modules:
  0.0 75.6 jit_solution(394676943407808151)
XLA Ops:
  0.6 4.0 %pack.1 = bf16[32,8,4096]{2,1,0:T(8,128)(2,1)} custom-call(s32[1]{0:T(128)} %bitcast.me_ref, f32[224]{0:T(256)} %mean_ref.1, f32[224]{0:T(256)} %scale_ref.1, f32[7,131072]{1,0:T(8,128)} %x_ref.1), custom_call_target="tpu_custom_call" | custom-call | flops 2097152 | bytes 6291456 | tf_op jit(solution)/shard_map/pack/pallas_call | solution.py:93
  4.6 0.0 copy-start.9
  4.6 0.0 copy-start.7
  4.6 0.0 copy-start.8
  4.6 0.0 copy-start
  4.7 0.0 copy-start.1
  4.7 0.0 copy-start.2
  4.7 0.0 copy-start.3
  4.7 0.0 copy-start.4
  4.7 0.0 copy-start.5
  4.7 0.0 copy-start.6
  4.7 8.8 %all-to-all-start = ((bf16[32,8,4096]{2,1,0:T(8,128)(2,1)}), bf16[32,8,4096]{2,1,0:T(8,128)(2,1)}, u32[]{:S(2)}, u32[]{:S(2)}) async-start(bf16[32,8,4096]{2,1,0:T(8,128)(2,1)} %pack.1), calls=%async_computation | async-start | bytes 4194304 | tf_op jit(solution)/shard_map/all_to_all | solution.py:446
  13.5 0.0 copy-done.9
  13.5 0.0 copy-done.7
  13.5 0.1 copy.23
  13.6 0.1 reshape.28.src_ref
  13.7 0.0 copy-done.8
  13.7 0.1 copy.24
  13.8 0.1 reshape.29.dst_ref
  13.9 0.0 copy-done
  13.9 0.0 copy-done.1
  13.9 0.0 copy-done.2
  13.9 0.0 copy-done.3
  13.9 0.0 copy-done.4
  13.9 0.0 copy-done.5
  13.9 0.0 copy-done.6
  13.9 16.7 %count.1 = (bf16[320,4608]{1,0:T(8,128)(2,1)}, bf16[256,512]{1,0:T(8,128)(2,1)S(1)}, f32[320,512]{1,0:T(8,128)}, bf16[512,512]{1,0:T(8,128)(2,1)S(1)}, bf16[512,...) custom-call(s32[1,4096]{1,0:T(1,128)S(1)} %copy-done.2, s32[1,4096]{1,0:T(1,128)S(1)} %copy-done.3, ...), custom_call_target="tpu_custom_call" | custom-call | flops 12079595520 | bytes 2949120 | tf_op jit(solution)/shard_map/count/pallas_call | solution.py:165
  30.6 11.6 %all-to-all-done = bf16[32,8,4096]{2,1,0:T(8,128)(2,1)} async-done(((bf16[32,8,4096]{2,1,0:T(8,128)(2,1)}), bf16[32,8,4096]{2,1,0:T(8,128)(2,1)}, u32[]{:S(2)}, u32[]{:S(2)}) %all-to-all-start) | async-done | bytes 2097184 | tf_op jit(solution)/shard_map/all_to_all | solution.py:446
  42.2 3.9 %select.1 = (bf16[256,256]{1,0:T(8,128)(2,1)S(1)}, bf16[256,256]{1,0:T(8,128)(2,1)S(1)}, bf16[256,512]{1,0:T(8,128)(2,1)S(1)}, bf16[256,4096]{1,0:T(8,128)(2,1)S(1)}) custom-call(bf16[256,4096]{1,0:T(8,128)(2,1)} %bitcast.1.x_ref.x_hbm, s32[1,512]{1,0:T(1,128)S(1)} %bitcast.10, s32[1,512]{1,0:T(1,128)S(1)} %reshape.28.src_ref), custom_call_target="tpu_custom_call" | custom-call | flops 2147483648 | bytes 2097152 | tf_op jit(solution)/shard_map/select/pallas_call | solution.py:219
  46.1 1.7 %collective-permute-start = (bf16[256,256]{1,0:T(8,128)(2,1)S(1)}, bf16[256,256]{1,0:T(8,128)(2,1)S(1)}, u32[]{:S(2)}, u32[]{:S(2)}) collective-permute-start(bf16[256,256]{1,0:T(8,128)(2,1)S(1)} %get-tuple-element.17), channel_id=1, source_target_pairs={{0,32},{32,64},{64,96},{96,0},{1,33},{33,65},{65,97},{97,1},{2,34}... | collective-permute-start | bytes 393224 | tf_op jit(solution)/shard_map/ppermute | solution.py:471
  47.8 2.2 %collective-permute-start.1 = (bf16[256,256]{1,0:T(8,128)(2,1)S(1)}, bf16[256,256]{1,0:T(8,128)(2,1)S(1)}, u32[]{:S(2)}, u32[]{:S(2)}) collective-permute-start(bf16[256,256]{1,0:T(8,128)(2,1)S(1)} %get-tuple-element.18), channel_id=1, source_target_pairs={{32,0},{64,32},{96,64},{0,96},{33,1},{65,33},{97,65},{1,97},{34,2}... | collective-permute-start | bytes 393224 | tf_op jit(solution)/shard_map/ppermute | solution.py:472
  50.1 6.3 %embed.2 = (bf16[4096,512]{1,0:T(8,128)(2,1)}, f32[320,512]{1,0:T(8,128)S(1)}) custom-call(bf16[256,4096]{1,0:T(8,128)(2,1)S(1)} %get-tuple-element.19.x_ref, bf16[256,512]{1,0:T(8,128)(2,1)S(1)} %get-tuple-element.20.w_in, bf16[512,512]{1,0:T(8,128)(2,1)S(1)} %get-tuple-element.21.w_out, bf16[512,512]{1,0:T(8,128)(2,1)S(1)} %get-tuple-element.22.w_msg, ...), custom_call_target="tpu_custom_call" | custom-call | flops 3355443200 | bytes 3145728 | tf_op jit(solution)/shard_map/embed/pallas_call | solution.py:356
  56.4 0.0 collective-permute-done.low_ref
  56.4 0.0 collective-permute-done.1.up_ref
  56.4 1.1 %slots.1 = bf16[512,256]{1,0:T(8,128)(2,1)} custom-call(bf16[256,512]{1,0:T(8,128)(2,1)S(1)} %get-tuple-element.28.own_ref, bf16[256,256]{1,0:T(8,128)(2,1)S(1)} %collective-permute-done.low_ref, bf16[256,256]{1,0:T(8,128)(2,1)S(1)} %collective-permute-done.1.up_ref, s32[1,512]{1,0:T(1,128)S(1)} %reshape.28.src_ref, s32[1,512]{1,0:T(1,128)S(1)} %reshape.29.dst_ref), custom_call_target="tpu_custom_call" | custom-call | flops 134217728 | bytes 524288 | tf_op jit(solution)/shard_map/slots/pallas_call | solution.py:251
  57.5 5.4 %all-to-all-start.1 = ((bf16[32,16,256]{2,1,0:T(8,128)(2,1)}), bf16[32,16,256]{2,1,0:T(8,128)(2,1)S(1)}, u32[]{:S(2)}, u32[]{:S(2)}) async-start(bf16[32,16,256]{2,1,0:T(8,128)(2,1)} %bitcast.5), calls=%async_computation.1 | async-start | bytes 524288 | tf_op jit(solution)/shard_map/all_to_all | solution.py:479
  62.9 7.2 %embed.3 = (bf16[4096,512]{1,0:T(8,128)(2,1)}, f32[320,512]{1,0:T(8,128)S(1)}) custom-call(bf16[256,256]{1,0:T(8,128)(2,1)S(1)} %collective-permute-done.low_ref, bf16[256,256]{1,0:T(8,128)(2,1)S(1)} %collective-permute-done.1.up_ref, f32[320,512]{1,0:T(8,128)S(1)} %get-tuple-element.25.before, ...), custom_call_target="tpu_custom_call", output_to_operand_aliasing={{0}: (9, {})} | custom-call | flops 3355443200 | bytes 3145728 | tf_op jit(solution)/shard_map/embed/pallas_call | solution.py:356
  70.1 1.8 %all-to-all-done.1 = bf16[32,16,256]{2,1,0:T(8,128)(2,1)S(1)} async-done(((bf16[32,16,256]{2,1,0:T(8,128)(2,1)}), bf16[32,16,256]{2,1,0:T(8,128)(2,1)S(1)}, u32[]{:S(2)}, u32[]{:S(2)}) %all-to-all-start.1) | async-done | bytes 262176 | tf_op jit(solution)/shard_map/all_to_all | solution.py:479
  71.9 3.7 %node.1 = bf16[320,512]{1,0:T(8,128)(2,1)} custom-call(bf16[512,256]{1,0:T(8,128)(2,1)S(1)} %bitcast.9, bf16[256,512]{1,0:T(8,128)(2,1)S(1)} %get-tuple-element.20.w_in, bf16[512,512]{1,0:T(8,128)(2,1)S(1)} %get-tuple-element.21.w_out, bf16[512,512]{1,0:T(8,128)(2,1)S(1)} %get-tuple-element.22.w_msg, f32[1,512]{1,0:T(1,128)S(1)} %get-tuple-element.23.b_msg, ...), custom_call_target="tpu_custom_call" | custom-call | flops 805306368 | bytes 3145728 | tf_op jit(solution)/shard_map/node/pallas_call | solution.py:402
  (1 shorter events, 0.0 us)
Async XLA Ops:
  4.6 8.9 %copy-start.9 = (s32[1,2,256]{2,1,0:T(2,128)S(1)}, s32[1,2,256]{2,1,0:T(2,128)}, u32[]{:S(2)}) copy-start(s32[1,2,256]{2,1,0:T(2,128)} %param.24) | copy-start | bytes 6148
  4.6 8.9 %copy-start.7 = (s32[1,32,16]{1,2,0:T(8,128)S(1)}, s32[1,32,16]{1,2,0:T(8,128)}, u32[]{:S(2)}) copy-start(s32[1,32,16]{1,2,0:T(8,128)} %param.27) | copy-start | bytes 6148
  4.6 9.1 %copy-start.8 = (s32[1,32,16]{1,2,0:T(8,128)S(1)}, s32[1,32,16]{1,2,0:T(8,128)}, u32[]{:S(2)}) copy-start(s32[1,32,16]{1,2,0:T(8,128)} %param.28) | copy-start | bytes 6148
  4.6 9.2 %copy-start = (bf16[320,512]{1,0:T(8,128)(2,1)S(1)}, bf16[320,512]{1,0:T(8,128)(2,1)}, u32[]{:S(2)}) copy-start(bf16[320,512]{1,0:T(8,128)(2,1)} %rest_4_.1) | copy-start | bytes 983044
  4.7 9.2 %copy-start.1 = (bf16[224,512]{1,0:T(8,128)(2,1)S(1)}, bf16[224,512]{1,0:T(8,128)(2,1)}, u32[]{:S(2)}) copy-start(bf16[224,512]{1,0:T(8,128)(2,1)} %w_ref.1) | copy-start | bytes 688132
  4.7 9.2 %copy-start.2 = (s32[1,4096]{1,0:T(1,128)S(1)}, s32[1,4096]{1,0:T(1,128)}, u32[]{:S(2)}) copy-start(s32[1,4096]{1,0:T(1,128)} %src_ref.1) | copy-start | bytes 49156
  4.7 9.2 %copy-start.3 = (s32[1,4096]{1,0:T(1,128)S(1)}, s32[1,4096]{1,0:T(1,128)}, u32[]{:S(2)}) copy-start(s32[1,4096]{1,0:T(1,128)} %dst_ref.1) | copy-start | bytes 49156
  4.7 9.2 %copy-start.4 = (f32[512]{0:T(512)S(1)}, f32[512]{0:T(512)}, u32[]{:S(2)}) copy-start(f32[512]{0:T(512)} %param.22) | copy-start | bytes 6148
  4.7 9.2 %copy-start.5 = (f32[512]{0:T(512)S(1)}, f32[512]{0:T(512)}, u32[]{:S(2)}) copy-start(f32[512]{0:T(512)} %param.34) | copy-start | bytes 6148
  4.7 9.2 %copy-start.6 = (f32[512]{0:T(512)S(1)}, f32[512]{0:T(512)}, u32[]{:S(2)}) copy-start(f32[512]{0:T(512)} %param.30) | copy-start | bytes 6148
  4.7 37.5 %all-to-all-start = ((bf16[32,8,4096]{2,1,0:T(8,128)(2,1)}), bf16[32,8,4096]{2,1,0:T(8,128)(2,1)}, u32[]{:S(2)}, u32[]{:S(2)}) async-start(bf16[32,8,4096]{2,1,0:T(8,128)(2,1)} %pack.1), calls=%async_computation | async-start | bytes 4194304 | tf_op jit(solution)/shard_map/all_to_all | solution.py:446
  46.1 10.2 %collective-permute-start = (bf16[256,256]{1,0:T(8,128)(2,1)S(1)}, bf16[256,256]{1,0:T(8,128)(2,1)S(1)}, u32[]{:S(2)}, u32[]{:S(2)}) collective-permute-start(bf16[256,256]{1,0:T(8,128)(2,1)S(1)} %get-tuple-element.17), channel_id=1, source_target_pairs={{0,32},{32,64},{64,96},{96,0},{1,33},{33,65},{65,97},{97,1},{2,34}... | collective-permute-start | bytes 393224 | tf_op jit(solution)/shard_map/ppermute | solution.py:471
  47.8 8.5 %collective-permute-start.1 = (bf16[256,256]{1,0:T(8,128)(2,1)S(1)}, bf16[256,256]{1,0:T(8,128)(2,1)S(1)}, u32[]{:S(2)}, u32[]{:S(2)}) collective-permute-start(bf16[256,256]{1,0:T(8,128)(2,1)S(1)} %get-tuple-element.18), channel_id=1, source_target_pairs={{32,0},{64,32},{96,64},{0,96},{33,1},{65,33},{97,65},{1,97},{34,2}... | collective-permute-start | bytes 393224 | tf_op jit(solution)/shard_map/ppermute | solution.py:472
  57.5 14.4 %all-to-all-start.1 = ((bf16[32,16,256]{2,1,0:T(8,128)(2,1)}), bf16[32,16,256]{2,1,0:T(8,128)(2,1)S(1)}, u32[]{:S(2)}, u32[]{:S(2)}) async-start(bf16[32,16,256]{2,1,0:T(8,128)(2,1)} %bitcast.5), calls=%async_computation.1 | async-start | bytes 524288 | tf_op jit(solution)/shard_map/all_to_all | solution.py:479

commit v4 on v3

--- a/solution.py
+++ b/solution.py
@@ -52,7 +52,8 @@
 
 def pack_kernel(me_ref, mean_ref, scale_ref, x_ref, o_ref, in_buf, out_buf, in_sem, out_sem, *, parts):
     chans, points = in_buf.shape
-    levels, _, pts = out_buf.shape
+    levels, _, main = out_buf.shape
+    pts = points // levels
     per = levels // parts
     width = per * pts
 
@@ -73,12 +74,12 @@
     for c in range(chans):
         mean = jnp.where(row == c, mean_ref[base + c], mean)
         scale = jnp.where(row == c, scale_ref[base + c], scale)
-    pad = jnp.ones((1, pts), F32)
     for k in range(parts):
         load(k).wait()
         for j in range(k * per, (k + 1) * per):
             val = (in_buf[:, j * pts : (j + 1) * pts] - mean) * scale
-            out_buf[j] = jnp.concatenate([val, pad], axis=0).astype(BF)
+            last = jnp.concatenate([val[c : c + 1, main:] for c in range(chans)], axis=1)
+            out_buf[j] = jnp.concatenate([val[:, :main], last], axis=0).astype(BF)
         store(k).start()
     for k in range(parts):
         store(k).wait()
@@ -89,7 +90,7 @@
     pts = points // levels
     parts = 8
     smem = pl.BlockSpec(memory_space=pltpu.SMEM)
-    shape = (levels, chans + 1, pts)
+    shape = (levels, chans + 1, pts * chans // (chans + 1))
     return pl.pallas_call(
         functools.partial(pack_kernel, parts=parts),
         in_specs=[smem, smem, smem, pl.BlockSpec(memory_space=pl.ANY)],
@@ -109,7 +110,7 @@
 
 def count_kernel(
     src_ref, dst_ref, w_ref, b_ref, mesh_ref, b_n, b_m, w_node, w_out, w_msg,
-    o_ref, w_in_ref, pre_ref, out_ref, msg_ref, bm_ref, nb_ref, hot_ref, na_ref, sem, *, chans,
+    o_ref, w_in_ref, pre_ref, out_ref, msg_ref, bi_ref, bm_ref, nb_ref, hot_ref, na_ref, sem, *, chans,
 ):
     nodes, edges = hot_ref.shape
     lat = w_out.shape[0]
@@ -131,14 +132,8 @@
     col = lax.broadcasted_iota(jnp.int32, shape, 1)
     lane = row % (chans + 1)
     place = jnp.where(lane < chans, row // (chans + 1) * chans + lane, -1)
-    w_in = dot(hot(col, place, 0.5), w_ref[...])
-    rest = 0.5 * b_ref[...]
-    row = lax.broadcasted_iota(jnp.int32, w_in.shape, 0)
-    for k in range(3):
-        part = rest.astype(BF).astype(F32)
-        rest = rest - part
-        w_in = jnp.where(row == (k + 3) * (chans + 1) - 1, part, w_in)
-    w_in_ref[...] = w_in.astype(BF)
+    w_in_ref[...] = dot(hot(col, place, 0.5), w_ref[...]).astype(BF)
+    bi_ref[...] = 0.5 * b_ref[...]
     bm_ref[...] = 0.5 * b_m[...]
 
     @pl.loop(0, o_ref.shape[1] // tile)
@@ -165,13 +160,14 @@
     return pl.pallas_call(
         functools.partial(count_kernel, chans=chans),
         in_specs=[VM] * 7 + [ANY] * 3,
-        out_specs=[VM] * 7,
+        out_specs=[VM] * 8,
         out_shape=(
             pltpu.HBM((nodes, table), BF),
             pltpu.VMEM((wide, lat), BF),
             pltpu.HBM((nodes, lat), F32),
             square,
             square,
+            pltpu.VMEM((1, lat), F32),
             pltpu.VMEM((1, lat), F32),
             pltpu.HBM((lat, lat), BF),
         ),
@@ -186,45 +182,51 @@
     )(src, dst, w_in, b_in, mesh, b_node, b_msg, *map(at_hbm, (w_node, w_out, w_msg)))
 
 
-def select_kernel(x_ref, idx_ref, src_ref, low_ref, high_ref, own_ref, keep_ref, near_hot, far_hot, sem):
-    pts = x_ref.shape[1]
+def hots(index, ref):
+    step = 1024
+    ids = lax.broadcasted_iota(jnp.int32, (step, ref.shape[1]), 0).astype(jnp.int16)
+    for start in range(0, ref.shape[0], step):
+        ref[pl.ds(start, step)] = hot(ids, (index - start).astype(jnp.int16))
+
+
+def select_kernel(x_ref, idx_ref, src_ref, low_ref, high_ref, own_ref, keep_ref, near_hot, far_hot, sem, *, chans):
+    rows, main = x_ref.shape
     half = low_ref.shape[1]
-    parts = sem.shape[0]
-    chunk = pts // parts
-
-    def load(c):
-        at = pl.ds(c * chunk, chunk)
-        return pltpu.make_async_copy(x_ref.at[:, at], keep_ref.at[:, at], sem.at[c])
-
-    for c in range(parts):
-        load(c).start()
-    rows = lax.broadcasted_iota(jnp.int32, (chunk, 2 * half), 0).astype(jnp.int16)
-    for c in range(parts):
-        at = pl.ds(c * chunk, chunk)
-        near_hot[at] = hot(rows, (idx_ref[...] - c * chunk).astype(jnp.int16))
-        far_hot[at] = hot(rows, (src_ref[...] - c * chunk).astype(jnp.int16))
-    for c in range(parts):
-        load(c).wait()
+    last = main // chans
+    group = chans + 1
+    load = pltpu.make_async_copy(x_ref, keep_ref.at[:, pl.ds(0, main)], sem)
+    load.start()
+    hots(idx_ref[...], near_hot)
+    hots(src_ref[...], far_hot)
+    load.wait()
+    row = lax.broadcasted_iota(jnp.int32, (1, group, 1), 1)
+    tail = jnp.zeros((rows // group, group, last), F32)
+    for c in range(chans):
+        part = keep_ref[:, c * last : (c + 1) * last].astype(F32).reshape(rows // group, group, last)
+        tail = jnp.where(row == c, part[:, chans:], tail)
+    tail = tail.reshape(rows, last).astype(BF)
+    keep_ref[:, main:] = tail
     near = dot(keep_ref[...], near_hot[...])
     low_ref[...] = near[:, :half].astype(BF)
     high_ref[...] = near[:, half:].astype(BF)
     own_ref[...] = dot(keep_ref[...], far_hot[...]).astype(BF)
 
 
-def select(x, idx, src):
-    rows, pts = x.shape
+def select(x, idx, src, chans):
+    rows, main = x.shape
+    pts = main // chans * (chans + 1)
     half = idx.shape[1] // 2
     slots = src.shape[1]
     out = jax.ShapeDtypeStruct((rows, half), BF)
     return pl.pallas_call(
-        select_kernel,
+        functools.partial(select_kernel, chans=chans),
         in_specs=[ANY, VM, VM],
         out_specs=[VM] * 4,
-        out_shape=(out, out, pltpu.VMEM((rows, slots), BF), pltpu.VMEM(x.shape, BF)),
+        out_shape=(out, out, pltpu.VMEM((rows, slots), BF), pltpu.VMEM((rows, pts), BF)),
         scratch_shapes=[
             pltpu.VMEM((pts, 2 * half), BF),
             pltpu.VMEM((pts, slots), BF),
-            pltpu.SemaphoreType.DMA((4,)),
+            pltpu.SemaphoreType.DMA,
         ],
         compiler_params=params(24),
         cost_estimate=cost(2 * rows * pts * (2 * half + slots), rows * pts * 2),
@@ -258,111 +260,108 @@
     )(*at_vmem(own, low, up), src, dst)
 
 
-def act_of(x, dims, w_in, w_out, w_msg, b_msg):
-    hidden = silu2(dot(x, w_in[...], dims))
+def act_of(x, dims, w_in, b_in, w_out, w_msg, b_msg):
+    hidden = silu2(dot(x, w_in[...], dims) + b_in[...])
     latent = dot(hidden, w_out[...]).astype(BF)
     return latent, silu2(dot(latent, w_msg[...]) + b_msg[...])
 
 
-def embed_tiles(x_ref, s_ref, weights, lat_hbm, sum_ref, buf, sem, first, steps, ready):
-    tile = buf.shape[1]
-
-    def store(i, slot):
-        at = pl.ds(pl.multiple_of((i + first) * tile, tile), tile)
-        return pltpu.make_async_copy(buf.at[slot], lat_hbm.at[at], sem.at[slot])
-
-    @pl.loop(0, steps)
-    def _(i):
-        slot = lax.rem(i, 2)
-
-        @pl.when(i >= 2)
-        def _():
-            store(i - 2, slot).wait()
-
-        ready(i)
-        at = pl.ds(pl.multiple_of(i * tile, tile), tile)
-        latent, act = act_of(x_ref[:, at], TN, *weights)
-        buf[slot] = latent
-        store(i, slot).start()
-        sum_ref[...] += dot(s_ref[:, at], act)
-
-    for i in range(max(steps - 2, 0), steps):
-        store(i, i % 2).wait()
-
-
-def columns(src, dst, sem, start):
-    width = dst.shape[1]
-    return pltpu.make_async_copy(src.at[:, pl.ds(start, width)], dst, sem)
-
-
-def first_kernel(
-    x_ref, w_in, w_out, w_msg, b_msg, s_hbm, lat_ref, sum_ref, s_buf, buf, sem, in_sem, *, first, steps
+def columns(src, dst, sem, spans):
+    copies = []
+    at = 0
+    for k, (start, width) in enumerate(spans):
+        copies.append(
+            pltpu.make_async_copy(
+                src.at[:, pl.ds(start, width)], dst.at[:, pl.ds(at, width)], sem.at[k]
+            )
+        )
+        copies[-1].start()
+        at += width
+    return copies
+
+
+def embed_tiles(x_ref, weights, lat_hbm, act_ref, buf, sem, starts, tile):
+    stores = []
+    for i, (col, point) in enumerate(starts):
+        rows = pl.ds(i * tile, tile)
+        latent, act = act_of(x_ref[:, col : col + tile], TN, *weights)
+        buf[rows] = latent
+        stores.append(
+            pltpu.make_async_copy(buf.at[rows], lat_hbm.at[pl.ds(point, tile)], sem.at[i])
+        )
+        stores[-1].start()
+        act_ref[rows] = act
+    return stores
+
+
+def first_kernel(x_ref, w_in, b_in, w_out, w_msg, b_msg, s_hbm, lat_ref, sum_ref, s_buf, act_buf, buf, sem, in_sem, *, spans, tile):
+    loads = columns(s_hbm, s_buf, in_sem, spans)
+    weights = (w_in, b_in, w_out, w_msg, b_msg)
+    starts = [(p, p) for start, width in spans for p in range(start, start + width, tile)]
+    stores = embed_tiles(x_ref, weights, lat_ref, act_buf, buf, sem, starts, tile)
+    for c in loads:
+        c.wait()
+    sum_ref[...] = dot(s_buf[...], act_buf[...])
+    for c in stores:
+        c.wait()
+
+
+def second_kernel(
+    low_ref, up_ref, before, w_in, b_in, w_out, w_msg, b_msg, s_hbm, x_hbm, _, lat_ref, sum_ref,
+    s_buf, act_buf, buf, x_buf, sem, in_sem, x_sem, *, spans, tile,
 ):
-    load = columns(s_hbm, s_buf, in_sem.at[0], 0)
-    load.start()
-    sum_ref[...] = jnp.zeros_like(sum_ref)
-
-    def ready(i):
-        @pl.when(i == 0)
-        def _():
-            load.wait()
-
-    embed_tiles(
-        x_ref, s_buf, (w_in, w_out, w_msg, b_msg), lat_ref, sum_ref, buf, sem, first, steps, ready
-    )
-
-
-def second_kernel(
-    low_ref, up_ref, before, w_in, w_out, w_msg, b_msg, s_hbm, x_hbm, _, lat_ref, sum_ref,
-    s_buf, x_buf, h_buf, buf, sem, in_sem, *, first, steps,
-):
-    weights = (w_in, w_out, w_msg, b_msg)
+    weights = (w_in, b_in, w_out, w_msg, b_msg)
     half = low_ref.shape[1]
-    start = first * buf.shape[1]
-    loads = (
-        columns(s_hbm, h_buf, in_sem.at[0], x_hbm.shape[1]),
-        columns(x_hbm, x_buf, in_sem.at[1], start),
-        columns(s_hbm, s_buf, in_sem.at[2], start),
-    )
+    x_load = columns(x_hbm, x_buf, x_sem, spans[:1])
+    loads = columns(s_hbm, s_buf, in_sem, spans)
+    start, width = spans[0]
+    for k, ref in enumerate((low_ref, up_ref)):
+        act_buf[pl.ds(width + k * half, half)] = act_of(ref[...], TN, *weights)[1]
+    x_load[0].wait()
+    starts = [(p, start + p) for p in range(0, width, tile)]
+    stores = embed_tiles(x_buf, weights, lat_ref, act_buf, buf, sem, starts, tile)
     for c in loads:
-        c.start()
-    acts = [act_of(ref[...], TN, *weights)[1] for ref in (low_ref, up_ref)]
-    loads[0].wait()
-    total = before[...]
-    for k, act in enumerate(acts):
-        total = total + dot(h_buf[:, k * half : (k + 1) * half], act)
-    sum_ref[...] = total
-    loads[1].wait()
-    loads[2].wait()
-    embed_tiles(x_buf, s_buf, weights, lat_ref, sum_ref, buf, sem, first, steps, lambda i: None)
-
-
-def embed(x, counts, weights, first, steps, tile, before=None):
-    rows, pts = x.shape
+        c.wait()
+    sum_ref[...] = before[...] + dot(s_buf[...], act_buf[...])
+    for c in stores:
+        c.wait()
+
+
+def embed(x, counts, weights, pts, spans, tile, before=None):
+    rows = x.shape[0]
     nodes = counts.shape[0]
     lat = weights[0].shape[1]
-    span = steps * tile
-    inner = [pltpu.VMEM((nodes, span), BF)]
+    wide = sum(width for _, width in spans)
     if before is None:
+        kernel = first_kernel
+        span = wide
         args = [*at_vmem(x, *weights), at_hbm(counts)]
-        specs = [VM] * 5 + [ANY]
+        specs = [VM] * 6 + [ANY]
         alias = {}
+        inner = []
+        tail = []
     else:
+        kernel = second_kernel
+        span = spans[0][1]
         latent, total, low, up = before
         args = [*at_vmem(low, up, total, *weights), at_hbm(counts), at_hbm(x), at_hbm(latent)]
-        specs = [VM] * 7 + [ANY] * 3
-        alias = {9: 0}
-        inner += [pltpu.VMEM((rows, span), BF), pltpu.VMEM((nodes, 2 * low.shape[1]), BF)]
+        specs = [VM] * 8 + [ANY] * 3
+        alias = {10: 0}
+        inner = [pltpu.VMEM((rows, span), BF)]
+        tail = [pltpu.SemaphoreType.DMA((1,))]
     return pl.pallas_call(
-        functools.partial(first_kernel if before is None else second_kernel, first=first, steps=steps),
+        functools.partial(kernel, spans=spans, tile=tile),
         in_specs=specs,
         out_specs=[ANY, VM],
         out_shape=(pltpu.HBM((pts, lat), BF), pltpu.VMEM((nodes, lat), F32)),
-        scratch_shapes=inner
-        + [
-            pltpu.VMEM((2, tile, lat), BF),
-            pltpu.SemaphoreType.DMA((2,)),
-            pltpu.SemaphoreType.DMA((3,)),
+        scratch_shapes=[
+            pltpu.VMEM((nodes, wide), BF),
+            pltpu.VMEM((wide, lat), BF),
+            pltpu.VMEM((span, lat), BF),
+            *inner,
+            pltpu.SemaphoreType.DMA((span // tile,)),
+            pltpu.SemaphoreType.DMA((len(spans),)),
+            *tail,
         ],
         input_output_aliases=alias,
         compiler_params=params(24),
@@ -371,7 +370,7 @@
     )(*args)
 
 
-def node_kernel(r_ref, w_in, w_out, w_msg, b_msg, sum_ref, *rest, pad):
+def node_kernel(r_ref, w_in, b_in, w_out, w_msg, b_msg, sum_ref, *rest, pad):
     sources, o_ref, buffers, sem = rest[:5], rest[5], rest[6:11], rest[11]
     loads = [pltpu.make_async_copy(f, t, sem.at[k]) for k, (f, t) in enumerate(zip(sources, buffers))]
     for c in loads:
@@ -379,7 +378,7 @@
     w_mo, w_nb, pre_ref, w_no, mesh_ref = buffers
     nodes = sum_ref.shape[0]
     rows = r_ref[...]
-    _, act = act_of(rows, (((1,), (0,)), ((), ())), w_in, w_out, w_msg, b_msg)
+    _, act = act_of(rows, (((1,), (0,)), ((), ())), w_in, b_in, w_out, w_msg, b_msg)
     lane = lax.broadcasted_iota(jnp.int32, (8, rows.shape[1]), 1)
     pick = jnp.where(lane == pad, 16.0, jnp.where(lane == 2 * pad + 1, 1.0, 0.0)).astype(BF)
     dst = dot(pick, rows, NT)[:1].astype(jnp.int32) - 1
@@ -444,9 +443,10 @@
     me = lax.axis_index("lev").astype(jnp.int32).reshape(1)
     sent = pack(me, chan_mean, chan_scale, fields, levels)
     got = lax.all_to_all(sent, "lev", split_axis=0, concat_axis=0, tiled=True)
-    x = got.reshape(wide, pts)
-
-    counts, w_in, pre, w_out, w_msg, b_half, w_nb = count_edges(
+    main = pts // (chans + 1) * chans
+    x = got.reshape(wide, main)
+
+    counts, w_in, pre, w_out, w_msg, b_in, b_out, w_nb = count_edges(
         local_src,
         local_dst,
         w_embed_in,
@@ -461,19 +461,19 @@
         wide,
         chans,
     )
-    weights = [w_in, w_out, w_msg, b_half]
+    weights = [w_in, b_in, w_out, w_msg, b_out]
 
     src = remote_src.reshape(1, -1)
     dst = remote_dst.reshape(1, -1)
-    low, high, own, kept = select(x, halo_index.reshape(1, 2 * halo), src)
+    low, high, own, kept = select(x, halo_index.reshape(1, 2 * halo), src, chans)
     ahead = [(i, (i + 1) % tiles) for i in range(tiles)]
     back = [(t, s) for s, t in ahead]
     from_low = lax.ppermute(high, "tile", ahead)
     from_up = lax.ppermute(low, "tile", back)
 
     tile = 512
-    steps = pts // tile
-    latent, total = embed(kept, counts, weights, 0, steps // 2, tile)
+    cut = pts // 2 - (pts - main)
+    latent, total = embed(kept, counts, weights, pts, ((0, cut), (main, pts - main)), tile)
 
     rows = slots_rows(own, from_low, from_up, src, dst, pts, chans)
     rows = lax.all_to_all(
@@ -481,7 +481,13 @@
     ).reshape(levels * slot_count, wide)
 
     latent, total = embed(
-        x, counts, weights, steps // 2, steps - steps // 2, tile, (latent, total, from_low, from_up)
+        x,
+        counts,
+        weights,
+        pts,
+        ((cut, main - cut), (pts, 2 * halo)),
+        tile,
+        (latent, total, from_low, from_up),
     )
     mesh_out = node_update(
         rows, weights, total, w_msg_out, mesh_nodes, pre, w_nb, w_node_out, chans

time: 76 us -> 71.3 us (0.938)
  Pallas kernels: 42.8 us -> 39.8 us
  waiting for transfers between devices: 13.4 us -> 11.6 us
    all_to_all x1, waiting for transfers between devices: 11.6 us -> 8.63 us  [shards(): got = lax.all_to_all(sent, 'lev', split_axis=0, concat_axis=0, tiled=True)]
    pallas_call x3, Pallas kernels: 17.4 us -> 14.5 us  [the longest x2 10.5 us: embed(): pl.pallas_call(functools.partial(kernel, spans=spans, tile=tile), in_spec...]
    all_to_all x1, waiting for transfers between devices: 1.79 us -> 2.93 us  [shards(): lax.all_to_all(rows.reshape(levels, slot_count, wide), 'lev', split_axis=...]
  transfers between devices with their start and end apart: 4 -> 4, of which waited for: 2 -> 2; matrix products, arithmetic and copies ran while one was open for 0% -> 0% of each run, Pallas kernels for 40% -> 38%
where the time goes in v4:
time: 71.3 us; the launch traced here: 70.8 us
  Pallas kernels  39.8 us (56%)
  starting transfers between devices  18 us (25%)
  waiting for transfers between devices  11.6 us (16%)
  between operations  1.03 us (1%)
    pallas_call x1, Pallas kernels, count_edges(): pl.pallas_call(functools.partial(count_kernel, chans=chans), in_specs=[VM...  16.7 us
    pallas_call x2, Pallas kernels, embed(): pl.pallas_call(functools.partial(kernel, spans=spans, tile=tile), in_spec...  10.5 us
    all_to_all x1, starting transfers between devices, shards(): got = lax.all_to_all(sent, 'lev', split_axis=0, concat_axis=0, tiled=True)  8.77 us
    all_to_all x1, waiting for transfers between devices, shards(): got = lax.all_to_all(sent, 'lev', split_axis=0, concat_axis=0, tiled=True)  8.63 us
    all_to_all x1, starting transfers between devices, shards(): lax.all_to_all(rows.reshape(levels, slot_count, wide), 'lev', split_axis=...  5.36 us
    pallas_call x1, Pallas kernels, select(): pl.pallas_call(functools.partial(select_kernel, chans=chans), in_specs=[A...  4.02 us
    pallas_call x1, Pallas kernels, pack(): pl.pallas_call(functools.partial(pack_kernel, parts=parts), in_specs=[sme...  3.92 us
    pallas_call x1, Pallas kernels, node_update(): pl.pallas_call(functools.partial(node_kernel, pad=pad), in_specs=[VM] * l...  3.58 us
  transfers between devices with their start and end apart: 4, of which 2 were waited for; matrix products, arithmetic and copies ran while one was open for 0% of the time, Pallas kernels for 38%

profile of v4, /device:TPU:1, one launch (start us, length us, event | category | flops | bytes accessed | tf_op | source)
XLA Modules:
  0.0 70.8 jit_solution(16681941467600708023)
XLA Ops:
  0.6 3.9 %pack.1 = bf16[32,8,3584]{2,1,0:T(8,128)(2,1)} custom-call(s32[1]{0:T(128)} %bitcast.me_ref, f32[224]{0:T(256)} %mean_ref.1, f32[224]{0:T(256)} %scale_ref.1, f32[7,131072]{1,0:T(8,128)} %x_ref.1), custom_call_target="tpu_custom_call" | custom-call | flops 2097152 | bytes 6291456 | tf_op jit(solution)/shard_map/pack/pallas_call | solution.py:94
  4.6 0.0 copy-start.9
  4.6 0.0 copy-start.7
  4.6 0.0 copy-start.8
  4.6 0.0 copy-start
  4.6 0.0 copy-start.1
  4.6 0.0 copy-start.2
  4.6 0.0 copy-start.3
  4.6 0.0 copy-start.4
  4.7 0.0 copy-start.5
  4.7 0.0 copy-start.6
  4.7 8.8 %all-to-all-start = ((bf16[32,8,3584]{2,1,0:T(8,128)(2,1)}), bf16[32,8,3584]{2,1,0:T(8,128)(2,1)}, u32[]{:S(2)}, u32[]{:S(2)}) async-start(bf16[32,8,3584]{2,1,0:T(8,128)(2,1)} %pack.1), calls=%async_computation | async-start | bytes 3670016 | tf_op jit(solution)/shard_map/all_to_all | solution.py:445
  13.5 0.0 copy-done.9
  13.5 0.0 copy-done.7
  13.5 0.1 copy.23
  13.6 0.1 reshape.28.src_ref
  13.7 0.0 copy-done.8
  13.7 0.1 copy.24
  13.7 0.1 reshape.29.dst_ref
  13.8 0.0 copy-done
  13.8 0.0 copy-done.1
  13.8 0.0 copy-done.2
  13.8 0.0 copy-done.3
  13.8 0.0 copy-done.4
  13.9 0.0 copy-done.5
  13.9 0.0 copy-done.6
  13.9 16.7 %count.1 = (bf16[320,4608]{1,0:T(8,128)(2,1)}, bf16[256,512]{1,0:T(8,128)(2,1)S(1)}, f32[320,512]{1,0:T(8,128)}, bf16[512,512]{1,0:T(8,128)(2,1)S(1)}, bf16[512,...) custom-call(s32[1,4096]{1,0:T(1,128)S(1)} %copy-done.2, ...), custom_call_target="tpu_custom_call" | custom-call | flops 12079595520 | bytes 2949120 | tf_op jit(solution)/shard_map/count/pallas_call | solution.py:160
  30.6 8.6 %all-to-all-done = bf16[32,8,3584]{2,1,0:T(8,128)(2,1)} async-done(((bf16[32,8,3584]{2,1,0:T(8,128)(2,1)}), bf16[32,8,3584]{2,1,0:T(8,128)(2,1)}, u32[]{:S(2)}, u32[]{:S(2)}) %all-to-all-start) | async-done | bytes 1835040 | tf_op jit(solution)/shard_map/all_to_all | solution.py:445
  39.2 4.0 %select.1 = (bf16[256,256]{1,0:T(8,128)(2,1)S(1)}, bf16[256,256]{1,0:T(8,128)(2,1)S(1)}, bf16[256,512]{1,0:T(8,128)(2,1)S(1)}, bf16[256,4096]{1,0:T(8,128)(2,1)S(1)}) custom-call(bf16[256,3584]{1,0:T(8,128)(2,1)} %bitcast.1.x_ref.x_hbm, s32[1,512]{1,0:T(1,128)S(1)} %bitcast.10, s32[1,512]{1,0:T(1,128)S(1)} %reshape.28.src_ref), custom_call_target="tpu_custom_call" | custom-call | flops 2147483648 | bytes 2097152 | tf_op jit(solution)/shard_map/select/pallas_call | solution.py:221
  43.2 1.7 %collective-permute-start = (bf16[256,256]{1,0:T(8,128)(2,1)S(1)}, bf16[256,256]{1,0:T(8,128)(2,1)S(1)}, u32[]{:S(2)}, u32[]{:S(2)}) collective-permute-start(bf16[256,256]{1,0:T(8,128)(2,1)S(1)} %get-tuple-element.18), channel_id=1, source_target_pairs={{0,32},{32,64},{64,96},{96,0},{1,33},{33,65},{65,97},{97,1},{2,34}... | collective-permute-start | bytes 393224 | tf_op jit(solution)/shard_map/ppermute | solution.py:471
  45.0 2.2 %collective-permute-start.1 = (bf16[256,256]{1,0:T(8,128)(2,1)S(1)}, bf16[256,256]{1,0:T(8,128)(2,1)S(1)}, u32[]{:S(2)}, u32[]{:S(2)}) collective-permute-start(bf16[256,256]{1,0:T(8,128)(2,1)S(1)} %get-tuple-element.19), channel_id=1, source_target_pairs={{32,0},{64,32},{96,64},{0,96},{33,1},{65,33},{97,65},{1,97},{34,2}... | collective-permute-start | bytes 393224 | tf_op jit(solution)/shard_map/ppermute | solution.py:472
  47.2 4.5 %embed.2 = (bf16[4096,512]{1,0:T(8,128)(2,1)}, f32[320,512]{1,0:T(8,128)S(1)}) custom-call(bf16[256,4096]{1,0:T(8,128)(2,1)S(1)} %get-tuple-element.20.x_ref, bf16[256,512]{1,0:T(8,128)(2,1)S(1)} %get-tuple-element.21.w_in, f32[1,512]{1,0:T(1,128)S(1)} %get-tuple-element.22.b_in, bf16[512,512]{1,0:T(8,128)(2,1)S(1)} %get-tuple-element.23.w_out, ...), custom_call_target="tpu_custom_call" | custom-call | flops 3355443200 | bytes 3145728 | tf_op jit(solution)/shard_map/embed/pallas_call | solution.py:352
  51.6 0.0 collective-permute-done.low_ref
  51.6 0.0 collective-permute-done.1.up_ref
  51.7 1.1 %slots.1 = bf16[512,256]{1,0:T(8,128)(2,1)} custom-call(bf16[256,512]{1,0:T(8,128)(2,1)S(1)} %get-tuple-element.30.own_ref, bf16[256,256]{1,0:T(8,128)(2,1)S(1)} %collective-permute-done.low_ref, bf16[256,256]{1,0:T(8,128)(2,1)S(1)} %collective-permute-done.1.up_ref, s32[1,512]{1,0:T(1,128)S(1)} %reshape.28.src_ref, s32[1,512]{1,0:T(1,128)S(1)} %reshape.29.dst_ref), custom_call_target="tpu_custom_call" | custom-call | flops 134217728 | bytes 524288 | tf_op jit(solution)/shard_map/slots/pallas_call | solution.py:253
  52.7 5.4 %all-to-all-start.1 = ((bf16[32,16,256]{2,1,0:T(8,128)(2,1)}), bf16[32,16,256]{2,1,0:T(8,128)(2,1)S(1)}, u32[]{:S(2)}, u32[]{:S(2)}) async-start(bf16[32,16,256]{2,1,0:T(8,128)(2,1)} %bitcast.5), calls=%async_computation.1 | async-start | bytes 524288 | tf_op jit(solution)/shard_map/all_to_all | solution.py:479
  58.1 6.0 %embed.3 = (bf16[4096,512]{1,0:T(8,128)(2,1)}, f32[320,512]{1,0:T(8,128)S(1)}) custom-call(bf16[256,256]{1,0:T(8,128)(2,1)S(1)} %collective-permute-done.low_ref, bf16[256,256]{1,0:T(8,128)(2,1)S(1)} %collective-permute-done.1.up_ref, f32[320,512]{1,0:T(8,128)S(1)} %get-tuple-element.27.before, ...), custom_call_target="tpu_custom_call", output_to_operand_aliasing={{0}: (10, {})} | custom-call | flops 3355443200 | bytes 3145728 | tf_op jit(solution)/shard_map/embed/pallas_call | solution.py:352
  64.2 2.9 %all-to-all-done.1 = bf16[32,16,256]{2,1,0:T(8,128)(2,1)S(1)} async-done(((bf16[32,16,256]{2,1,0:T(8,128)(2,1)}), bf16[32,16,256]{2,1,0:T(8,128)(2,1)S(1)}, u32[]{:S(2)}, u32[]{:S(2)}) %all-to-all-start.1) | async-done | bytes 262176 | tf_op jit(solution)/shard_map/all_to_all | solution.py:479
  67.1 3.6 %node.1 = bf16[320,512]{1,0:T(8,128)(2,1)} custom-call(bf16[512,256]{1,0:T(8,128)(2,1)S(1)} %bitcast.9, bf16[256,512]{1,0:T(8,128)(2,1)S(1)} %get-tuple-element.21.w_in, f32[1,512]{1,0:T(1,128)S(1)} %get-tuple-element.22.b_in, bf16[512,512]{1,0:T(8,128)(2,1)S(1)} %get-tuple-element.23.w_out, bf16[512,512]{1,0:T(8,128)(2,1)S(1)} %get-tuple-element.24.w_msg, ...), custom_call_target="tpu_custom_call" | custom-call | flops 805306368 | bytes 3145728 | tf_op jit(solution)/shard_map/node/pallas_call | solution.py:401
  (1 shorter events, 0.0 us)
Async XLA Ops:
  4.6 8.9 %copy-start.9 = (s32[1,2,256]{2,1,0:T(2,128)S(1)}, s32[1,2,256]{2,1,0:T(2,128)}, u32[]{:S(2)}) copy-start(s32[1,2,256]{2,1,0:T(2,128)} %param.24) | copy-start | bytes 6148
  4.6 8.9 %copy-start.7 = (s32[1,32,16]{1,2,0:T(8,128)S(1)}, s32[1,32,16]{1,2,0:T(8,128)}, u32[]{:S(2)}) copy-start(s32[1,32,16]{1,2,0:T(8,128)} %param.27) | copy-start | bytes 6148
  4.6 9.1 %copy-start.8 = (s32[1,32,16]{1,2,0:T(8,128)S(1)}, s32[1,32,16]{1,2,0:T(8,128)}, u32[]{:S(2)}) copy-start(s32[1,32,16]{1,2,0:T(8,128)} %param.28) | copy-start | bytes 6148
  4.6 9.2 %copy-start = (bf16[320,512]{1,0:T(8,128)(2,1)S(1)}, bf16[320,512]{1,0:T(8,128)(2,1)}, u32[]{:S(2)}) copy-start(bf16[320,512]{1,0:T(8,128)(2,1)} %rest_4_.1) | copy-start | bytes 983044
  4.6 9.2 %copy-start.1 = (bf16[224,512]{1,0:T(8,128)(2,1)S(1)}, bf16[224,512]{1,0:T(8,128)(2,1)}, u32[]{:S(2)}) copy-start(bf16[224,512]{1,0:T(8,128)(2,1)} %w_ref.1) | copy-start | bytes 688132
  4.6 9.2 %copy-start.2 = (s32[1,4096]{1,0:T(1,128)S(1)}, s32[1,4096]{1,0:T(1,128)}, u32[]{:S(2)}) copy-start(s32[1,4096]{1,0:T(1,128)} %src_ref.1) | copy-start | bytes 49156
  4.6 9.2 %copy-start.3 = (s32[1,4096]{1,0:T(1,128)S(1)}, s32[1,4096]{1,0:T(1,128)}, u32[]{:S(2)}) copy-start(s32[1,4096]{1,0:T(1,128)} %dst_ref.1) | copy-start | bytes 49156
  4.6 9.2 %copy-start.4 = (f32[512]{0:T(512)S(1)}, f32[512]{0:T(512)}, u32[]{:S(2)}) copy-start(f32[512]{0:T(512)} %param.22) | copy-start | bytes 6148
  4.7 9.2 %copy-start.5 = (f32[512]{0:T(512)S(1)}, f32[512]{0:T(512)}, u32[]{:S(2)}) copy-start(f32[512]{0:T(512)} %param.34) | copy-start | bytes 6148
  4.7 9.2 %copy-start.6 = (f32[512]{0:T(512)S(1)}, f32[512]{0:T(512)}, u32[]{:S(2)}) copy-start(f32[512]{0:T(512)} %param.30) | copy-start | bytes 6148
  4.7 34.5 %all-to-all-start = ((bf16[32,8,3584]{2,1,0:T(8,128)(2,1)}), bf16[32,8,3584]{2,1,0:T(8,128)(2,1)}, u32[]{:S(2)}, u32[]{:S(2)}) async-start(bf16[32,8,3584]{2,1,0:T(8,128)(2,1)} %pack.1), calls=%async_computation | async-start | bytes 3670016 | tf_op jit(solution)/shard_map/all_to_all | solution.py:445
  43.2 8.4 %collective-permute-start = (bf16[256,256]{1,0:T(8,128)(2,1)S(1)}, bf16[256,256]{1,0:T(8,128)(2,1)S(1)}, u32[]{:S(2)}, u32[]{:S(2)}) collective-permute-start(bf16[256,256]{1,0:T(8,128)(2,1)S(1)} %get-tuple-element.18), channel_id=1, source_target_pairs={{0,32},{32,64},{64,96},{96,0},{1,33},{33,65},{65,97},{97,1},{2,34}... | collective-permute-start | bytes 393224 | tf_op jit(solution)/shard_map/ppermute | solution.py:471
  45.0 6.7 %collective-permute-start.1 = (bf16[256,256]{1,0:T(8,128)(2,1)S(1)}, bf16[256,256]{1,0:T(8,128)(2,1)S(1)}, u32[]{:S(2)}, u32[]{:S(2)}) collective-permute-start(bf16[256,256]{1,0:T(8,128)(2,1)S(1)} %get-tuple-element.19), channel_id=1, source_target_pairs={{32,0},{64,32},{96,64},{0,96},{33,1},{65,33},{97,65},{1,97},{34,2}... | collective-permute-start | bytes 393224 | tf_op jit(solution)/shard_map/ppermute | solution.py:472
  52.7 14.3 %all-to-all-start.1 = ((bf16[32,16,256]{2,1,0:T(8,128)(2,1)}), bf16[32,16,256]{2,1,0:T(8,128)(2,1)S(1)}, u32[]{:S(2)}, u32[]{:S(2)}) async-start(bf16[32,16,256]{2,1,0:T(8,128)(2,1)} %bitcast.5), calls=%async_computation.1 | async-start | bytes 524288 | tf_op jit(solution)/shard_map/all_to_all | solution.py:479

commit v5 on v4

--- a/solution.py
+++ b/solution.py
@@ -11,6 +11,7 @@
 F32 = jnp.float32
 NT = (((1,), (1,)), ((), ()))
 TN = (((0,), (0,)), ((), ()))
+CUT = 1
 MIB = 1024 * 1024
 
 
@@ -189,7 +190,7 @@
         ref[pl.ds(start, step)] = hot(ids, (index - start).astype(jnp.int16))
 
 
-def select_kernel(x_ref, idx_ref, src_ref, low_ref, high_ref, own_ref, keep_ref, near_hot, far_hot, sem, *, chans):
+def select_kernel(x_ref, idx_ref, low_ref, high_ref, keep_ref, near_hot, sem, *, chans):
     rows, main = x_ref.shape
     half = low_ref.shape[1]
     last = main // chans
@@ -197,8 +198,8 @@
     load = pltpu.make_async_copy(x_ref, keep_ref.at[:, pl.ds(0, main)], sem)
     load.start()
     hots(idx_ref[...], near_hot)
-    hots(src_ref[...], far_hot)
     load.wait()
+    near = dot(keep_ref[:, :main], near_hot[:main])
     row = lax.broadcasted_iota(jnp.int32, (1, group, 1), 1)
     tail = jnp.zeros((rows // group, group, last), F32)
     for c in range(chans):
@@ -206,32 +207,26 @@
         tail = jnp.where(row == c, part[:, chans:], tail)
     tail = tail.reshape(rows, last).astype(BF)
     keep_ref[:, main:] = tail
-    near = dot(keep_ref[...], near_hot[...])
+    near = near + dot(tail, near_hot[main:])
     low_ref[...] = near[:, :half].astype(BF)
     high_ref[...] = near[:, half:].astype(BF)
-    own_ref[...] = dot(keep_ref[...], far_hot[...]).astype(BF)
-
-
-def select(x, idx, src, chans):
+
+
+def select(x, idx, chans):
     rows, main = x.shape
     pts = main // chans * (chans + 1)
     half = idx.shape[1] // 2
-    slots = src.shape[1]
     out = jax.ShapeDtypeStruct((rows, half), BF)
     return pl.pallas_call(
         functools.partial(select_kernel, chans=chans),
-        in_specs=[ANY, VM, VM],
-        out_specs=[VM] * 4,
-        out_shape=(out, out, pltpu.VMEM((rows, slots), BF), pltpu.VMEM((rows, pts), BF)),
-        scratch_shapes=[
-            pltpu.VMEM((pts, 2 * half), BF),
-            pltpu.VMEM((pts, slots), BF),
-            pltpu.SemaphoreType.DMA,
-        ],
+        in_specs=[ANY, VM],
+        out_specs=[VM] * 3,
+        out_shape=(out, out, pltpu.VMEM((rows, pts), BF)),
+        scratch_shapes=[pltpu.VMEM((pts, 2 * half), BF), pltpu.SemaphoreType.DMA],
         compiler_params=params(24),
-        cost_estimate=cost(2 * rows * pts * (2 * half + slots), rows * pts * 2),
+        cost_estimate=cost(4 * rows * pts * half, rows * pts * 2),
         name="select",
-    )(at_hbm(x), idx, src)
+    )(at_hbm(x), idx)
 
 
 def slots_kernel(own_ref, low_ref, up_ref, src_ref, dst_ref, o_ref, *, start, pad):
@@ -294,11 +289,16 @@
     return stores
 
 
-def first_kernel(x_ref, w_in, b_in, w_out, w_msg, b_msg, s_hbm, lat_ref, sum_ref, s_buf, act_buf, buf, sem, in_sem, *, spans, tile):
+def first_kernel(
+    x_ref, src_ref, w_in, b_in, w_out, w_msg, b_msg, s_hbm, lat_ref, sum_ref, own_ref,
+    s_buf, act_buf, buf, far_hot, sem, in_sem, *, spans, tile,
+):
     loads = columns(s_hbm, s_buf, in_sem, spans)
     weights = (w_in, b_in, w_out, w_msg, b_msg)
     starts = [(p, p) for start, width in spans for p in range(start, start + width, tile)]
+    hots(src_ref[...], far_hot)
     stores = embed_tiles(x_ref, weights, lat_ref, act_buf, buf, sem, starts, tile)
+    own_ref[...] = dot(x_ref[...], far_hot[...]).astype(BF)
     for c in loads:
         c.wait()
     sum_ref[...] = dot(s_buf[...], act_buf[...])
@@ -327,7 +327,7 @@
         c.wait()
 
 
-def embed(x, counts, weights, pts, spans, tile, before=None):
+def embed(x, counts, weights, pts, spans, tile, src=None, before=None):
     rows = x.shape[0]
     nodes = counts.shape[0]
     lat = weights[0].shape[1]
@@ -335,11 +335,12 @@
     if before is None:
         kernel = first_kernel
         span = wide
-        args = [*at_vmem(x, *weights), at_hbm(counts)]
-        specs = [VM] * 6 + [ANY]
+        args = [*at_vmem(x), src, *at_vmem(*weights), at_hbm(counts)]
+        specs = [VM] * 7 + [ANY]
         alias = {}
-        inner = []
+        inner = [pltpu.VMEM((pts, src.shape[1]), BF)]
         tail = []
+        more = [pltpu.VMEM((rows, src.shape[1]), BF)]
     else:
         kernel = second_kernel
         span = spans[0][1]
@@ -349,11 +350,12 @@
         alias = {10: 0}
         inner = [pltpu.VMEM((rows, span), BF)]
         tail = [pltpu.SemaphoreType.DMA((1,))]
+        more = []
     return pl.pallas_call(
         functools.partial(kernel, spans=spans, tile=tile),
         in_specs=specs,
-        out_specs=[ANY, VM],
-        out_shape=(pltpu.HBM((pts, lat), BF), pltpu.VMEM((nodes, lat), F32)),
+        out_specs=[ANY, VM] + [VM] * len(more),
+        out_shape=(pltpu.HBM((pts, lat), BF), pltpu.VMEM((nodes, lat), F32), *more),
         scratch_shapes=[
             pltpu.VMEM((nodes, wide), BF),
             pltpu.VMEM((wide, lat), BF),
@@ -465,15 +467,17 @@
 
     src = remote_src.reshape(1, -1)
     dst = remote_dst.reshape(1, -1)
-    low, high, own, kept = select(x, halo_index.reshape(1, 2 * halo), src, chans)
+    low, high, kept = select(x, halo_index.reshape(1, 2 * halo), chans)
     ahead = [(i, (i + 1) % tiles) for i in range(tiles)]
     back = [(t, s) for s, t in ahead]
     from_low = lax.ppermute(high, "tile", ahead)
     from_up = lax.ppermute(low, "tile", back)
 
     tile = 512
-    cut = pts // 2 - (pts - main)
-    latent, total = embed(kept, counts, weights, pts, ((0, cut), (main, pts - main)), tile)
+    cut = CUT * tile
+    latent, total, own = embed(
+        kept, counts, weights, pts, ((0, cut), (main, pts - main)), tile, src
+    )
 
     rows = slots_rows(own, from_low, from_up, src, dst, pts, chans)
     rows = lax.all_to_all(
@@ -487,7 +491,7 @@
         pts,
         ((cut, main - cut), (pts, 2 * halo)),
         tile,
-        (latent, total, from_low, from_up),
+        before=(latent, total, from_low, from_up),
     )
     mesh_out = node_update(
         rows, weights, total, w_msg_out, mesh_nodes, pre, w_nb, w_node_out, chans

time: 71.3 us -> 69.9 us (0.980)
  waiting for transfers between devices: 11.6 us -> 9.38 us
  Pallas kernels: 39.8 us -> 40.6 us
    all_to_all x1, waiting for transfers between devices: 2.93 us -> 0.74 us  [shards(): lax.all_to_all(rows.reshape(levels, slot_count, wide), 'lev', split_axis=...]
    pallas_call x2, Pallas kernels: 10.5 us -> 12.4 us  [embed(): pl.pallas_call(functools.partial(kernel, spans=spans, tile=tile), in_spec...]
    pallas_call x1, Pallas kernels: 4.02 us -> 2.98 us  [select(): pl.pallas_call(functools.partial(select_kernel, chans=chans), in_specs=[A...]
  transfers between devices with their start and end apart: 4 -> 4, of which waited for: 2 -> 2; matrix products, arithmetic and copies ran while one was open for 0% -> 0% of each run, Pallas kernels for 38% -> 42%
where the time goes in v5:
time: 69.9 us; the launch traced here: 69.5 us
  Pallas kernels  40.6 us (58%)
  starting transfers between devices  18.1 us (26%)
  waiting for transfers between devices  9.38 us (13%)
  between operations  1.03 us (1%)
    pallas_call x1, Pallas kernels, count_edges(): pl.pallas_call(functools.partial(count_kernel, chans=chans), in_specs=[VM...  16.7 us
    pallas_call x2, Pallas kernels, embed(): pl.pallas_call(functools.partial(kernel, spans=spans, tile=tile), in_spec...  12.4 us
    all_to_all x1, starting transfers between devices, shards(): got = lax.all_to_all(sent, 'lev', split_axis=0, concat_axis=0, tiled=True)  8.77 us
    all_to_all x1, waiting for transfers between devices, shards(): got = lax.all_to_all(sent, 'lev', split_axis=0, concat_axis=0, tiled=True)  8.63 us
    all_to_all x1, starting transfers between devices, shards(): lax.all_to_all(rows.reshape(levels, slot_count, wide), 'lev', split_axis=...  5.37 us
    pallas_call x1, Pallas kernels, pack(): pl.pallas_call(functools.partial(pack_kernel, parts=parts), in_specs=[sme...  3.92 us
    pallas_call x1, Pallas kernels, node_update(): pl.pallas_call(functools.partial(node_kernel, pad=pad), in_specs=[VM] * l...  3.58 us
    pallas_call x1, Pallas kernels, select(): pl.pallas_call(functools.partial(select_kernel, chans=chans), in_specs=[A...  2.98 us
  transfers between devices with their start and end apart: 4, of which 2 were waited for; matrix products, arithmetic and copies ran while one was open for 0% of the time, Pallas kernels for 42%

profile of v5, /device:TPU:1, one launch (start us, length us, event | category | flops | bytes accessed | tf_op | source)
XLA Modules:
  0.0 69.5 jit_solution(18181711887222325770)
XLA Ops:
  0.6 3.9 %pack.1 = bf16[32,8,3584]{2,1,0:T(8,128)(2,1)} custom-call(s32[1]{0:T(128)} %bitcast.me_ref, f32[224]{0:T(256)} %mean_ref.1, f32[224]{0:T(256)} %scale_ref.1, f32[7,131072]{1,0:T(8,128)} %x_ref.1), custom_call_target="tpu_custom_call" | custom-call | flops 2097152 | bytes 6291456 | tf_op jit(solution)/shard_map/pack/pallas_call | solution.py:95
  4.6 0.0 copy-start.9
  4.6 0.0 copy-start.7
  4.6 0.0 copy-start.8
  4.6 0.0 copy-start
  4.6 0.0 copy-start.1
  4.6 0.0 copy-start.2
  4.6 0.0 copy-start.3
  4.6 0.0 copy-start.4
  4.7 0.0 copy-start.5
  4.7 0.0 copy-start.6
  4.7 8.8 %all-to-all-start = ((bf16[32,8,3584]{2,1,0:T(8,128)(2,1)}), bf16[32,8,3584]{2,1,0:T(8,128)(2,1)}, u32[]{:S(2)}, u32[]{:S(2)}) async-start(bf16[32,8,3584]{2,1,0:T(8,128)(2,1)} %pack.1), calls=%async_computation | async-start | bytes 3670016 | tf_op jit(solution)/shard_map/all_to_all | solution.py:447
  13.5 0.0 copy-done.9
  13.5 0.0 copy-done.7
  13.5 0.1 copy.23
  13.6 0.1 reshape.28.src_ref
  13.7 0.0 copy-done.8
  13.7 0.1 copy.24
  13.7 0.1 reshape.29.dst_ref
  13.8 0.0 copy-done
  13.8 0.0 copy-done.1
  13.8 0.0 copy-done.2
  13.8 0.0 copy-done.3
  13.8 0.0 copy-done.4
  13.9 0.0 copy-done.5
  13.9 0.0 copy-done.6
  13.9 16.7 %count.1 = (bf16[320,4608]{1,0:T(8,128)(2,1)}, bf16[256,512]{1,0:T(8,128)(2,1)S(1)}, f32[320,512]{1,0:T(8,128)}, bf16[512,512]{1,0:T(8,128)(2,1)S(1)}, bf16[512,...) custom-call(s32[1,4096]{1,0:T(1,128)S(1)} %copy-done.2, ...), custom_call_target="tpu_custom_call" | custom-call | flops 12079595520 | bytes 2949120 | tf_op jit(solution)/shard_map/count/pallas_call | solution.py:161
  30.6 8.6 %all-to-all-done = bf16[32,8,3584]{2,1,0:T(8,128)(2,1)} async-done(((bf16[32,8,3584]{2,1,0:T(8,128)(2,1)}), bf16[32,8,3584]{2,1,0:T(8,128)(2,1)}, u32[]{:S(2)}, u32[]{:S(2)}) %all-to-all-start) | async-done | bytes 1835040 | tf_op jit(solution)/shard_map/all_to_all | solution.py:447
  39.2 3.0 %select.1 = (bf16[256,256]{1,0:T(8,128)(2,1)S(1)}, bf16[256,256]{1,0:T(8,128)(2,1)S(1)}, bf16[256,4096]{1,0:T(8,128)(2,1)S(1)}) custom-call(bf16[256,3584]{1,0:T(8,128)(2,1)} %bitcast.1.x_ref.x_hbm, s32[1,512]{1,0:T(1,128)S(1)} %bitcast.10), custom_call_target="tpu_custom_call" | custom-call | flops 1073741824 | bytes 2097152 | tf_op jit(solution)/shard_map/select/pallas_call | solution.py:220
  42.2 1.7 %collective-permute-start = (bf16[256,256]{1,0:T(8,128)(2,1)S(1)}, bf16[256,256]{1,0:T(8,128)(2,1)S(1)}, u32[]{:S(2)}, u32[]{:S(2)}) collective-permute-start(bf16[256,256]{1,0:T(8,128)(2,1)S(1)} %get-tuple-element.18), channel_id=1, source_target_pairs={{0,32},{32,64},{64,96},{96,0},{1,33},{33,65},{65,97},{97,1},{2,34}... | collective-permute-start | bytes 393224 | tf_op jit(solution)/shard_map/ppermute | solution.py:473
  43.9 2.2 %collective-permute-start.1 = (bf16[256,256]{1,0:T(8,128)(2,1)S(1)}, bf16[256,256]{1,0:T(8,128)(2,1)S(1)}, u32[]{:S(2)}, u32[]{:S(2)}) collective-permute-start(bf16[256,256]{1,0:T(8,128)(2,1)S(1)} %get-tuple-element.19), channel_id=1, source_target_pairs={{32,0},{64,32},{96,64},{0,96},{33,1},{65,33},{97,65},{1,97},{34,2}... | collective-permute-start | bytes 393224 | tf_op jit(solution)/shard_map/ppermute | solution.py:474
  46.1 4.1 %embed.2 = (bf16[4096,512]{1,0:T(8,128)(2,1)}, f32[320,512]{1,0:T(8,128)S(1)}, bf16[256,512]{1,0:T(8,128)(2,1)S(1)}) custom-call(bf16[256,4096]{1,0:T(8,128)(2,1)S(1)} %get-tuple-element.20.x_ref, s32[1,512]{1,0:T(1,128)S(1)} %reshape.28.src_ref, bf16[256,512]{1,0:T(8,128)(2,1)S(1)} %get-tuple-element.21.w_in, f32[1,512]{1,0:T(1,128)S(1)} %get-tuple-element.22.b_in, ...), custom_call_target="tpu_custom_call" | custom-call | flops 1677721600 | bytes 1572864 | tf_op jit(solution)/shard_map/embed/pallas_call | solution.py:354
  50.2 0.0 collective-permute-done.low_ref
  50.3 0.0 collective-permute-done.1.up_ref
  50.3 1.1 %slots.1 = bf16[512,256]{1,0:T(8,128)(2,1)} custom-call(bf16[256,512]{1,0:T(8,128)(2,1)S(1)} %get-tuple-element.30.own_ref, bf16[256,256]{1,0:T(8,128)(2,1)S(1)} %collective-permute-done.low_ref, bf16[256,256]{1,0:T(8,128)(2,1)S(1)} %collective-permute-done.1.up_ref, s32[1,512]{1,0:T(1,128)S(1)} %reshape.28.src_ref, s32[1,512]{1,0:T(1,128)S(1)} %reshape.29.dst_ref), custom_call_target="tpu_custom_call" | custom-call | flops 134217728 | bytes 524288 | tf_op jit(solution)/shard_map/slots/pallas_call | solution.py:248
  51.4 5.4 %all-to-all-start.1 = ((bf16[32,16,256]{2,1,0:T(8,128)(2,1)}), bf16[32,16,256]{2,1,0:T(8,128)(2,1)S(1)}, u32[]{:S(2)}, u32[]{:S(2)}) async-start(bf16[32,16,256]{2,1,0:T(8,128)(2,1)} %bitcast.5), calls=%async_computation.1 | async-start | bytes 524288 | tf_op jit(solution)/shard_map/all_to_all | solution.py:483
  56.7 8.2 %embed.3 = (bf16[4096,512]{1,0:T(8,128)(2,1)}, f32[320,512]{1,0:T(8,128)S(1)}) custom-call(bf16[256,256]{1,0:T(8,128)(2,1)S(1)} %collective-permute-done.low_ref, bf16[256,256]{1,0:T(8,128)(2,1)S(1)} %collective-permute-done.1.up_ref, f32[320,512]{1,0:T(8,128)S(1)} %get-tuple-element.27.before, ...), custom_call_target="tpu_custom_call", output_to_operand_aliasing={{0}: (10, {})} | custom-call | flops 5033164800 | bytes 4718592 | tf_op jit(solution)/shard_map/embed/pallas_call | solution.py:354
  65.0 0.7 %all-to-all-done.1 = bf16[32,16,256]{2,1,0:T(8,128)(2,1)S(1)} async-done(((bf16[32,16,256]{2,1,0:T(8,128)(2,1)}), bf16[32,16,256]{2,1,0:T(8,128)(2,1)S(1)}, u32[]{:S(2)}, u32[]{:S(2)}) %all-to-all-start.1) | async-done | bytes 262176 | tf_op jit(solution)/shard_map/all_to_all | solution.py:483
  65.7 3.6 %node.1 = bf16[320,512]{1,0:T(8,128)(2,1)} custom-call(bf16[512,256]{1,0:T(8,128)(2,1)S(1)} %bitcast.9, bf16[256,512]{1,0:T(8,128)(2,1)S(1)} %get-tuple-element.21.w_in, f32[1,512]{1,0:T(1,128)S(1)} %get-tuple-element.22.b_in, bf16[512,512]{1,0:T(8,128)(2,1)S(1)} %get-tuple-element.23.w_out, bf16[512,512]{1,0:T(8,128)(2,1)S(1)} %get-tuple-element.24.w_msg, ...), custom_call_target="tpu_custom_call" | custom-call | flops 805306368 | bytes 3145728 | tf_op jit(solution)/shard_map/node/pallas_call | solution.py:403
  (1 shorter events, 0.0 us)
Async XLA Ops:
  4.6 8.9 %copy-start.9 = (s32[1,2,256]{2,1,0:T(2,128)S(1)}, s32[1,2,256]{2,1,0:T(2,128)}, u32[]{:S(2)}) copy-start(s32[1,2,256]{2,1,0:T(2,128)} %param.24) | copy-start | bytes 6148
  4.6 8.9 %copy-start.7 = (s32[1,32,16]{1,2,0:T(8,128)S(1)}, s32[1,32,16]{1,2,0:T(8,128)}, u32[]{:S(2)}) copy-start(s32[1,32,16]{1,2,0:T(8,128)} %param.27) | copy-start | bytes 6148
  4.6 9.1 %copy-start.8 = (s32[1,32,16]{1,2,0:T(8,128)S(1)}, s32[1,32,16]{1,2,0:T(8,128)}, u32[]{:S(2)}) copy-start(s32[1,32,16]{1,2,0:T(8,128)} %param.28) | copy-start | bytes 6148
  4.6 9.2 %copy-start = (bf16[320,512]{1,0:T(8,128)(2,1)S(1)}, bf16[320,512]{1,0:T(8,128)(2,1)}, u32[]{:S(2)}) copy-start(bf16[320,512]{1,0:T(8,128)(2,1)} %rest_4_.1) | copy-start | bytes 983044
  4.6 9.2 %copy-start.1 = (bf16[224,512]{1,0:T(8,128)(2,1)S(1)}, bf16[224,512]{1,0:T(8,128)(2,1)}, u32[]{:S(2)}) copy-start(bf16[224,512]{1,0:T(8,128)(2,1)} %w_ref.1) | copy-start | bytes 688132
  4.6 9.2 %copy-start.2 = (s32[1,4096]{1,0:T(1,128)S(1)}, s32[1,4096]{1,0:T(1,128)}, u32[]{:S(2)}) copy-start(s32[1,4096]{1,0:T(1,128)} %src_ref.1) | copy-start | bytes 49156
  4.6 9.2 %copy-start.3 = (s32[1,4096]{1,0:T(1,128)S(1)}, s32[1,4096]{1,0:T(1,128)}, u32[]{:S(2)}) copy-start(s32[1,4096]{1,0:T(1,128)} %dst_ref.1) | copy-start | bytes 49156
  4.6 9.2 %copy-start.4 = (f32[512]{0:T(512)S(1)}, f32[512]{0:T(512)}, u32[]{:S(2)}) copy-start(f32[512]{0:T(512)} %param.22) | copy-start | bytes 6148
  4.7 9.2 %copy-start.5 = (f32[512]{0:T(512)S(1)}, f32[512]{0:T(512)}, u32[]{:S(2)}) copy-start(f32[512]{0:T(512)} %param.34) | copy-start | bytes 6148
  4.7 9.2 %copy-start.6 = (f32[512]{0:T(512)S(1)}, f32[512]{0:T(512)}, u32[]{:S(2)}) copy-start(f32[512]{0:T(512)} %param.30) | copy-start | bytes 6148
  4.7 34.5 %all-to-all-start = ((bf16[32,8,3584]{2,1,0:T(8,128)(2,1)}), bf16[32,8,3584]{2,1,0:T(8,128)(2,1)}, u32[]{:S(2)}, u32[]{:S(2)}) async-start(bf16[32,8,3584]{2,1,0:T(8,128)(2,1)} %pack.1), calls=%async_computation | async-start | bytes 3670016 | tf_op jit(solution)/shard_map/all_to_all | solution.py:447
  42.2 8.0 %collective-permute-start = (bf16[256,256]{1,0:T(8,128)(2,1)S(1)}, bf16[256,256]{1,0:T(8,128)(2,1)S(1)}, u32[]{:S(2)}, u32[]{:S(2)}) collective-permute-start(bf16[256,256]{1,0:T(8,128)(2,1)S(1)} %get-tuple-element.18), channel_id=1, source_target_pairs={{0,32},{32,64},{64,96},{96,0},{1,33},{33,65},{65,97},{97,1},{2,34}... | collective-permute-start | bytes 393224 | tf_op jit(solution)/shard_map/ppermute | solution.py:473
  43.9 6.3 %collective-permute-start.1 = (bf16[256,256]{1,0:T(8,128)(2,1)S(1)}, bf16[256,256]{1,0:T(8,128)(2,1)S(1)}, u32[]{:S(2)}, u32[]{:S(2)}) collective-permute-start(bf16[256,256]{1,0:T(8,128)(2,1)S(1)} %get-tuple-element.19), channel_id=1, source_target_pairs={{32,0},{64,32},{96,64},{0,96},{33,1},{65,33},{97,65},{1,97},{34,2}... | collective-permute-start | bytes 393224 | tf_op jit(solution)/shard_map/ppermute | solution.py:474
  51.4 14.4 %all-to-all-start.1 = ((bf16[32,16,256]{2,1,0:T(8,128)(2,1)}), bf16[32,16,256]{2,1,0:T(8,128)(2,1)S(1)}, u32[]{:S(2)}, u32[]{:S(2)}) async-start(bf16[32,16,256]{2,1,0:T(8,128)(2,1)} %bitcast.5), calls=%async_computation.1 | async-start | bytes 524288 | tf_op jit(solution)/shard_map/all_to_all | solution.py:483

commit v6 on v5

--- a/solution.py
+++ b/solution.py
@@ -11,7 +11,7 @@
 F32 = jnp.float32
 NT = (((1,), (1,)), ((), ()))
 TN = (((0,), (0,)), ((), ()))
-CUT = 1
+PIECE = 512
 MIB = 1024 * 1024
 
 
@@ -111,7 +111,7 @@
 
 def count_kernel(
     src_ref, dst_ref, w_ref, b_ref, mesh_ref, b_n, b_m, w_node, w_out, w_msg,
-    o_ref, w_in_ref, pre_ref, out_ref, msg_ref, bi_ref, bm_ref, nb_ref, hot_ref, na_ref, sem, *, chans,
+    o_ref, w_in_ref, pre_ref, msg_ref, both_ref, bi_ref, bm_ref, nb_ref, hot_ref, na_ref, out_ref, sem, *, chans,
 ):
     nodes, edges = hot_ref.shape
     lat = w_out.shape[0]
@@ -150,6 +150,7 @@
     for c in copies:
         c.wait()
     msg_ref[...] = msg_ref[...] * 0.5
+    both_ref[...] = dot(out_ref[...], msg_ref[...]).astype(BF)
     nb_ref[...] = nb_ref[...] * 0.5
     pre_ref[...] = 0.5 * (dot(mesh_ref[...], na_ref[...]) + b_n[...])
 
@@ -166,7 +167,7 @@
             pltpu.HBM((nodes, table), BF),
             pltpu.VMEM((wide, lat), BF),
             pltpu.HBM((nodes, lat), F32),
-            square,
+            pltpu.HBM((lat, lat), BF),
             square,
             pltpu.VMEM((1, lat), F32),
             pltpu.VMEM((1, lat), F32),
@@ -175,6 +176,7 @@
         scratch_shapes=[
             pltpu.VMEM((nodes, edges), BF),
             pltpu.VMEM((lat, lat), BF),
+            pltpu.VMEM((lat, lat), BF),
             pltpu.SemaphoreType.DMA((4,)),
         ],
         compiler_params=params(24),
@@ -190,23 +192,20 @@
         ref[pl.ds(start, step)] = hot(ids, (index - start).astype(jnp.int16))
 
 
-def select_kernel(x_ref, idx_ref, low_ref, high_ref, keep_ref, near_hot, sem, *, chans):
+def select_kernel(x_ref, idx_ref, low_ref, high_ref, tail_ref, near_hot, *, chans):
     rows, main = x_ref.shape
     half = low_ref.shape[1]
     last = main // chans
     group = chans + 1
-    load = pltpu.make_async_copy(x_ref, keep_ref.at[:, pl.ds(0, main)], sem)
-    load.start()
     hots(idx_ref[...], near_hot)
-    load.wait()
-    near = dot(keep_ref[:, :main], near_hot[:main])
+    near = dot(x_ref[...], near_hot[:main])
     row = lax.broadcasted_iota(jnp.int32, (1, group, 1), 1)
     tail = jnp.zeros((rows // group, group, last), F32)
     for c in range(chans):
-        part = keep_ref[:, c * last : (c + 1) * last].astype(F32).reshape(rows // group, group, last)
+        part = x_ref[:, c * last : (c + 1) * last].astype(F32).reshape(rows // group, group, last)
         tail = jnp.where(row == c, part[:, chans:], tail)
     tail = tail.reshape(rows, last).astype(BF)
-    keep_ref[:, main:] = tail
+    tail_ref[...] = tail
     near = near + dot(tail, near_hot[main:])
     low_ref[...] = near[:, :half].astype(BF)
     high_ref[...] = near[:, half:].astype(BF)
@@ -214,19 +213,20 @@
 
 def select(x, idx, chans):
     rows, main = x.shape
-    pts = main // chans * (chans + 1)
+    last = main // chans
+    pts = main + last
     half = idx.shape[1] // 2
     out = jax.ShapeDtypeStruct((rows, half), BF)
     return pl.pallas_call(
         functools.partial(select_kernel, chans=chans),
-        in_specs=[ANY, VM],
+        in_specs=[VM, VM],
         out_specs=[VM] * 3,
-        out_shape=(out, out, pltpu.VMEM((rows, pts), BF)),
-        scratch_shapes=[pltpu.VMEM((pts, 2 * half), BF), pltpu.SemaphoreType.DMA],
+        out_shape=(out, out, pltpu.VMEM((rows, last), BF)),
+        scratch_shapes=[pltpu.VMEM((pts, 2 * half), BF)],
         compiler_params=params(24),
         cost_estimate=cost(4 * rows * pts * half, rows * pts * 2),
         name="select",
-    )(at_hbm(x), idx)
+    )(*at_vmem(x), idx)
 
 
 def slots_kernel(own_ref, low_ref, up_ref, src_ref, dst_ref, o_ref, *, start, pad):
@@ -261,6 +261,11 @@
     return latent, silu2(dot(latent, w_msg[...]) + b_msg[...])
 
 
+def act_only(x, dims, w_in, b_in, w_both, b_msg):
+    hidden = silu2(dot(x, w_in[...], dims) + b_in[...])
+    return silu2(dot(hidden, w_both[...]) + b_msg[...])
+
+
 def columns(src, dst, sem, spans):
     copies = []
     at = 0
@@ -275,30 +280,44 @@
     return copies
 
 
-def embed_tiles(x_ref, weights, lat_hbm, act_ref, buf, sem, starts, tile):
+def embed_tile(x, weights, lat_hbm, act_ref, buf, sem, row, pieces):
+    latent, act = act_of(x, TN, *weights)
+    rows = pl.ds(row, x.shape[1])
+    buf[rows] = latent
+    act_ref[rows] = act
     stores = []
-    for i, (col, point) in enumerate(starts):
-        rows = pl.ds(i * tile, tile)
-        latent, act = act_of(x_ref[:, col : col + tile], TN, *weights)
-        buf[rows] = latent
+    for point, width in pieces:
         stores.append(
-            pltpu.make_async_copy(buf.at[rows], lat_hbm.at[pl.ds(point, tile)], sem.at[i])
+            pltpu.make_async_copy(
+                buf.at[pl.ds(row, width)], lat_hbm.at[pl.ds(point, width)], sem.at[row // PIECE]
+            )
         )
         stores[-1].start()
-        act_ref[rows] = act
+        row += width
     return stores
 
 
+def whole_copies(pairs, sem):
+    copies = [pltpu.make_async_copy(f, t, sem.at[k]) for k, (f, t) in enumerate(pairs)]
+    for c in copies:
+        c.start()
+    return copies
+
+
 def first_kernel(
-    x_ref, src_ref, w_in, b_in, w_out, w_msg, b_msg, s_hbm, lat_ref, sum_ref, own_ref,
-    s_buf, act_buf, buf, far_hot, sem, in_sem, *, spans, tile,
+    x_ref, tail_ref, src_ref, w_in, b_in, b_msg, w_out_hbm, w_msg_hbm, s_hbm, lat_ref, sum_ref, own_ref,
+    s_buf, act_buf, buf, w_out, w_msg, far_hot, sem, in_sem, w_sem, *, spans,
 ):
+    w_loads = whole_copies(((w_out_hbm, w_out), (w_msg_hbm, w_msg)), w_sem)
     loads = columns(s_hbm, s_buf, in_sem, spans)
-    weights = (w_in, b_in, w_out, w_msg, b_msg)
-    starts = [(p, p) for start, width in spans for p in range(start, start + width, tile)]
     hots(src_ref[...], far_hot)
-    stores = embed_tiles(x_ref, weights, lat_ref, act_buf, buf, sem, starts, tile)
-    own_ref[...] = dot(x_ref[...], far_hot[...]).astype(BF)
+    main = x_ref.shape[1]
+    far = dot(x_ref[...], far_hot[:main]) + dot(tail_ref[...], far_hot[main:])
+    own_ref[...] = far.astype(BF)
+    x = jnp.concatenate([x_ref[:, : spans[0][1]], tail_ref[...]], axis=1)
+    for c in w_loads:
+        c.wait()
+    stores = embed_tile(x, (w_in, b_in, w_out, w_msg, b_msg), lat_ref, act_buf, buf, sem, 0, spans)
     for c in loads:
         c.wait()
     sum_ref[...] = dot(s_buf[...], act_buf[...])
@@ -307,52 +326,61 @@
 
 
 def second_kernel(
-    low_ref, up_ref, before, w_in, b_in, w_out, w_msg, b_msg, s_hbm, x_hbm, _, lat_ref, sum_ref,
-    s_buf, act_buf, buf, x_buf, sem, in_sem, x_sem, *, spans, tile,
+    low_ref, up_ref, w_both, w_in, b_in, b_msg, w_out_hbm, w_msg_hbm, s_hbm, before, x_hbm, _, lat_ref, sum_ref,
+    s_buf, act_buf, buf, w_out, w_msg, x_buf, sem, in_sem, w_sem, x_sem, *, spans, tile,
 ):
-    weights = (w_in, b_in, w_out, w_msg, b_msg)
     half = low_ref.shape[1]
     x_load = columns(x_hbm, x_buf, x_sem, spans[:1])
+    w_loads = whole_copies(((w_out_hbm, w_out), (w_msg_hbm, w_msg), (before, sum_ref)), w_sem)
     loads = columns(s_hbm, s_buf, in_sem, spans)
     start, width = spans[0]
-    for k, ref in enumerate((low_ref, up_ref)):
-        act_buf[pl.ds(width + k * half, half)] = act_of(ref[...], TN, *weights)[1]
+    halo = jnp.concatenate([low_ref[...], up_ref[...]], axis=1)
+    act_buf[pl.ds(width, 2 * half)] = act_only(halo, TN, w_in, b_in, w_both, b_msg)
     x_load[0].wait()
-    starts = [(p, start + p) for p in range(0, width, tile)]
-    stores = embed_tiles(x_buf, weights, lat_ref, act_buf, buf, sem, starts, tile)
+    for c in w_loads:
+        c.wait()
+    weights = (w_in, b_in, w_out, w_msg, b_msg)
+    stores = []
+    for p in range(0, width, tile):
+        stores += embed_tile(
+            x_buf[:, p : p + tile], weights, lat_ref, act_buf, buf, sem, p, [(start + p, tile)]
+        )
     for c in loads:
         c.wait()
-    sum_ref[...] = before[...] + dot(s_buf[...], act_buf[...])
+    sum_ref[...] += dot(s_buf[...], act_buf[...])
     for c in stores:
         c.wait()
 
 
-def embed(x, counts, weights, pts, spans, tile, src=None, before=None):
+def embed(x, counts, weights, later, pts, spans, tile, tail=None, src=None, before=None):
     rows = x.shape[0]
     nodes = counts.shape[0]
-    lat = weights[0].shape[1]
+    w_in, b_in, w_both, b_msg = weights
+    lat = w_in.shape[1]
     wide = sum(width for _, width in spans)
+    held = at_vmem(w_in, b_in, b_msg)
+    remote = [at_hbm(a) for a in (*later, counts)]
     if before is None:
-        kernel = first_kernel
+        kernel = functools.partial(first_kernel, spans=spans)
         span = wide
-        args = [*at_vmem(x), src, *at_vmem(*weights), at_hbm(counts)]
-        specs = [VM] * 7 + [ANY]
+        args = [*at_vmem(x, tail), src, *held, *remote]
+        specs = [VM] * 6 + [ANY] * 3
         alias = {}
         inner = [pltpu.VMEM((pts, src.shape[1]), BF)]
-        tail = []
+        sems = []
         more = [pltpu.VMEM((rows, src.shape[1]), BF)]
     else:
-        kernel = second_kernel
+        kernel = functools.partial(second_kernel, spans=spans, tile=tile)
         span = spans[0][1]
         latent, total, low, up = before
-        args = [*at_vmem(low, up, total, *weights), at_hbm(counts), at_hbm(x), at_hbm(latent)]
-        specs = [VM] * 8 + [ANY] * 3
-        alias = {10: 0}
+        args = [*at_vmem(low, up, w_both), *held, *remote, at_hbm(total), at_hbm(x), at_hbm(latent)]
+        specs = [VM] * 6 + [ANY] * 6
+        alias = {11: 0}
         inner = [pltpu.VMEM((rows, span), BF)]
-        tail = [pltpu.SemaphoreType.DMA((1,))]
+        sems = [pltpu.SemaphoreType.DMA((1,))]
         more = []
     return pl.pallas_call(
-        functools.partial(kernel, spans=spans, tile=tile),
+        kernel,
         in_specs=specs,
         out_specs=[ANY, VM] + [VM] * len(more),
         out_shape=(pltpu.HBM((pts, lat), BF), pltpu.VMEM((nodes, lat), F32), *more),
@@ -360,19 +388,22 @@
             pltpu.VMEM((nodes, wide), BF),
             pltpu.VMEM((wide, lat), BF),
             pltpu.VMEM((span, lat), BF),
+            pltpu.VMEM((lat, lat), BF),
+            pltpu.VMEM((lat, lat), BF),
             *inner,
-            pltpu.SemaphoreType.DMA((span // tile,)),
+            pltpu.SemaphoreType.DMA((span // PIECE,)),
             pltpu.SemaphoreType.DMA((len(spans),)),
-            *tail,
+            pltpu.SemaphoreType.DMA((3,)),
+            *sems,
         ],
         input_output_aliases=alias,
-        compiler_params=params(24),
+        compiler_params=params(28),
         cost_estimate=cost(2 * span * lat * (rows + 2 * lat + nodes), span * (rows + lat) * 2),
         name="embed",
     )(*args)
 
 
-def node_kernel(r_ref, w_in, b_in, w_out, w_msg, b_msg, sum_ref, *rest, pad):
+def node_kernel(r_ref, w_in, b_in, w_both, b_msg, sum_ref, *rest, pad):
     sources, o_ref, buffers, sem = rest[:5], rest[5], rest[6:11], rest[11]
     loads = [pltpu.make_async_copy(f, t, sem.at[k]) for k, (f, t) in enumerate(zip(sources, buffers))]
     for c in loads:
@@ -380,17 +411,15 @@
     w_mo, w_nb, pre_ref, w_no, mesh_ref = buffers
     nodes = sum_ref.shape[0]
     rows = r_ref[...]
-    _, act = act_of(rows, (((1,), (0,)), ((), ())), w_in, b_in, w_out, w_msg, b_msg)
+    act = act_only(rows, (((1,), (0,)), ((), ())), w_in, b_in, w_both, b_msg)
     lane = lax.broadcasted_iota(jnp.int32, (8, rows.shape[1]), 1)
     pick = jnp.where(lane == pad, 16.0, jnp.where(lane == 2 * pad + 1, 1.0, 0.0)).astype(BF)
     dst = dot(pick, rows, NT)[:1].astype(jnp.int32) - 1
     ids = lax.broadcasted_iota(jnp.int32, (nodes, rows.shape[0]), 0)
     total = sum_ref[...] + dot(hot(ids, dst), act)
-    high = total.astype(BF)
-    low = (total - high.astype(F32)).astype(BF)
     for c in loads:
         c.wait()
-    summed = (dot(high, w_mo[...]) + dot(low, w_mo[...])).astype(BF)
+    summed = dot(total.astype(BF), w_mo[...]).astype(BF)
     node = silu2(pre_ref[...] + dot(summed, w_nb[...]))
     o_ref[...] = (mesh_ref[...].astype(F32) + dot(node, w_no[...])).astype(BF)
 
@@ -448,7 +477,7 @@
     main = pts // (chans + 1) * chans
     x = got.reshape(wide, main)
 
-    counts, w_in, pre, w_out, w_msg, b_in, b_out, w_nb = count_edges(
+    counts, w_in, pre, w_msg, w_both, b_in, b_out, w_nb = count_edges(
         local_src,
         local_dst,
         w_embed_in,
@@ -463,20 +492,21 @@
         wide,
         chans,
     )
-    weights = [w_in, b_in, w_out, w_msg, b_out]
+    weights = [w_in, b_in, w_both, b_out]
+    later = [w_embed_out, w_msg]
 
     src = remote_src.reshape(1, -1)
     dst = remote_dst.reshape(1, -1)
-    low, high, kept = select(x, halo_index.reshape(1, 2 * halo), chans)
+    low, high, tail = select(x, halo_index.reshape(1, 2 * halo), chans)
     ahead = [(i, (i + 1) % tiles) for i in range(tiles)]
     back = [(t, s) for s, t in ahead]
     from_low = lax.ppermute(high, "tile", ahead)
     from_up = lax.ppermute(low, "tile", back)
 
-    tile = 512
-    cut = CUT * tile
+    tile = 2 * PIECE
+    cut = PIECE
     latent, total, own = embed(
-        kept, counts, weights, pts, ((0, cut), (main, pts - main)), tile, src
+        x, counts, weights, later, pts, ((0, cut), (main, pts - main)), tile, tail, src
     )
 
     rows = slots_rows(own, from_low, from_up, src, dst, pts, chans)
@@ -488,6 +518,7 @@
         x,
         counts,
         weights,
+        later,
         pts,
         ((cut, main - cut), (pts, 2 * halo)),
         tile,

time: 69.9 us -> 67.4 us (0.964)
  Pallas kernels: 40.6 us -> 38 us
    pallas_call x3, Pallas kernels: 15.3 us -> 12.8 us  [the longest x2 11.3 us: embed(): pl.pallas_call(kernel, in_specs=specs, out_specs=[ANY, VM] + [VM] * len(m...]
where the time goes in v6:
time: 67.4 us; the launch traced here: 67 us
  Pallas kernels  38 us (56%)
  starting transfers between devices  17.7 us (26%)
  waiting for transfers between devices  9.81 us (15%)
  between operations  1.05 us (2%)
    pallas_call x1, Pallas kernels, count_edges(): pl.pallas_call(functools.partial(count_kernel, chans=chans), in_specs=[VM...  16.7 us
    pallas_call x2, Pallas kernels, embed(): pl.pallas_call(kernel, in_specs=specs, out_specs=[ANY, VM] + [VM] * len(m...  11.3 us
    all_to_all x1, waiting for transfers between devices, shards(): got = lax.all_to_all(sent, 'lev', split_axis=0, concat_axis=0, tiled=True)  8.69 us
    all_to_all x1, starting transfers between devices, shards(): got = lax.all_to_all(sent, 'lev', split_axis=0, concat_axis=0, tiled=True)  8.59 us
    all_to_all x1, starting transfers between devices, shards(): lax.all_to_all(rows.reshape(levels, slot_count, wide), 'lev', split_axis=...  5.25 us
    pallas_call x1, Pallas kernels, pack(): pl.pallas_call(functools.partial(pack_kernel, parts=parts), in_specs=[sme...  4.05 us
    pallas_call x1, Pallas kernels, node_update(): pl.pallas_call(functools.partial(node_kernel, pad=pad), in_specs=[VM] * l...  3.37 us
    ppermute x1, starting transfers between devices, shards(): from_up = lax.ppermute(low, 'tile', back)  2.2 us
  transfers between devices with their start and end apart: 4, of which 2 were waited for; matrix products, arithmetic and copies ran while one was open for 0% of the time, Pallas kernels for 42%

profile of v6, /device:TPU:1, one launch (start us, length us, event | category | flops | bytes accessed | tf_op | source)
XLA Modules:
  0.0 67.0 jit_solution(10320396844933039080)
XLA Ops:
  0.6 0.0 copy-start.11
  0.6 0.0 copy-start.9
  0.7 0.0 copy-start.10
  0.7 0.0 copy-start.1
  0.7 0.0 copy-start.3
  0.7 0.0 copy-start.4
  0.7 0.0 copy-start.5
  0.7 0.0 copy-start.6
  0.7 0.0 copy-start.7
  0.7 0.0 copy-start.8
  0.7 4.1 %pack.1 = bf16[32,8,3584]{2,1,0:T(8,128)(2,1)} custom-call(s32[1]{0:T(128)} %bitcast.me_ref, f32[224]{0:T(256)} %mean_ref.1, f32[224]{0:T(256)} %scale_ref.1, f32[7,131072]{1,0:T(8,128)} %x_ref.1), custom_call_target="tpu_custom_call" | custom-call | flops 2097152 | bytes 6291456 | tf_op jit(solution)/shard_map/pack/pallas_call | solution.py:95
  4.8 8.6 %all-to-all-start = ((bf16[32,8,3584]{2,1,0:T(8,128)(2,1)}), bf16[32,8,3584]{2,1,0:T(8,128)(2,1)S(1)}, u32[]{:S(2)}, u32[]{:S(2)}) async-start(bf16[32,8,3584]{2,1,0:T(8,128)(2,1)} %pack.1), calls=%async_computation | async-start | bytes 3670016 | tf_op jit(solution)/shard_map/all_to_all | solution.py:476
  13.4 0.0 copy-done.11
  13.4 0.0 copy-done.9
  13.4 0.1 copy.23
  13.5 0.1 reshape.28.src_ref
  13.6 0.0 copy-done.10
  13.6 0.1 copy.24
  13.7 0.1 reshape.29.dst_ref
  13.7 0.0 copy-done.1
  13.8 0.0 copy-done.3
  13.8 0.0 copy-done.4
  13.8 0.0 copy-done.5
  13.8 0.0 copy-done.6
  13.8 0.0 copy-done.7
  13.8 0.0 copy-done.8
  13.8 16.7 %count.1 = (bf16[320,4608]{1,0:T(8,128)(2,1)}, bf16[256,512]{1,0:T(8,128)(2,1)S(1)}, f32[320,512]{1,0:T(8,128)}, bf16[512,512]{1,0:T(8,128)(2,1)}, bf16[512,512]...) custom-call(s32[1,4096]{1,0:T(1,128)S(1)} %copy-done.4, ...), custom_call_target="tpu_custom_call" | custom-call | flops 12079595520 | bytes 2949120 | tf_op jit(solution)/shard_map/count/pallas_call | solution.py:162
  30.5 8.7 %all-to-all-done = bf16[32,8,3584]{2,1,0:T(8,128)(2,1)S(1)} async-done(((bf16[32,8,3584]{2,1,0:T(8,128)(2,1)}), bf16[32,8,3584]{2,1,0:T(8,128)(2,1)S(1)}, u32[]{:S(2)}, u32[]{:S(2)}) %all-to-all-start) | async-done | bytes 1835040 | tf_op jit(solution)/shard_map/all_to_all | solution.py:476
  39.2 0.0 copy-start
  39.2 1.5 %select.1 = (bf16[256,256]{1,0:T(8,128)(2,1)S(1)}, bf16[256,256]{1,0:T(8,128)(2,1)S(1)}, bf16[256,512]{1,0:T(8,128)(2,1)S(1)}) custom-call(bf16[256,3584]{1,0:T(8,128)(2,1)S(1)} %bitcast.9, s32[1,512]{1,0:T(1,128)S(1)} %bitcast.13), custom_call_target="tpu_custom_call" | custom-call | flops 1073741824 | bytes 2097152 | tf_op jit(solution)/shard_map/select/pallas_call | solution.py:220
  40.7 1.7 %collective-permute-start = (bf16[256,256]{1,0:T(8,128)(2,1)S(1)}, bf16[256,256]{1,0:T(8,128)(2,1)S(1)}, u32[]{:S(2)}, u32[]{:S(2)}) collective-permute-start(bf16[256,256]{1,0:T(8,128)(2,1)S(1)} %get-tuple-element.18), channel_id=1, source_target_pairs={{0,32},{32,64},{64,96},{96,0},{1,33},{33,65},{65,97},{97,1},{2,34}... | collective-permute-start | bytes 393224 | tf_op jit(solution)/shard_map/ppermute | solution.py:503
  42.4 2.2 %collective-permute-start.1 = (bf16[256,256]{1,0:T(8,128)(2,1)S(1)}, bf16[256,256]{1,0:T(8,128)(2,1)S(1)}, u32[]{:S(2)}, u32[]{:S(2)}) collective-permute-start(bf16[256,256]{1,0:T(8,128)(2,1)S(1)} %get-tuple-element.19), channel_id=1, source_target_pairs={{32,0},{64,32},{96,64},{0,96},{33,1},{65,33},{97,65},{1,97},{34,2}... | collective-permute-start | bytes 393224 | tf_op jit(solution)/shard_map/ppermute | solution.py:504
  44.6 3.5 %embed.2 = (bf16[4096,512]{1,0:T(8,128)(2,1)}, f32[320,512]{1,0:T(8,128)S(1)}, bf16[256,512]{1,0:T(8,128)(2,1)S(1)}) custom-call(bf16[256,3584]{1,0:T(8,128)(2,1)S(1)} %bitcast.10, bf16[256,512]{1,0:T(8,128)(2,1)S(1)} %get-tuple-element.26.tail_ref, s32[1,512]{1,0:T(1,128)S(1)} %reshape.28.src_ref, bf16[256,512]{1,0:T(8,128)(2,1)S(1)} %get-tuple-element.21.w_in, ...), custom_call_target="tpu_custom_call" | custom-call | flops 1677721600 | bytes 1572864 | tf_op jit(solution)/shard_map/embed/pallas_call | solution.py:382
  48.1 0.0 copy-done
  48.1 0.0 copy-start.2
  48.1 0.0 collective-permute-done.low_ref
  48.1 0.0 collective-permute-done.1.up_ref
  48.2 1.1 %slots.1 = bf16[512,256]{1,0:T(8,128)(2,1)} custom-call(bf16[256,512]{1,0:T(8,128)(2,1)S(1)} %get-tuple-element.30.own_ref, bf16[256,256]{1,0:T(8,128)(2,1)S(1)} %collective-permute-done.low_ref, bf16[256,256]{1,0:T(8,128)(2,1)S(1)} %collective-permute-done.1.up_ref, s32[1,512]{1,0:T(1,128)S(1)} %reshape.28.src_ref, s32[1,512]{1,0:T(1,128)S(1)} %reshape.29.dst_ref), custom_call_target="tpu_custom_call" | custom-call | flops 134217728 | bytes 524288 | tf_op jit(solution)/shard_map/slots/pallas_call | solution.py:248
  49.2 0.0 copy-done.2
  49.2 5.3 %all-to-all-start.1 = ((bf16[32,16,256]{2,1,0:T(8,128)(2,1)}), bf16[32,16,256]{2,1,0:T(8,128)(2,1)S(1)}, u32[]{:S(2)}, u32[]{:S(2)}) async-start(bf16[32,16,256]{2,1,0:T(8,128)(2,1)} %bitcast.5), calls=%async_computation.1 | async-start | bytes 524288 | tf_op jit(solution)/shard_map/all_to_all | solution.py:513
  54.5 7.8 %embed.3 = (bf16[4096,512]{1,0:T(8,128)(2,1)}, f32[320,512]{1,0:T(8,128)S(1)}) custom-call(bf16[256,256]{1,0:T(8,128)(2,1)S(1)} %collective-permute-done.low_ref, bf16[256,256]{1,0:T(8,128)(2,1)S(1)} %collective-permute-done.1.up_ref, bf16[512,512]{1,0:T(8,128)(2,1)S(1)} %get-tuple-element.20.w_both, ...), custom_call_target="tpu_custom_call", output_to_operand_aliasing={{0}: (11, {})} | custom-call | flops 5033164800 | bytes 4718592 | tf_op jit(solution)/shard_map/embed/pallas_call | solution.py:382
  62.4 1.1 %all-to-all-done.1 = bf16[32,16,256]{2,1,0:T(8,128)(2,1)S(1)} async-done(((bf16[32,16,256]{2,1,0:T(8,128)(2,1)}), bf16[32,16,256]{2,1,0:T(8,128)(2,1)S(1)}, u32[]{:S(2)}, u32[]{:S(2)}) %all-to-all-start.1) | async-done | bytes 262176 | tf_op jit(solution)/shard_map/all_to_all | solution.py:513
  63.5 3.4 %node.1 = bf16[320,512]{1,0:T(8,128)(2,1)} custom-call(bf16[512,256]{1,0:T(8,128)(2,1)S(1)} %bitcast.12, bf16[256,512]{1,0:T(8,128)(2,1)S(1)} %get-tuple-element.21.w_in, f32[1,512]{1,0:T(1,128)S(1)} %get-tuple-element.22.b_in, bf16[512,512]{1,0:T(8,128)(2,1)S(1)} %get-tuple-element.20.w_both, f32[1,512]{1,0:T(1,128)S(1)} %get-tuple-element.23.b_msg, ...), custom_call_target="tpu_custom_call" | custom-call | flops 805306368 | bytes 3145728 | tf_op jit(solution)/shard_map/node/pallas_call | solution.py:432
  (1 shorter events, 0.0 us)
Async XLA Ops:
  0.6 12.8 %copy-start.11 = (s32[1,2,256]{2,1,0:T(2,128)S(1)}, s32[1,2,256]{2,1,0:T(2,128)}, u32[]{:S(2)}) copy-start(s32[1,2,256]{2,1,0:T(2,128)} %param.24) | copy-start | bytes 6148
  0.6 12.8 %copy-start.9 = (s32[1,32,16]{1,2,0:T(8,128)S(1)}, s32[1,32,16]{1,2,0:T(8,128)}, u32[]{:S(2)}) copy-start(s32[1,32,16]{1,2,0:T(8,128)} %param.27) | copy-start | bytes 6148
  0.7 12.9 %copy-start.10 = (s32[1,32,16]{1,2,0:T(8,128)S(1)}, s32[1,32,16]{1,2,0:T(8,128)}, u32[]{:S(2)}) copy-start(s32[1,32,16]{1,2,0:T(8,128)} %param.28) | copy-start | bytes 6148
  0.7 13.1 %copy-start.1 = (bf16[320,512]{1,0:T(8,128)(2,1)S(1)}, bf16[320,512]{1,0:T(8,128)(2,1)}, u32[]{:S(2)}) copy-start(bf16[320,512]{1,0:T(8,128)(2,1)} %rest_4_.1) | copy-start | bytes 983044
  0.7 13.1 %copy-start.3 = (bf16[224,512]{1,0:T(8,128)(2,1)S(1)}, bf16[224,512]{1,0:T(8,128)(2,1)}, u32[]{:S(2)}) copy-start(bf16[224,512]{1,0:T(8,128)(2,1)} %w_ref.1) | copy-start | bytes 688132
  0.7 13.1 %copy-start.4 = (s32[1,4096]{1,0:T(1,128)S(1)}, s32[1,4096]{1,0:T(1,128)}, u32[]{:S(2)}) copy-start(s32[1,4096]{1,0:T(1,128)} %src_ref.1) | copy-start | bytes 49156
  0.7 13.1 %copy-start.5 = (s32[1,4096]{1,0:T(1,128)S(1)}, s32[1,4096]{1,0:T(1,128)}, u32[]{:S(2)}) copy-start(s32[1,4096]{1,0:T(1,128)} %dst_ref.1) | copy-start | bytes 49156
  0.7 13.1 %copy-start.6 = (f32[512]{0:T(512)S(1)}, f32[512]{0:T(512)}, u32[]{:S(2)}) copy-start(f32[512]{0:T(512)} %param.22) | copy-start | bytes 6148
  0.7 13.1 %copy-start.7 = (f32[512]{0:T(512)S(1)}, f32[512]{0:T(512)}, u32[]{:S(2)}) copy-start(f32[512]{0:T(512)} %param.34) | copy-start | bytes 6148
  0.7 13.1 %copy-start.8 = (f32[512]{0:T(512)S(1)}, f32[512]{0:T(512)}, u32[]{:S(2)}) copy-start(f32[512]{0:T(512)} %param.30) | copy-start | bytes 6148
  4.8 34.4 %all-to-all-start = ((bf16[32,8,3584]{2,1,0:T(8,128)(2,1)}), bf16[32,8,3584]{2,1,0:T(8,128)(2,1)S(1)}, u32[]{:S(2)}, u32[]{:S(2)}) async-start(bf16[32,8,3584]{2,1,0:T(8,128)(2,1)} %pack.1), calls=%async_computation | async-start | bytes 3670016 | tf_op jit(solution)/shard_map/all_to_all | solution.py:476
  39.2 8.9 %copy-start = (bf16[32,8,3584]{2,1,0:T(8,128)(2,1)}, bf16[32,8,3584]{2,1,0:T(8,128)(2,1)S(1)}, u32[]{:S(2)}) copy-start(bf16[32,8,3584]{2,1,0:T(8,128)(2,1)S(1)} %all-to-all-done) | copy-start | bytes 5505028
  40.7 7.4 %collective-permute-start = (bf16[256,256]{1,0:T(8,128)(2,1)S(1)}, bf16[256,256]{1,0:T(8,128)(2,1)S(1)}, u32[]{:S(2)}, u32[]{:S(2)}) collective-permute-start(bf16[256,256]{1,0:T(8,128)(2,1)S(1)} %get-tuple-element.18), channel_id=1, source_target_pairs={{0,32},{32,64},{64,96},{96,0},{1,33},{33,65},{65,97},{97,1},{2,34}... | collective-permute-start | bytes 393224 | tf_op jit(solution)/shard_map/ppermute | solution.py:503
  42.4 5.7 %collective-permute-start.1 = (bf16[256,256]{1,0:T(8,128)(2,1)S(1)}, bf16[256,256]{1,0:T(8,128)(2,1)S(1)}, u32[]{:S(2)}, u32[]{:S(2)}) collective-permute-start(bf16[256,256]{1,0:T(8,128)(2,1)S(1)} %get-tuple-element.19), channel_id=1, source_target_pairs={{32,0},{64,32},{96,64},{0,96},{33,1},{65,33},{97,65},{1,97},{34,2}... | collective-permute-start | bytes 393224 | tf_op jit(solution)/shard_map/ppermute | solution.py:504
  48.1 1.1 %copy-start.2 = (f32[320,512]{1,0:T(8,128)}, f32[320,512]{1,0:T(8,128)S(1)}, u32[]{:S(2)}) copy-start(f32[320,512]{1,0:T(8,128)S(1)} %get-tuple-element.27.before) | copy-start | bytes 1966084
  49.2 14.2 %all-to-all-start.1 = ((bf16[32,16,256]{2,1,0:T(8,128)(2,1)}), bf16[32,16,256]{2,1,0:T(8,128)(2,1)S(1)}, u32[]{:S(2)}, u32[]{:S(2)}) async-start(bf16[32,16,256]{2,1,0:T(8,128)(2,1)} %bitcast.5), calls=%async_computation.1 | async-start | bytes 524288 | tf_op jit(solution)/shard_map/all_to_all | solution.py:513

commit v7 on v6

--- a/solution.py
+++ b/solution.py
@@ -89,7 +89,7 @@
 def pack(me, mean, scale, fields, levels):
     chans, points = fields.shape
     pts = points // levels
-    parts = 8
+    parts = 16
     smem = pl.BlockSpec(memory_space=pltpu.SMEM)
     shape = (levels, chans + 1, pts * chans // (chans + 1))
     return pl.pallas_call(
@@ -280,21 +280,16 @@
     return copies
 
 
-def embed_tile(x, weights, lat_hbm, act_ref, buf, sem, row, pieces):
+def embed_tile(x, weights, lat_hbm, act_ref, buf, sem, row, point):
     latent, act = act_of(x, TN, *weights)
     rows = pl.ds(row, x.shape[1])
     buf[rows] = latent
     act_ref[rows] = act
-    stores = []
-    for point, width in pieces:
-        stores.append(
-            pltpu.make_async_copy(
-                buf.at[pl.ds(row, width)], lat_hbm.at[pl.ds(point, width)], sem.at[row // PIECE]
-            )
-        )
-        stores[-1].start()
-        row += width
-    return stores
+    store = pltpu.make_async_copy(
+        buf.at[rows], lat_hbm.at[pl.ds(point, x.shape[1])], sem.at[row // PIECE]
+    )
+    store.start()
+    return [store]
 
 
 def whole_copies(pairs, sem):
@@ -314,10 +309,12 @@
     main = x_ref.shape[1]
     far = dot(x_ref[...], far_hot[:main]) + dot(tail_ref[...], far_hot[main:])
     own_ref[...] = far.astype(BF)
-    x = jnp.concatenate([x_ref[:, : spans[0][1]], tail_ref[...]], axis=1)
     for c in w_loads:
         c.wait()
-    stores = embed_tile(x, (w_in, b_in, w_out, w_msg, b_msg), lat_ref, act_buf, buf, sem, 0, spans)
+    weights = (w_in, b_in, w_out, w_msg, b_msg)
+    cut = spans[0][1]
+    stores = embed_tile(x_ref[:, :cut], weights, lat_ref, act_buf, buf, sem, 0, spans[0][0])
+    stores += embed_tile(tail_ref[...], weights, lat_ref, act_buf, buf, sem, cut, spans[1][0])
     for c in loads:
         c.wait()
     sum_ref[...] = dot(s_buf[...], act_buf[...])
@@ -342,9 +339,8 @@
     weights = (w_in, b_in, w_out, w_msg, b_msg)
     stores = []
     for p in range(0, width, tile):
-        stores += embed_tile(
-            x_buf[:, p : p + tile], weights, lat_ref, act_buf, buf, sem, p, [(start + p, tile)]
-        )
+        x = x_buf[:, p : min(p + tile, width)]
+        stores += embed_tile(x, weights, lat_ref, act_buf, buf, sem, p, start + p)
     for c in loads:
         c.wait()
     sum_ref[...] += dot(s_buf[...], act_buf[...])
@@ -417,10 +413,15 @@
     dst = dot(pick, rows, NT)[:1].astype(jnp.int32) - 1
     ids = lax.broadcasted_iota(jnp.int32, (nodes, rows.shape[0]), 0)
     total = sum_ref[...] + dot(hot(ids, dst), act)
-    for c in loads:
-        c.wait()
-    summed = dot(total.astype(BF), w_mo[...]).astype(BF)
+    high = total.astype(BF)
+    low = (total - high.astype(F32)).astype(BF)
+    loads[0].wait()
+    summed = (dot(high, w_mo[...]) + dot(low, w_mo[...])).astype(BF)
+    loads[1].wait()
+    loads[2].wait()
     node = silu2(pre_ref[...] + dot(summed, w_nb[...]))
+    loads[3].wait()
+    loads[4].wait()
     o_ref[...] = (mesh_ref[...].astype(F32) + dot(node, w_no[...])).astype(BF)
 
 
@@ -504,7 +505,7 @@
     from_up = lax.ppermute(low, "tile", back)
 
     tile = 2 * PIECE
-    cut = PIECE
+    cut = tile
     latent, total, own = embed(
         x, counts, weights, later, pts, ((0, cut), (main, pts - main)), tile, tail, src
     )

time: 67.4 us -> 68.6 us (1.018)
  waiting for transfers between devices: 9.81 us -> 10.8 us
    all_to_all x1, waiting for transfers between devices: 1.12 us -> 2.13 us  [shards(): lax.all_to_all(rows.reshape(levels, slot_count, wide), 'lev', split_axis=...]
where the time goes in v7:
time: 68.6 us; the launch traced here: 68.3 us
  Pallas kernels  38.3 us (56%)
  starting transfers between devices  17.7 us (26%)
  waiting for transfers between devices  10.8 us (16%)
  between operations  1.05 us (2%)
    pallas_call x1, Pallas kernels, count_edges(): pl.pallas_call(functools.partial(count_kernel, chans=chans), in_specs=[VM...  16.7 us
    pallas_call x2, Pallas kernels, embed(): pl.pallas_call(kernel, in_specs=specs, out_specs=[ANY, VM] + [VM] * len(m...  11.7 us
    all_to_all x1, waiting for transfers between devices, shards(): got = lax.all_to_all(sent, 'lev', split_axis=0, concat_axis=0, tiled=True)  8.65 us
    all_to_all x1, starting transfers between devices, shards(): got = lax.all_to_all(sent, 'lev', split_axis=0, concat_axis=0, tiled=True)  8.59 us
    all_to_all x1, starting transfers between devices, shards(): lax.all_to_all(rows.reshape(levels, slot_count, wide), 'lev', split_axis=...  5.25 us
    pallas_call x1, Pallas kernels, pack(): pl.pallas_call(functools.partial(pack_kernel, parts=parts), in_specs=[sme...  4.23 us
    pallas_call x1, Pallas kernels, node_update(): pl.pallas_call(functools.partial(node_kernel, pad=pad), in_specs=[VM] * l...  3.11 us
    ppermute x1, starting transfers between devices, shards(): from_up = lax.ppermute(low, 'tile', back)  2.2 us
  transfers between devices with their start and end apart: 4, of which 2 were waited for; matrix products, arithmetic and copies ran while one was open for 0% of the time, Pallas kernels for 42%

profile of v7, /device:TPU:1, one launch (start us, length us, event | category | flops | bytes accessed | tf_op | source)
XLA Modules:
  0.0 68.3 jit_solution(2767471051673033295)
XLA Ops:
  0.6 0.0 copy-start.11
  0.6 0.0 copy-start.9
  0.7 0.0 copy-start.10
  0.7 0.0 copy-start.1
  0.7 0.0 copy-start.2
  0.7 0.0 copy-start.3
  0.7 0.0 copy-start.4
  0.7 0.0 copy-start.5
  0.7 0.0 copy-start.6
  0.7 0.0 copy-start.7
  0.7 4.2 %pack.1 = bf16[32,8,3584]{2,1,0:T(8,128)(2,1)} custom-call(s32[1]{0:T(128)} %bitcast.me_ref, f32[224]{0:T(256)} %mean_ref.1, f32[224]{0:T(256)} %scale_ref.1, f32[7,131072]{1,0:T(8,128)} %x_ref.1), custom_call_target="tpu_custom_call" | custom-call | flops 2097152 | bytes 6291456 | tf_op jit(solution)/shard_map/pack/pallas_call | solution.py:95
  5.0 8.6 %all-to-all-start = ((bf16[32,8,3584]{2,1,0:T(8,128)(2,1)}), bf16[32,8,3584]{2,1,0:T(8,128)(2,1)S(1)}, u32[]{:S(2)}, u32[]{:S(2)}) async-start(bf16[32,8,3584]{2,1,0:T(8,128)(2,1)} %pack.1), calls=%async_computation | async-start | bytes 3670016 | tf_op jit(solution)/shard_map/all_to_all | solution.py:477
  13.6 0.0 copy-done.11
  13.6 0.0 copy-done.9
  13.6 0.1 copy.23
  13.7 0.1 reshape.28.src_ref
  13.8 0.0 copy-done.10
  13.8 0.1 copy.24
  13.8 0.1 reshape.29.dst_ref
  13.9 0.0 copy-done.1
  13.9 0.0 copy-done.2
  13.9 0.0 copy-done.3
  13.9 0.0 copy-done.4
  14.0 0.0 copy-done.5
  14.0 0.0 copy-done.6
  14.0 0.0 copy-done.7
  14.0 16.7 %count.1 = (bf16[320,4608]{1,0:T(8,128)(2,1)}, bf16[256,512]{1,0:T(8,128)(2,1)S(1)}, f32[320,512]{1,0:T(8,128)}, bf16[512,512]{1,0:T(8,128)(2,1)}, bf16[512,512]...) custom-call(s32[1,4096]{1,0:T(1,128)S(1)} %copy-done.3, ...), custom_call_target="tpu_custom_call" | custom-call | flops 12079595520 | bytes 2949120 | tf_op jit(solution)/shard_map/count/pallas_call | solution.py:162
  30.7 8.7 %all-to-all-done = bf16[32,8,3584]{2,1,0:T(8,128)(2,1)S(1)} async-done(((bf16[32,8,3584]{2,1,0:T(8,128)(2,1)}), bf16[32,8,3584]{2,1,0:T(8,128)(2,1)S(1)}, u32[]{:S(2)}, u32[]{:S(2)}) %all-to-all-start) | async-done | bytes 1835040 | tf_op jit(solution)/shard_map/all_to_all | solution.py:477
  39.4 0.0 copy-start
  39.4 1.5 %select.1 = (bf16[256,256]{1,0:T(8,128)(2,1)S(1)}, bf16[256,256]{1,0:T(8,128)(2,1)S(1)}, bf16[256,512]{1,0:T(8,128)(2,1)S(1)}) custom-call(bf16[256,3584]{1,0:T(8,128)(2,1)S(1)} %bitcast.9, s32[1,512]{1,0:T(1,128)S(1)} %bitcast.13), custom_call_target="tpu_custom_call" | custom-call | flops 1073741824 | bytes 2097152 | tf_op jit(solution)/shard_map/select/pallas_call | solution.py:220
  40.9 1.7 %collective-permute-start = (bf16[256,256]{1,0:T(8,128)(2,1)S(1)}, bf16[256,256]{1,0:T(8,128)(2,1)S(1)}, u32[]{:S(2)}, u32[]{:S(2)}) collective-permute-start(bf16[256,256]{1,0:T(8,128)(2,1)S(1)} %get-tuple-element.18), channel_id=1, source_target_pairs={{0,32},{32,64},{64,96},{96,0},{1,33},{33,65},{65,97},{97,1},{2,34}... | collective-permute-start | bytes 393224 | tf_op jit(solution)/shard_map/ppermute | solution.py:504
  42.6 2.2 %collective-permute-start.1 = (bf16[256,256]{1,0:T(8,128)(2,1)S(1)}, bf16[256,256]{1,0:T(8,128)(2,1)S(1)}, u32[]{:S(2)}, u32[]{:S(2)}) collective-permute-start(bf16[256,256]{1,0:T(8,128)(2,1)S(1)} %get-tuple-element.19), channel_id=1, source_target_pairs={{32,0},{64,32},{96,64},{0,96},{33,1},{65,33},{97,65},{1,97},{34,2}... | collective-permute-start | bytes 393224 | tf_op jit(solution)/shard_map/ppermute | solution.py:505
  44.8 4.8 %embed.2 = (bf16[4096,512]{1,0:T(8,128)(2,1)}, f32[320,512]{1,0:T(8,128)S(1)}, bf16[256,512]{1,0:T(8,128)(2,1)S(1)}) custom-call(bf16[256,3584]{1,0:T(8,128)(2,1)S(1)} %bitcast.10, bf16[256,512]{1,0:T(8,128)(2,1)S(1)} %get-tuple-element.26.tail_ref, s32[1,512]{1,0:T(1,128)S(1)} %reshape.28.src_ref, bf16[256,512]{1,0:T(8,128)(2,1)S(1)} %get-tuple-element.21.w_in, ...), custom_call_target="tpu_custom_call" | custom-call | flops 2516582400 | bytes 2359296 | tf_op jit(solution)/shard_map/embed/pallas_call | solution.py:378
  49.6 0.0 copy-done
  49.6 0.0 copy-start.8
  49.7 0.0 collective-permute-done.low_ref
  49.7 0.0 collective-permute-done.1.up_ref
  49.7 1.1 %slots.1 = bf16[512,256]{1,0:T(8,128)(2,1)} custom-call(bf16[256,512]{1,0:T(8,128)(2,1)S(1)} %get-tuple-element.30.own_ref, bf16[256,256]{1,0:T(8,128)(2,1)S(1)} %collective-permute-done.low_ref, bf16[256,256]{1,0:T(8,128)(2,1)S(1)} %collective-permute-done.1.up_ref, s32[1,512]{1,0:T(1,128)S(1)} %reshape.28.src_ref, s32[1,512]{1,0:T(1,128)S(1)} %reshape.29.dst_ref), custom_call_target="tpu_custom_call" | custom-call | flops 134217728 | bytes 524288 | tf_op jit(solution)/shard_map/slots/pallas_call | solution.py:248
  50.8 0.0 copy-done.8
  50.8 5.3 %all-to-all-start.1 = ((bf16[32,16,256]{2,1,0:T(8,128)(2,1)}), bf16[32,16,256]{2,1,0:T(8,128)(2,1)S(1)}, u32[]{:S(2)}, u32[]{:S(2)}) async-start(bf16[32,16,256]{2,1,0:T(8,128)(2,1)} %bitcast.5), calls=%async_computation.1 | async-start | bytes 524288 | tf_op jit(solution)/shard_map/all_to_all | solution.py:514
  56.0 6.8 %embed.3 = (bf16[4096,512]{1,0:T(8,128)(2,1)}, f32[320,512]{1,0:T(8,128)S(1)}) custom-call(bf16[256,256]{1,0:T(8,128)(2,1)S(1)} %collective-permute-done.low_ref, bf16[256,256]{1,0:T(8,128)(2,1)S(1)} %collective-permute-done.1.up_ref, bf16[512,512]{1,0:T(8,128)(2,1)S(1)} %get-tuple-element.20.w_both, ...), custom_call_target="tpu_custom_call", output_to_operand_aliasing={{0}: (11, {})} | custom-call | flops 4194304000 | bytes 3932160 | tf_op jit(solution)/shard_map/embed/pallas_call | solution.py:378
  62.9 2.1 %all-to-all-done.1 = bf16[32,16,256]{2,1,0:T(8,128)(2,1)S(1)} async-done(((bf16[32,16,256]{2,1,0:T(8,128)(2,1)}), bf16[32,16,256]{2,1,0:T(8,128)(2,1)S(1)}, u32[]{:S(2)}, u32[]{:S(2)}) %all-to-all-start.1) | async-done | bytes 262176 | tf_op jit(solution)/shard_map/all_to_all | solution.py:514
  65.0 3.1 %node.1 = bf16[320,512]{1,0:T(8,128)(2,1)} custom-call(bf16[512,256]{1,0:T(8,128)(2,1)S(1)} %bitcast.12, bf16[256,512]{1,0:T(8,128)(2,1)S(1)} %get-tuple-element.21.w_in, f32[1,512]{1,0:T(1,128)S(1)} %get-tuple-element.22.b_in, bf16[512,512]{1,0:T(8,128)(2,1)S(1)} %get-tuple-element.20.w_both, f32[1,512]{1,0:T(1,128)S(1)} %get-tuple-element.23.b_msg, ...), custom_call_target="tpu_custom_call" | custom-call | flops 805306368 | bytes 3145728 | tf_op jit(solution)/shard_map/node/pallas_call | solution.py:433
  (1 shorter events, 0.0 us)
Async XLA Ops:
  0.6 12.9 %copy-start.11 = (s32[1,2,256]{2,1,0:T(2,128)S(1)}, s32[1,2,256]{2,1,0:T(2,128)}, u32[]{:S(2)}) copy-start(s32[1,2,256]{2,1,0:T(2,128)} %param.24) | copy-start | bytes 6148
  0.6 12.9 %copy-start.9 = (s32[1,32,16]{1,2,0:T(8,128)S(1)}, s32[1,32,16]{1,2,0:T(8,128)}, u32[]{:S(2)}) copy-start(s32[1,32,16]{1,2,0:T(8,128)} %param.27) | copy-start | bytes 6148
  0.7 13.1 %copy-start.10 = (s32[1,32,16]{1,2,0:T(8,128)S(1)}, s32[1,32,16]{1,2,0:T(8,128)}, u32[]{:S(2)}) copy-start(s32[1,32,16]{1,2,0:T(8,128)} %param.28) | copy-start | bytes 6148
  0.7 13.3 %copy-start.1 = (bf16[320,512]{1,0:T(8,128)(2,1)S(1)}, bf16[320,512]{1,0:T(8,128)(2,1)}, u32[]{:S(2)}) copy-start(bf16[320,512]{1,0:T(8,128)(2,1)} %rest_4_.1) | copy-start | bytes 983044
  0.7 13.3 %copy-start.2 = (bf16[224,512]{1,0:T(8,128)(2,1)S(1)}, bf16[224,512]{1,0:T(8,128)(2,1)}, u32[]{:S(2)}) copy-start(bf16[224,512]{1,0:T(8,128)(2,1)} %w_ref.1) | copy-start | bytes 688132
  0.7 13.3 %copy-start.3 = (s32[1,4096]{1,0:T(1,128)S(1)}, s32[1,4096]{1,0:T(1,128)}, u32[]{:S(2)}) copy-start(s32[1,4096]{1,0:T(1,128)} %src_ref.1) | copy-start | bytes 49156
  0.7 13.3 %copy-start.4 = (s32[1,4096]{1,0:T(1,128)S(1)}, s32[1,4096]{1,0:T(1,128)}, u32[]{:S(2)}) copy-start(s32[1,4096]{1,0:T(1,128)} %dst_ref.1) | copy-start | bytes 49156
  0.7 13.3 %copy-start.5 = (f32[512]{0:T(512)S(1)}, f32[512]{0:T(512)}, u32[]{:S(2)}) copy-start(f32[512]{0:T(512)} %param.22) | copy-start | bytes 6148
  0.7 13.3 %copy-start.6 = (f32[512]{0:T(512)S(1)}, f32[512]{0:T(512)}, u32[]{:S(2)}) copy-start(f32[512]{0:T(512)} %param.34) | copy-start | bytes 6148
  0.7 13.3 %copy-start.7 = (f32[512]{0:T(512)S(1)}, f32[512]{0:T(512)}, u32[]{:S(2)}) copy-start(f32[512]{0:T(512)} %param.30) | copy-start | bytes 6148
  5.0 34.4 %all-to-all-start = ((bf16[32,8,3584]{2,1,0:T(8,128)(2,1)}), bf16[32,8,3584]{2,1,0:T(8,128)(2,1)S(1)}, u32[]{:S(2)}, u32[]{:S(2)}) async-start(bf16[32,8,3584]{2,1,0:T(8,128)(2,1)} %pack.1), calls=%async_computation | async-start | bytes 3670016 | tf_op jit(solution)/shard_map/all_to_all | solution.py:477
  39.4 10.3 %copy-start = (bf16[32,8,3584]{2,1,0:T(8,128)(2,1)}, bf16[32,8,3584]{2,1,0:T(8,128)(2,1)S(1)}, u32[]{:S(2)}) copy-start(bf16[32,8,3584]{2,1,0:T(8,128)(2,1)S(1)} %all-to-all-done) | copy-start | bytes 5505028
  40.9 8.8 %collective-permute-start = (bf16[256,256]{1,0:T(8,128)(2,1)S(1)}, bf16[256,256]{1,0:T(8,128)(2,1)S(1)}, u32[]{:S(2)}, u32[]{:S(2)}) collective-permute-start(bf16[256,256]{1,0:T(8,128)(2,1)S(1)} %get-tuple-element.18), channel_id=1, source_target_pairs={{0,32},{32,64},{64,96},{96,0},{1,33},{33,65},{65,97},{97,1},{2,34}... | collective-permute-start | bytes 393224 | tf_op jit(solution)/shard_map/ppermute | solution.py:504
  42.6 7.1 %collective-permute-start.1 = (bf16[256,256]{1,0:T(8,128)(2,1)S(1)}, bf16[256,256]{1,0:T(8,128)(2,1)S(1)}, u32[]{:S(2)}, u32[]{:S(2)}) collective-permute-start(bf16[256,256]{1,0:T(8,128)(2,1)S(1)} %get-tuple-element.19), channel_id=1, source_target_pairs={{32,0},{64,32},{96,64},{0,96},{33,1},{65,33},{97,65},{1,97},{34,2}... | collective-permute-start | bytes 393224 | tf_op jit(solution)/shard_map/ppermute | solution.py:505
  49.6 1.1 %copy-start.8 = (f32[320,512]{1,0:T(8,128)}, f32[320,512]{1,0:T(8,128)S(1)}, u32[]{:S(2)}) copy-start(f32[320,512]{1,0:T(8,128)S(1)} %get-tuple-element.27.before) | copy-start | bytes 1966084
  50.8 14.2 %all-to-all-start.1 = ((bf16[32,16,256]{2,1,0:T(8,128)(2,1)}), bf16[32,16,256]{2,1,0:T(8,128)(2,1)S(1)}, u32[]{:S(2)}, u32[]{:S(2)}) async-start(bf16[32,16,256]{2,1,0:T(8,128)(2,1)} %bitcast.5), calls=%async_computation.1 | async-start | bytes 524288 | tf_op jit(solution)/shard_map/all_to_all | solution.py:514

commit v8 on v7

--- a/solution.py
+++ b/solution.py
@@ -89,7 +89,7 @@
 def pack(me, mean, scale, fields, levels):
     chans, points = fields.shape
     pts = points // levels
-    parts = 16
+    parts = 8
     smem = pl.BlockSpec(memory_space=pltpu.SMEM)
     shape = (levels, chans + 1, pts * chans // (chans + 1))
     return pl.pallas_call(
@@ -312,9 +312,7 @@
     for c in w_loads:
         c.wait()
     weights = (w_in, b_in, w_out, w_msg, b_msg)
-    cut = spans[0][1]
-    stores = embed_tile(x_ref[:, :cut], weights, lat_ref, act_buf, buf, sem, 0, spans[0][0])
-    stores += embed_tile(tail_ref[...], weights, lat_ref, act_buf, buf, sem, cut, spans[1][0])
+    stores = embed_tile(tail_ref[...], weights, lat_ref, act_buf, buf, sem, 0, spans[0][0])
     for c in loads:
         c.wait()
     sum_ref[...] = dot(s_buf[...], act_buf[...])
@@ -505,9 +503,8 @@
     from_up = lax.ppermute(low, "tile", back)
 
     tile = 2 * PIECE
-    cut = tile
     latent, total, own = embed(
-        x, counts, weights, later, pts, ((0, cut), (main, pts - main)), tile, tail, src
+        x, counts, weights, later, pts, ((main, pts - main),), tile, tail, src
     )
 
     rows = slots_rows(own, from_low, from_up, src, dst, pts, chans)
@@ -521,7 +518,7 @@
         weights,
         later,
         pts,
-        ((cut, main - cut), (pts, 2 * halo)),
+        ((0, main), (pts, 2 * halo)),
         tile,
         before=(latent, total, from_low, from_up),
     )

time: 68.6 us -> 85 us (1.24)
  waiting for transfers between devices: 10.8 us -> 26.1 us
  local copies, waits for them, and re-layouts: 0.37 us -> 1.31 us
    all_to_all x1, waiting for transfers between devices: 8.65 us -> 25.8 us  [shards(): got = lax.all_to_all(sent, 'lev', split_axis=0, concat_axis=0, tiled=True)]
    all_to_all x1, waiting for transfers between devices: 2.13 us -> 0.27 us  [shards(): lax.all_to_all(rows.reshape(levels, slot_count, wide), 'lev', split_axis=...]
    unnamed x27, local copies, waits for them, and re-layouts: 0.21 us -> 1.14 us
  transfers between devices with their start and end apart: 4 -> 4, of which waited for: 2 -> 2; matrix products, arithmetic and copies ran while one was open for 0% -> 0% of each run, Pallas kernels for 42% -> 33%
where the time goes in v8:
time: 85 us; the launch traced here: 84.7 us
  Pallas kernels  38.6 us (45%)
  waiting for transfers between devices  26.1 us (31%)
  starting transfers between devices  17.7 us (21%)
  local copies, waits for them, and re-layouts  1.31 us (2%)
  between operations  0.99 us (1%)
    all_to_all x1, waiting for transfers between devices, shards(): got = lax.all_to_all(sent, 'lev', split_axis=0, concat_axis=0, tiled=True)  25.8 us
    pallas_call x1, Pallas kernels, count_edges(): pl.pallas_call(functools.partial(count_kernel, chans=chans), in_specs=[VM...  16.7 us
    pallas_call x2, Pallas kernels, embed(): pl.pallas_call(kernel, in_specs=specs, out_specs=[ANY, VM] + [VM] * len(m...  11.4 us
    all_to_all x1, starting transfers between devices, shards(): got = lax.all_to_all(sent, 'lev', split_axis=0, concat_axis=0, tiled=True)  8.72 us
    all_to_all x1, starting transfers between devices, shards(): lax.all_to_all(rows.reshape(levels, slot_count, wide), 'lev', split_axis=...  5.23 us
    pallas_call x1, Pallas kernels, pack(): pl.pallas_call(functools.partial(pack_kernel, parts=parts), in_specs=[sme...  4.05 us
    pallas_call x1, Pallas kernels, node_update(): pl.pallas_call(functools.partial(node_kernel, pad=pad), in_specs=[VM] * l...  3.11 us
    pallas_call x1, Pallas kernels, select(): pl.pallas_call(functools.partial(select_kernel, chans=chans), in_specs=[V...  2.2 us
  transfers between devices with their start and end apart: 4, of which 2 were waited for; matrix products, arithmetic and copies ran while one was open for 0% of the time, Pallas kernels for 33%

profile of v8, /device:TPU:1, one launch (start us, length us, event | category | flops | bytes accessed | tf_op | source)
XLA Modules:
  0.0 84.7 jit_solution(3295268590242047983)
XLA Ops:
  0.6 0.0 copy-start.11
  0.6 4.1 %pack.1 = bf16[32,8,3584]{2,1,0:T(8,128)(2,1)} custom-call(s32[1]{0:T(128)} %bitcast.me_ref, f32[224]{0:T(256)} %mean_ref.1, f32[224]{0:T(256)} %scale_ref.1, f32[7,131072]{1,0:T(8,128)} %x_ref.1), custom_call_target="tpu_custom_call" | custom-call | flops 2097152 | bytes 6291456 | tf_op jit(solution)/shard_map/pack/pallas_call | solution.py:95
  4.7 0.0 copy-start.1
  4.7 0.0 copy-start.4
  4.7 0.0 copy-start.5
  4.7 0.0 copy-start.6
  4.8 0.0 copy-start.7
  4.8 0.0 copy-start.8
  4.8 8.7 %all-to-all-start = ((bf16[32,8,3584]{2,1,0:T(8,128)(2,1)}), bf16[32,8,3584]{2,1,0:T(8,128)(2,1)S(1)}, u32[]{:S(2)}, u32[]{:S(2)}) async-start(bf16[32,8,3584]{2,1,0:T(8,128)(2,1)} %pack.1), calls=%async_computation | async-start | bytes 3670016 | tf_op jit(solution)/shard_map/all_to_all | solution.py:475
  13.5 0.0 copy-done.11
  13.5 25.8 %all-to-all-done = bf16[32,8,3584]{2,1,0:T(8,128)(2,1)S(1)} async-done(((bf16[32,8,3584]{2,1,0:T(8,128)(2,1)}), bf16[32,8,3584]{2,1,0:T(8,128)(2,1)S(1)}, u32[]{:S(2)}, u32[]{:S(2)}) %all-to-all-start) | async-done | bytes 1835040 | tf_op jit(solution)/shard_map/all_to_all | solution.py:475
  39.3 0.0 copy-start
  39.3 2.2 %select.1 = (bf16[256,256]{1,0:T(8,128)(2,1)}, bf16[256,256]{1,0:T(8,128)(2,1)}, bf16[256,512]{1,0:T(8,128)(2,1)S(1)}) custom-call(bf16[256,3584]{1,0:T(8,128)(2,1)S(1)} %bitcast.9, s32[1,512]{1,0:T(1,128)S(1)} %bitcast.13), custom_call_target="tpu_custom_call" | custom-call | flops 1073741824 | bytes 2097152 | tf_op jit(solution)/shard_map/select/pallas_call | solution.py:220
  41.5 1.6 %collective-permute-start = (bf16[256,256]{1,0:T(8,128)(2,1)}, bf16[256,256]{1,0:T(8,128)(2,1)S(1)}, u32[]{:S(2)}, u32[]{:S(2)}) collective-permute-start(bf16[256,256]{1,0:T(8,128)(2,1)} %get-tuple-element.18), channel_id=1, source_target_pairs={{0,32},{32,64},{64,96},{96,0},{1,33},{33,65},{65,97},{97,1},{2,34}... | collective-permute-start | bytes 393224 | tf_op jit(solution)/shard_map/ppermute | solution.py:502
  43.2 2.1 %collective-permute-start.1 = (bf16[256,256]{1,0:T(8,128)(2,1)}, bf16[256,256]{1,0:T(8,128)(2,1)S(1)}, u32[]{:S(2)}, u32[]{:S(2)}) collective-permute-start(bf16[256,256]{1,0:T(8,128)(2,1)} %get-tuple-element.19), channel_id=1, source_target_pairs={{32,0},{64,32},{96,64},{0,96},{33,1},{65,33},{97,65},{1,97},{34,2}... | collective-permute-start | bytes 393224 | tf_op jit(solution)/shard_map/ppermute | solution.py:503
  45.3 0.0 copy-done.1
  45.3 0.0 copy-done.4
  45.3 0.0 copy-done.5
  45.3 0.0 copy-done.6
  45.3 0.0 copy-done.7
  45.3 0.0 copy-done.8
  45.3 0.0 copy-start.3
  45.3 0.9 %copy-done.3 = bf16[224,512]{1,0:T(8,128)(2,1)S(1)} copy-done((bf16[224,512]{1,0:T(8,128)(2,1)S(1)}, bf16[224,512]{1,0:T(8,128)(2,1)}, u32[]{:S(2)}) %copy-start.3) | copy-done | bytes 229400
  46.3 0.0 copy-start.9
  46.3 0.0 copy-start.10
  46.3 16.7 %count.1 = (bf16[320,4608]{1,0:T(8,128)(2,1)}, bf16[256,512]{1,0:T(8,128)(2,1)S(1)}, f32[320,512]{1,0:T(8,128)}, bf16[512,512]{1,0:T(8,128)(2,1)}, bf16[512,512]...) custom-call(s32[1,4096]{1,0:T(1,128)S(1)} %copy-done.4, ...), custom_call_target="tpu_custom_call" | custom-call | flops 12079595520 | bytes 2949120 | tf_op jit(solution)/shard_map/count/pallas_call | solution.py:162
  63.0 0.0 copy-done.9
  63.0 0.1 copy.23
  63.1 0.1 reshape.28.src_ref
  63.2 0.0 copy-done.10
  63.2 0.1 copy.24
  63.3 0.1 reshape.29.dst_ref
  63.3 0.0 copy-done
  63.3 2.7 %embed.2 = (bf16[4096,512]{1,0:T(8,128)(2,1)}, f32[320,512]{1,0:T(8,128)S(1)}, bf16[256,512]{1,0:T(8,128)(2,1)S(1)}) custom-call(bf16[256,3584]{1,0:T(8,128)(2,1)S(1)} %bitcast.10, bf16[256,512]{1,0:T(8,128)(2,1)S(1)} %get-tuple-element.26.tail_ref, s32[1,512]{1,0:T(1,128)S(1)} %reshape.28.src_ref, bf16[256,512]{1,0:T(8,128)(2,1)S(1)} %get-tuple-element.21.w_in, ...), custom_call_target="tpu_custom_call" | custom-call | flops 838860800 | bytes 786432 | tf_op jit(solution)/shard_map/embed/pallas_call | solution.py:376
  66.0 0.0 copy-start.2
  66.1 0.0 collective-permute-done.low_ref
  66.1 0.0 collective-permute-done.1.up_ref
  66.1 1.1 %slots.1 = bf16[512,256]{1,0:T(8,128)(2,1)} custom-call(bf16[256,512]{1,0:T(8,128)(2,1)S(1)} %get-tuple-element.30.own_ref, bf16[256,256]{1,0:T(8,128)(2,1)S(1)} %collective-permute-done.low_ref, bf16[256,256]{1,0:T(8,128)(2,1)S(1)} %collective-permute-done.1.up_ref, s32[1,512]{1,0:T(1,128)S(1)} %reshape.28.src_ref, s32[1,512]{1,0:T(1,128)S(1)} %reshape.29.dst_ref), custom_call_target="tpu_custom_call" | custom-call | flops 134217728 | bytes 524288 | tf_op jit(solution)/shard_map/slots/pallas_call | solution.py:248
  67.2 0.0 copy-done.2
  67.2 5.2 %all-to-all-start.1 = ((bf16[32,16,256]{2,1,0:T(8,128)(2,1)}), bf16[32,16,256]{2,1,0:T(8,128)(2,1)S(1)}, u32[]{:S(2)}, u32[]{:S(2)}) async-start(bf16[32,16,256]{2,1,0:T(8,128)(2,1)} %bitcast.5), calls=%async_computation.1 | async-start | bytes 524288 | tf_op jit(solution)/shard_map/all_to_all | solution.py:511
  72.4 8.7 %embed.3 = (bf16[4096,512]{1,0:T(8,128)(2,1)}, f32[320,512]{1,0:T(8,128)S(1)}) custom-call(bf16[256,256]{1,0:T(8,128)(2,1)S(1)} %collective-permute-done.low_ref, bf16[256,256]{1,0:T(8,128)(2,1)S(1)} %collective-permute-done.1.up_ref, bf16[512,512]{1,0:T(8,128)(2,1)S(1)} %get-tuple-element.20.w_both, ...), custom_call_target="tpu_custom_call", output_to_operand_aliasing={{0}: (11, {})} | custom-call | flops 5872025600 | bytes 5505024 | tf_op jit(solution)/shard_map/embed/pallas_call | solution.py:376
  81.1 0.3 all-to-all-done.1
  81.4 3.1 %node.1 = bf16[320,512]{1,0:T(8,128)(2,1)} custom-call(bf16[512,256]{1,0:T(8,128)(2,1)S(1)} %bitcast.12, bf16[256,512]{1,0:T(8,128)(2,1)S(1)} %get-tuple-element.21.w_in, f32[1,512]{1,0:T(1,128)S(1)} %get-tuple-element.22.b_in, bf16[512,512]{1,0:T(8,128)(2,1)S(1)} %get-tuple-element.20.w_both, f32[1,512]{1,0:T(1,128)S(1)} %get-tuple-element.23.b_msg, ...), custom_call_target="tpu_custom_call" | custom-call | flops 805306368 | bytes 3145728 | tf_op jit(solution)/shard_map/node/pallas_call | solution.py:431
  (1 shorter events, 0.0 us)
Async XLA Ops:
  0.6 12.9 %copy-start.11 = (s32[1,2,256]{2,1,0:T(2,128)S(1)}, s32[1,2,256]{2,1,0:T(2,128)}, u32[]{:S(2)}) copy-start(s32[1,2,256]{2,1,0:T(2,128)} %param.24) | copy-start | bytes 6148
  4.7 40.6 %copy-start.1 = (bf16[320,512]{1,0:T(8,128)(2,1)S(1)}, bf16[320,512]{1,0:T(8,128)(2,1)}, u32[]{:S(2)}) copy-start(bf16[320,512]{1,0:T(8,128)(2,1)} %rest_4_.1) | copy-start | bytes 983044
  4.7 40.6 %copy-start.4 = (s32[1,4096]{1,0:T(1,128)S(1)}, s32[1,4096]{1,0:T(1,128)}, u32[]{:S(2)}) copy-start(s32[1,4096]{1,0:T(1,128)} %src_ref.1) | copy-start | bytes 49156
  4.7 40.6 %copy-start.5 = (s32[1,4096]{1,0:T(1,128)S(1)}, s32[1,4096]{1,0:T(1,128)}, u32[]{:S(2)}) copy-start(s32[1,4096]{1,0:T(1,128)} %dst_ref.1) | copy-start | bytes 49156
  4.7 40.6 %copy-start.6 = (f32[512]{0:T(512)S(1)}, f32[512]{0:T(512)}, u32[]{:S(2)}) copy-start(f32[512]{0:T(512)} %param.22) | copy-start | bytes 6148
  4.8 40.6 %copy-start.7 = (f32[512]{0:T(512)S(1)}, f32[512]{0:T(512)}, u32[]{:S(2)}) copy-start(f32[512]{0:T(512)} %param.34) | copy-start | bytes 6148
  4.8 40.5 %copy-start.8 = (f32[512]{0:T(512)S(1)}, f32[512]{0:T(512)}, u32[]{:S(2)}) copy-start(f32[512]{0:T(512)} %param.30) | copy-start | bytes 6148
  4.8 34.5 %all-to-all-start = ((bf16[32,8,3584]{2,1,0:T(8,128)(2,1)}), bf16[32,8,3584]{2,1,0:T(8,128)(2,1)S(1)}, u32[]{:S(2)}, u32[]{:S(2)}) async-start(bf16[32,8,3584]{2,1,0:T(8,128)(2,1)} %pack.1), calls=%async_computation | async-start | bytes 3670016 | tf_op jit(solution)/shard_map/all_to_all | solution.py:475
  39.3 24.0 %copy-start = (bf16[32,8,3584]{2,1,0:T(8,128)(2,1)}, bf16[32,8,3584]{2,1,0:T(8,128)(2,1)S(1)}, u32[]{:S(2)}) copy-start(bf16[32,8,3584]{2,1,0:T(8,128)(2,1)S(1)} %all-to-all-done) | copy-start | bytes 5505028
  41.5 24.5 %collective-permute-start = (bf16[256,256]{1,0:T(8,128)(2,1)}, bf16[256,256]{1,0:T(8,128)(2,1)S(1)}, u32[]{:S(2)}, u32[]{:S(2)}) collective-permute-start(bf16[256,256]{1,0:T(8,128)(2,1)} %get-tuple-element.18), channel_id=1, source_target_pairs={{0,32},{32,64},{64,96},{96,0},{1,33},{33,65},{65,97},{97,1},{2,34}... | collective-permute-start | bytes 393224 | tf_op jit(solution)/shard_map/ppermute | solution.py:502
  43.2 22.9 %collective-permute-start.1 = (bf16[256,256]{1,0:T(8,128)(2,1)}, bf16[256,256]{1,0:T(8,128)(2,1)S(1)}, u32[]{:S(2)}, u32[]{:S(2)}) collective-permute-start(bf16[256,256]{1,0:T(8,128)(2,1)} %get-tuple-element.19), channel_id=1, source_target_pairs={{32,0},{64,32},{96,64},{0,96},{33,1},{65,33},{97,65},{1,97},{34,2}... | collective-permute-start | bytes 393224 | tf_op jit(solution)/shard_map/ppermute | solution.py:503
  45.3 0.9 %copy-start.3 = (bf16[224,512]{1,0:T(8,128)(2,1)S(1)}, bf16[224,512]{1,0:T(8,128)(2,1)}, u32[]{:S(2)}) copy-start(bf16[224,512]{1,0:T(8,128)(2,1)} %w_ref.1) | copy-start | bytes 688132
  46.3 16.7 %copy-start.9 = (s32[1,32,16]{1,2,0:T(8,128)S(1)}, s32[1,32,16]{1,2,0:T(8,128)}, u32[]{:S(2)}) copy-start(s32[1,32,16]{1,2,0:T(8,128)} %param.27) | copy-start | bytes 6148
  46.3 16.9 %copy-start.10 = (s32[1,32,16]{1,2,0:T(8,128)S(1)}, s32[1,32,16]{1,2,0:T(8,128)}, u32[]{:S(2)}) copy-start(s32[1,32,16]{1,2,0:T(8,128)} %param.28) | copy-start | bytes 6148
  66.0 1.1 %copy-start.2 = (f32[320,512]{1,0:T(8,128)}, f32[320,512]{1,0:T(8,128)S(1)}, u32[]{:S(2)}) copy-start(f32[320,512]{1,0:T(8,128)S(1)} %get-tuple-element.27.before) | copy-start | bytes 1966084
  67.2 14.2 %all-to-all-start.1 = ((bf16[32,16,256]{2,1,0:T(8,128)(2,1)}), bf16[32,16,256]{2,1,0:T(8,128)(2,1)S(1)}, u32[]{:S(2)}, u32[]{:S(2)}) async-start(bf16[32,16,256]{2,1,0:T(8,128)(2,1)} %bitcast.5), calls=%async_computation.1 | async-start | bytes 524288 | tf_op jit(solution)/shard_map/all_to_all | solution.py:511

commit v9 on v8

--- a/solution.py
+++ b/solution.py
@@ -7,6 +7,7 @@
 from jax.experimental.pallas import tpu as pltpu
 from jax.sharding import PartitionSpec as P
 
+
 BF = jnp.bfloat16
 F32 = jnp.float32
 NT = (((1,), (1,)), ((), ()))
@@ -17,10 +18,6 @@
 
 def params(mib, **kw):
     return pltpu.CompilerParams(vmem_limit_bytes=mib * MIB, **kw)
-
-
-def whole(shape):
-    return pl.BlockSpec(shape, lambda *_: (0,) * len(shape))
 
 
 def cost(flops, nbytes):
@@ -476,8 +473,12 @@
     main = pts // (chans + 1) * chans
     x = got.reshape(wide, main)
 
+    src = remote_src.reshape(1, -1)
+    dst = remote_dst.reshape(1, -1)
+    idx = halo_index.reshape(1, 2 * halo)
+    first_src, src, dst, idx = lax.optimization_barrier((local_src, src, dst, idx))
     counts, w_in, pre, w_msg, w_both, b_in, b_out, w_nb = count_edges(
-        local_src,
+        first_src,
         local_dst,
         w_embed_in,
         b_embed[None, :],
@@ -494,9 +495,7 @@
     weights = [w_in, b_in, w_both, b_out]
     later = [w_embed_out, w_msg]
 
-    src = remote_src.reshape(1, -1)
-    dst = remote_dst.reshape(1, -1)
-    low, high, tail = select(x, halo_index.reshape(1, 2 * halo), chans)
+    low, high, tail = select(x, idx, chans)
     ahead = [(i, (i + 1) % tiles) for i in range(tiles)]
     back = [(t, s) for s, t in ahead]
     from_low = lax.ppermute(high, "tile", ahead)

time: 85 us -> 83.3 us (0.980)
  local copies, waits for them, and re-layouts: 1.31 us -> 0.38 us
    unnamed x27, local copies, waits for them, and re-layouts: 1.14 us -> 0.22 us
  transfers between devices with their start and end apart: 4 -> 4, of which waited for: 2 -> 2; matrix products, arithmetic and copies ran while one was open for 0% -> 0% of each run, Pallas kernels for 33% -> 34%
where the time goes in v9:
time: 83.3 us; the launch traced here: 82.9 us
  Pallas kernels  37.9 us (45%)
  waiting for transfers between devices  25.7 us (31%)
  starting transfers between devices  17.9 us (21%)
  between operations  1.02 us (1%)
    all_to_all x1, waiting for transfers between devices, shards(): got = lax.all_to_all(sent, 'lev', split_axis=0, concat_axis=0, tiled=True)  25.5 us
    pallas_call x1, Pallas kernels, count_edges(): pl.pallas_call(functools.partial(count_kernel, chans=chans), in_specs=[VM...  16.7 us
    pallas_call x2, Pallas kernels, embed(): pl.pallas_call(kernel, in_specs=specs, out_specs=[ANY, VM] + [VM] * len(m...  11.4 us
    all_to_all x1, starting transfers between devices, shards(): got = lax.all_to_all(sent, 'lev', split_axis=0, concat_axis=0, tiled=True)  8.72 us
    all_to_all x1, starting transfers between devices, shards(): lax.all_to_all(rows.reshape(levels, slot_count, wide), 'lev', split_axis=...  5.23 us
    pallas_call x1, Pallas kernels, pack(): pl.pallas_call(functools.partial(pack_kernel, parts=parts), in_specs=[sme...  4.05 us
    pallas_call x1, Pallas kernels, node_update(): pl.pallas_call(functools.partial(node_kernel, pad=pad), in_specs=[VM] * l...  3.11 us
    ppermute x1, starting transfers between devices, shards(): from_up = lax.ppermute(low, 'tile', back)  2.2 us
  transfers between devices with their start and end apart: 4, of which 2 were waited for; matrix products, arithmetic and copies ran while one was open for 0% of the time, Pallas kernels for 34%

profile of v9, /device:TPU:1, one launch (start us, length us, event | category | flops | bytes accessed | tf_op | source)
XLA Modules:
  0.0 82.9 jit_solution(13415005074804354083)
XLA Ops:
  0.6 0.0 copy-start.9
  0.6 0.0 copy-start.10
  0.7 0.0 copy-start.11
  0.7 4.1 %pack.1 = bf16[32,8,3584]{2,1,0:T(8,128)(2,1)} custom-call(s32[1]{0:T(128)} %bitcast.me_ref, f32[224]{0:T(256)} %mean_ref.1, f32[224]{0:T(256)} %scale_ref.1, f32[7,131072]{1,0:T(8,128)} %x_ref.1), custom_call_target="tpu_custom_call" | custom-call | flops 2097152 | bytes 6291456 | tf_op jit(solution)/shard_map/pack/pallas_call | solution.py:92
  4.7 0.0 copy-start.1
  4.7 0.0 copy-start.3
  4.7 0.0 copy-start.4
  4.8 0.0 copy-start.5
  4.8 0.0 copy-start.6
  4.8 0.0 copy-start.7
  4.8 0.0 copy-start.8
  4.8 8.7 %all-to-all-start = ((bf16[32,8,3584]{2,1,0:T(8,128)(2,1)}), bf16[32,8,3584]{2,1,0:T(8,128)(2,1)S(1)}, u32[]{:S(2)}, u32[]{:S(2)}) async-start(bf16[32,8,3584]{2,1,0:T(8,128)(2,1)} %pack.1), calls=%async_computation | async-start | bytes 3670016 | tf_op jit(solution)/shard_map/all_to_all | solution.py:472
  13.5 0.0 copy-done.9
  13.5 0.1 copy.23
  13.6 0.1 reshape.27.src_ref
  13.7 0.0 copy-done.10
  13.7 0.1 copy.24
  13.8 0.1 reshape.28.dst_ref
  13.9 0.0 copy-done.11
  13.9 25.5 %all-to-all-done = bf16[32,8,3584]{2,1,0:T(8,128)(2,1)S(1)} async-done(((bf16[32,8,3584]{2,1,0:T(8,128)(2,1)}), bf16[32,8,3584]{2,1,0:T(8,128)(2,1)S(1)}, u32[]{:S(2)}, u32[]{:S(2)}) %all-to-all-start) | async-done | bytes 1835040 | tf_op jit(solution)/shard_map/all_to_all | solution.py:472
  39.4 0.0 copy-start
  39.4 1.5 %select.1 = (bf16[256,256]{1,0:T(8,128)(2,1)S(1)}, bf16[256,256]{1,0:T(8,128)(2,1)S(1)}, bf16[256,512]{1,0:T(8,128)(2,1)S(1)}) custom-call(bf16[256,3584]{1,0:T(8,128)(2,1)S(1)} %bitcast.9, s32[1,512]{1,0:T(1,128)S(1)} %bitcast.13), custom_call_target="tpu_custom_call" | custom-call | flops 1073741824 | bytes 2097152 | tf_op jit(solution)/shard_map/select/pallas_call | solution.py:217
  40.9 1.7 %collective-permute-start = (bf16[256,256]{1,0:T(8,128)(2,1)S(1)}, bf16[256,256]{1,0:T(8,128)(2,1)S(1)}, u32[]{:S(2)}, u32[]{:S(2)}) collective-permute-start(bf16[256,256]{1,0:T(8,128)(2,1)S(1)} %get-tuple-element.23), channel_id=1, source_target_pairs={{0,32},{32,64},{64,96},{96,0},{1,33},{33,65},{65,97},{97,1},{2,34}... | collective-permute-start | bytes 393224 | tf_op jit(solution)/shard_map/ppermute | solution.py:501
  42.6 2.2 %collective-permute-start.1 = (bf16[256,256]{1,0:T(8,128)(2,1)S(1)}, bf16[256,256]{1,0:T(8,128)(2,1)S(1)}, u32[]{:S(2)}, u32[]{:S(2)}) collective-permute-start(bf16[256,256]{1,0:T(8,128)(2,1)S(1)} %get-tuple-element.24), channel_id=1, source_target_pairs={{32,0},{64,32},{96,64},{0,96},{33,1},{65,33},{97,65},{1,97},{34,2}... | collective-permute-start | bytes 393224 | tf_op jit(solution)/shard_map/ppermute | solution.py:502
  44.8 0.0 copy-done.1
  44.8 0.0 copy-done.3
  44.8 0.0 copy-done.4
  44.8 0.0 copy-done.5
  44.8 0.0 copy-done.6
  44.8 0.0 copy-done.7
  44.8 0.0 copy-done.8
  44.8 16.7 %count.1 = (bf16[320,4608]{1,0:T(8,128)(2,1)}, bf16[256,512]{1,0:T(8,128)(2,1)S(1)}, f32[320,512]{1,0:T(8,128)}, bf16[512,512]{1,0:T(8,128)(2,1)}, bf16[512,512]...) custom-call(s32[1,4096]{1,0:T(1,128)S(1)} %copy-done.4, ...), custom_call_target="tpu_custom_call" | custom-call | flops 12079595520 | bytes 2949120 | tf_op jit(solution)/shard_map/count/pallas_call | solution.py:159
  61.6 0.0 copy-done
  61.6 2.7 %embed.2 = (bf16[4096,512]{1,0:T(8,128)(2,1)}, f32[320,512]{1,0:T(8,128)S(1)}, bf16[256,512]{1,0:T(8,128)(2,1)S(1)}) custom-call(bf16[256,3584]{1,0:T(8,128)(2,1)S(1)} %bitcast.10, bf16[256,512]{1,0:T(8,128)(2,1)S(1)} %get-tuple-element.32.tail_ref, s32[1,512]{1,0:T(1,128)S(1)} %reshape.27.src_ref, bf16[256,512]{1,0:T(8,128)(2,1)S(1)} %get-tuple-element.27.w_in, ...), custom_call_target="tpu_custom_call" | custom-call | flops 838860800 | bytes 786432 | tf_op jit(solution)/shard_map/embed/pallas_call | solution.py:373
  64.3 0.0 copy-start.2
  64.3 0.0 collective-permute-done.low_ref
  64.3 0.0 collective-permute-done.1.up_ref
  64.3 1.1 %slots.1 = bf16[512,256]{1,0:T(8,128)(2,1)} custom-call(bf16[256,512]{1,0:T(8,128)(2,1)S(1)} %get-tuple-element.37.own_ref, bf16[256,256]{1,0:T(8,128)(2,1)S(1)} %collective-permute-done.low_ref, bf16[256,256]{1,0:T(8,128)(2,1)S(1)} %collective-permute-done.1.up_ref, s32[1,512]{1,0:T(1,128)S(1)} %reshape.27.src_ref, s32[1,512]{1,0:T(1,128)S(1)} %reshape.28.dst_ref), custom_call_target="tpu_custom_call" | custom-call | flops 134217728 | bytes 524288 | tf_op jit(solution)/shard_map/slots/pallas_call | solution.py:245
  65.4 0.0 copy-done.2
  65.4 5.2 %all-to-all-start.1 = ((bf16[32,16,256]{2,1,0:T(8,128)(2,1)}), bf16[32,16,256]{2,1,0:T(8,128)(2,1)S(1)}, u32[]{:S(2)}, u32[]{:S(2)}) async-start(bf16[32,16,256]{2,1,0:T(8,128)(2,1)} %bitcast.5), calls=%async_computation.1 | async-start | bytes 524288 | tf_op jit(solution)/shard_map/all_to_all | solution.py:510
  70.7 8.7 %embed.3 = (bf16[4096,512]{1,0:T(8,128)(2,1)}, f32[320,512]{1,0:T(8,128)S(1)}) custom-call(bf16[256,256]{1,0:T(8,128)(2,1)S(1)} %collective-permute-done.low_ref, bf16[256,256]{1,0:T(8,128)(2,1)S(1)} %collective-permute-done.1.up_ref, bf16[512,512]{1,0:T(8,128)(2,1)S(1)} %get-tuple-element.26.w_both, ...), custom_call_target="tpu_custom_call", output_to_operand_aliasing={{0}: (11, {})} | custom-call | flops 5872025600 | bytes 5505024 | tf_op jit(solution)/shard_map/embed/pallas_call | solution.py:373
  79.4 0.3 all-to-all-done.1
  79.6 3.1 %node.1 = bf16[320,512]{1,0:T(8,128)(2,1)} custom-call(bf16[512,256]{1,0:T(8,128)(2,1)S(1)} %bitcast.12, bf16[256,512]{1,0:T(8,128)(2,1)S(1)} %get-tuple-element.27.w_in, f32[1,512]{1,0:T(1,128)S(1)} %get-tuple-element.28.b_in, bf16[512,512]{1,0:T(8,128)(2,1)S(1)} %get-tuple-element.26.w_both, f32[1,512]{1,0:T(1,128)S(1)} %get-tuple-element.29.b_msg, ...), custom_call_target="tpu_custom_call" | custom-call | flops 805306368 | bytes 3145728 | tf_op jit(solution)/shard_map/node/pallas_call | solution.py:428
  (1 shorter events, 0.0 us)
Async XLA Ops:
  0.6 12.9 %copy-start.9 = (s32[1,32,16]{1,2,0:T(8,128)S(1)}, s32[1,32,16]{1,2,0:T(8,128)}, u32[]{:S(2)}) copy-start(s32[1,32,16]{1,2,0:T(8,128)} %param.27) | copy-start | bytes 6148
  0.6 13.1 %copy-start.10 = (s32[1,32,16]{1,2,0:T(8,128)S(1)}, s32[1,32,16]{1,2,0:T(8,128)}, u32[]{:S(2)}) copy-start(s32[1,32,16]{1,2,0:T(8,128)} %param.28) | copy-start | bytes 6148
  0.7 13.2 %copy-start.11 = (s32[1,2,256]{2,1,0:T(2,128)S(1)}, s32[1,2,256]{2,1,0:T(2,128)}, u32[]{:S(2)}) copy-start(s32[1,2,256]{2,1,0:T(2,128)} %param.24) | copy-start | bytes 6148
  4.7 40.1 %copy-start.1 = (bf16[320,512]{1,0:T(8,128)(2,1)S(1)}, bf16[320,512]{1,0:T(8,128)(2,1)}, u32[]{:S(2)}) copy-start(bf16[320,512]{1,0:T(8,128)(2,1)} %rest_4_.1) | copy-start | bytes 983044
  4.7 40.0 %copy-start.3 = (bf16[224,512]{1,0:T(8,128)(2,1)S(1)}, bf16[224,512]{1,0:T(8,128)(2,1)}, u32[]{:S(2)}) copy-start(bf16[224,512]{1,0:T(8,128)(2,1)} %w_ref.1) | copy-start | bytes 688132
  4.7 40.0 %copy-start.4 = (s32[1,4096]{1,0:T(1,128)S(1)}, s32[1,4096]{1,0:T(1,128)}, u32[]{:S(2)}) copy-start(s32[1,4096]{1,0:T(1,128)} %src_ref) | copy-start | bytes 49156
  4.8 40.0 %copy-start.5 = (s32[1,4096]{1,0:T(1,128)S(1)}, s32[1,4096]{1,0:T(1,128)}, u32[]{:S(2)}) copy-start(s32[1,4096]{1,0:T(1,128)} %dst_ref.1) | copy-start | bytes 49156
  4.8 40.0 %copy-start.6 = (f32[512]{0:T(512)S(1)}, f32[512]{0:T(512)}, u32[]{:S(2)}) copy-start(f32[512]{0:T(512)} %param.22) | copy-start | bytes 6148
  4.8 40.0 %copy-start.7 = (f32[512]{0:T(512)S(1)}, f32[512]{0:T(512)}, u32[]{:S(2)}) copy-start(f32[512]{0:T(512)} %param.34) | copy-start | bytes 6148
  4.8 40.0 %copy-start.8 = (f32[512]{0:T(512)S(1)}, f32[512]{0:T(512)}, u32[]{:S(2)}) copy-start(f32[512]{0:T(512)} %param.30) | copy-start | bytes 6148
  4.8 34.5 %all-to-all-start = ((bf16[32,8,3584]{2,1,0:T(8,128)(2,1)}), bf16[32,8,3584]{2,1,0:T(8,128)(2,1)S(1)}, u32[]{:S(2)}, u32[]{:S(2)}) async-start(bf16[32,8,3584]{2,1,0:T(8,128)(2,1)} %pack.1), calls=%async_computation | async-start | bytes 3670016 | tf_op jit(solution)/shard_map/all_to_all | solution.py:472
  39.4 22.2 %copy-start = (bf16[32,8,3584]{2,1,0:T(8,128)(2,1)}, bf16[32,8,3584]{2,1,0:T(8,128)(2,1)S(1)}, u32[]{:S(2)}) copy-start(bf16[32,8,3584]{2,1,0:T(8,128)(2,1)S(1)} %all-to-all-done) | copy-start | bytes 5505028
  40.9 23.4 %collective-permute-start = (bf16[256,256]{1,0:T(8,128)(2,1)S(1)}, bf16[256,256]{1,0:T(8,128)(2,1)S(1)}, u32[]{:S(2)}, u32[]{:S(2)}) collective-permute-start(bf16[256,256]{1,0:T(8,128)(2,1)S(1)} %get-tuple-element.23), channel_id=1, source_target_pairs={{0,32},{32,64},{64,96},{96,0},{1,33},{33,65},{65,97},{97,1},{2,34}... | collective-permute-start | bytes 393224 | tf_op jit(solution)/shard_map/ppermute | solution.py:501
  42.6 21.7 %collective-permute-start.1 = (bf16[256,256]{1,0:T(8,128)(2,1)S(1)}, bf16[256,256]{1,0:T(8,128)(2,1)S(1)}, u32[]{:S(2)}, u32[]{:S(2)}) collective-permute-start(bf16[256,256]{1,0:T(8,128)(2,1)S(1)} %get-tuple-element.24), channel_id=1, source_target_pairs={{32,0},{64,32},{96,64},{0,96},{33,1},{65,33},{97,65},{1,97},{34,2}... | collective-permute-start | bytes 393224 | tf_op jit(solution)/shard_map/ppermute | solution.py:502
  64.3 1.1 %copy-start.2 = (f32[320,512]{1,0:T(8,128)}, f32[320,512]{1,0:T(8,128)S(1)}, u32[]{:S(2)}) copy-start(f32[320,512]{1,0:T(8,128)S(1)} %get-tuple-element.34.before) | copy-start | bytes 1966084
  65.4 14.2 %all-to-all-start.1 = ((bf16[32,16,256]{2,1,0:T(8,128)(2,1)}), bf16[32,16,256]{2,1,0:T(8,128)(2,1)S(1)}, u32[]{:S(2)}, u32[]{:S(2)}) async-start(bf16[32,16,256]{2,1,0:T(8,128)(2,1)} %bitcast.5), calls=%async_computation.1 | async-start | bytes 524288 | tf_op jit(solution)/shard_map/all_to_all | solution.py:510

commit v10 on v9

--- a/solution.py
+++ b/solution.py
@@ -263,20 +263,6 @@
     return silu2(dot(hidden, w_both[...]) + b_msg[...])
 
 
-def columns(src, dst, sem, spans):
-    copies = []
-    at = 0
-    for k, (start, width) in enumerate(spans):
-        copies.append(
-            pltpu.make_async_copy(
-                src.at[:, pl.ds(start, width)], dst.at[:, pl.ds(at, width)], sem.at[k]
-            )
-        )
-        copies[-1].start()
-        at += width
-    return copies
-
-
 def embed_tile(x, weights, lat_hbm, act_ref, buf, sem, row, point):
     latent, act = act_of(x, TN, *weights)
     rows = pl.ds(row, x.shape[1])
@@ -297,11 +283,10 @@
 
 
 def first_kernel(
-    x_ref, tail_ref, src_ref, w_in, b_in, b_msg, w_out_hbm, w_msg_hbm, s_hbm, lat_ref, sum_ref, own_ref,
-    s_buf, act_buf, buf, w_out, w_msg, far_hot, sem, in_sem, w_sem, *, spans,
+    x_ref, tail_ref, src_ref, w_in, b_in, b_msg, w_out_hbm, w_msg_hbm, lat_ref, act_hbm, own_ref,
+    act_buf, buf, w_out, w_msg, far_hot, sem, w_sem, act_sem, *, point,
 ):
     w_loads = whole_copies(((w_out_hbm, w_out), (w_msg_hbm, w_msg)), w_sem)
-    loads = columns(s_hbm, s_buf, in_sem, spans)
     hots(src_ref[...], far_hot)
     main = x_ref.shape[1]
     far = dot(x_ref[...], far_hot[:main]) + dot(tail_ref[...], far_hot[main:])
@@ -309,89 +294,108 @@
     for c in w_loads:
         c.wait()
     weights = (w_in, b_in, w_out, w_msg, b_msg)
-    stores = embed_tile(tail_ref[...], weights, lat_ref, act_buf, buf, sem, 0, spans[0][0])
-    for c in loads:
-        c.wait()
-    sum_ref[...] = dot(s_buf[...], act_buf[...])
+    stores = embed_tile(tail_ref[...], weights, lat_ref, act_buf, buf, sem, 0, point)
+    stores.append(pltpu.make_async_copy(act_buf, act_hbm, act_sem))
+    stores[-1].start()
     for c in stores:
         c.wait()
 
 
 def second_kernel(
-    low_ref, up_ref, w_both, w_in, b_in, b_msg, w_out_hbm, w_msg_hbm, s_hbm, before, x_hbm, _, lat_ref, sum_ref,
-    s_buf, act_buf, buf, w_out, w_msg, x_buf, sem, in_sem, w_sem, x_sem, *, spans, tile,
+    low_ref, up_ref, w_both, w_in, b_in, b_msg, w_out_hbm, w_msg_hbm, s_hbm, act_hbm, x_hbm, _, lat_ref, sum_ref,
+    act_buf, buf, w_out, w_msg, s_buf, x_buf, sem, w_sem, in_sem, *, tile,
 ):
     half = low_ref.shape[1]
-    x_load = columns(x_hbm, x_buf, x_sem, spans[:1])
-    w_loads = whole_copies(((w_out_hbm, w_out), (w_msg_hbm, w_msg), (before, sum_ref)), w_sem)
-    loads = columns(s_hbm, s_buf, in_sem, spans)
-    start, width = spans[0]
+    width = x_hbm.shape[1]
+    pts = width + act_hbm.shape[0]
+    x_load = whole_copies(((x_hbm, x_buf),), in_sem)[0]
+    w_loads = whole_copies(((w_out_hbm, w_out), (w_msg_hbm, w_msg)), w_sem)
+    s_load = pltpu.make_async_copy(s_hbm, s_buf, in_sem.at[1])
+    act_load = pltpu.make_async_copy(act_hbm, act_buf.at[pl.ds(width, pts - width)], in_sem.at[2])
+    s_load.start()
+    act_load.start()
     halo = jnp.concatenate([low_ref[...], up_ref[...]], axis=1)
-    act_buf[pl.ds(width, 2 * half)] = act_only(halo, TN, w_in, b_in, w_both, b_msg)
-    x_load[0].wait()
+    act_buf[pl.ds(pts, 2 * half)] = act_only(halo, TN, w_in, b_in, w_both, b_msg)
+    x_load.wait()
     for c in w_loads:
         c.wait()
     weights = (w_in, b_in, w_out, w_msg, b_msg)
     stores = []
     for p in range(0, width, tile):
         x = x_buf[:, p : min(p + tile, width)]
-        stores += embed_tile(x, weights, lat_ref, act_buf, buf, sem, p, start + p)
-    for c in loads:
-        c.wait()
-    sum_ref[...] += dot(s_buf[...], act_buf[...])
+        stores += embed_tile(x, weights, lat_ref, act_buf, buf, sem, p, p)
+    s_load.wait()
+    act_load.wait()
+    sum_ref[...] = dot(s_buf[...], act_buf[...])
     for c in stores:
         c.wait()
 
 
-def embed(x, counts, weights, later, pts, spans, tile, tail=None, src=None, before=None):
-    rows = x.shape[0]
-    nodes = counts.shape[0]
-    w_in, b_in, w_both, b_msg = weights
-    lat = w_in.shape[1]
-    wide = sum(width for _, width in spans)
-    held = at_vmem(w_in, b_in, b_msg)
-    remote = [at_hbm(a) for a in (*later, counts)]
-    if before is None:
-        kernel = functools.partial(first_kernel, spans=spans)
-        span = wide
-        args = [*at_vmem(x, tail), src, *held, *remote]
-        specs = [VM] * 6 + [ANY] * 3
-        alias = {}
-        inner = [pltpu.VMEM((pts, src.shape[1]), BF)]
-        sems = []
-        more = [pltpu.VMEM((rows, src.shape[1]), BF)]
-    else:
-        kernel = functools.partial(second_kernel, spans=spans, tile=tile)
-        span = spans[0][1]
-        latent, total, low, up = before
-        args = [*at_vmem(low, up, w_both), *held, *remote, at_hbm(total), at_hbm(x), at_hbm(latent)]
-        specs = [VM] * 6 + [ANY] * 6
-        alias = {11: 0}
-        inner = [pltpu.VMEM((rows, span), BF)]
-        sems = [pltpu.SemaphoreType.DMA((1,))]
-        more = []
+def embed_call(kernel, args, specs, out_shape, out_specs, span, acts, lat, inner, sems, alias, flops):
     return pl.pallas_call(
         kernel,
         in_specs=specs,
-        out_specs=[ANY, VM] + [VM] * len(more),
-        out_shape=(pltpu.HBM((pts, lat), BF), pltpu.VMEM((nodes, lat), F32), *more),
+        out_specs=[ANY, *out_specs],
+        out_shape=out_shape,
         scratch_shapes=[
-            pltpu.VMEM((nodes, wide), BF),
-            pltpu.VMEM((wide, lat), BF),
+            pltpu.VMEM((acts, lat), BF),
             pltpu.VMEM((span, lat), BF),
             pltpu.VMEM((lat, lat), BF),
             pltpu.VMEM((lat, lat), BF),
             *inner,
-            pltpu.SemaphoreType.DMA((span // PIECE,)),
-            pltpu.SemaphoreType.DMA((len(spans),)),
-            pltpu.SemaphoreType.DMA((3,)),
+            pltpu.SemaphoreType.DMA((-(-span // PIECE),)),
+            pltpu.SemaphoreType.DMA((2,)),
             *sems,
         ],
         input_output_aliases=alias,
         compiler_params=params(28),
-        cost_estimate=cost(2 * span * lat * (rows + 2 * lat + nodes), span * (rows + lat) * 2),
+        cost_estimate=cost(flops, span * lat * 4),
         name="embed",
     )(*args)
+
+
+def embed_first(x, tail, src, weights, later):
+    w_in, b_in, _, b_msg = weights
+    rows, main = x.shape
+    span = tail.shape[1]
+    pts = main + span
+    lat = w_in.shape[1]
+    slots = src.shape[1]
+    return embed_call(
+        functools.partial(first_kernel, point=main),
+        [*at_vmem(x, tail), src, *at_vmem(w_in, b_in, b_msg), *map(at_hbm, later)],
+        [VM] * 6 + [ANY] * 2,
+        (pltpu.HBM((pts, lat), BF), pltpu.HBM((span, lat), BF), pltpu.VMEM((rows, slots), BF)),
+        [ANY, VM],
+        span,
+        span,
+        lat,
+        [pltpu.VMEM((pts, slots), BF)],
+        [pltpu.SemaphoreType.DMA],
+        {},
+        2 * rows * pts * slots + 2 * span * lat * (rows + 2 * lat),
+    )
+
+
+def embed_second(x, counts, weights, later, latent, acts, low, up, tile):
+    w_in, b_in, w_both, b_msg = weights
+    rows, main = x.shape
+    nodes, table = counts.shape
+    lat = w_in.shape[1]
+    return embed_call(
+        functools.partial(second_kernel, tile=tile),
+        [*at_vmem(low, up, w_both, w_in, b_in, b_msg), *map(at_hbm, (*later, counts, acts, x, latent))],
+        [VM] * 6 + [ANY] * 6,
+        (pltpu.HBM(latent.shape, BF), pltpu.VMEM((nodes, lat), F32)),
+        [VM],
+        main,
+        table,
+        lat,
+        [pltpu.VMEM((nodes, table), BF), pltpu.VMEM((rows, main), BF)],
+        [pltpu.SemaphoreType.DMA((3,))],
+        {11: 0},
+        2 * main * lat * (rows + 2 * lat) + 2 * nodes * table * lat,
+    )
 
 
 def node_kernel(r_ref, w_in, b_in, w_both, b_msg, sum_ref, *rest, pad):
@@ -501,25 +505,15 @@
     from_low = lax.ppermute(high, "tile", ahead)
     from_up = lax.ppermute(low, "tile", back)
 
-    tile = 2 * PIECE
-    latent, total, own = embed(
-        x, counts, weights, later, pts, ((main, pts - main),), tile, tail, src
-    )
+    latent, acts, own = embed_first(x, tail, src, weights, later)
 
     rows = slots_rows(own, from_low, from_up, src, dst, pts, chans)
     rows = lax.all_to_all(
         rows.reshape(levels, slot_count, wide), "lev", split_axis=0, concat_axis=0, tiled=True
     ).reshape(levels * slot_count, wide)
 
-    latent, total = embed(
-        x,
-        counts,
-        weights,
-        later,
-        pts,
-        ((0, main), (pts, 2 * halo)),
-        tile,
-        before=(latent, total, from_low, from_up),
+    latent, total = embed_second(
+        x, counts, weights, later, latent, acts, from_low, from_up, 2 * PIECE
     )
     mesh_out = node_update(
         rows, weights, total, w_msg_out, mesh_nodes, pre, w_nb, w_node_out, chans

time: 83.3 us -> 67.5 us (0.81)
  waiting for transfers between devices: 25.7 us -> 8.62 us
  Pallas kernels: 37.9 us -> 39.4 us
    all_to_all x1, waiting for transfers between devices: 25.5 us -> 8.61 us  [shards(): got = lax.all_to_all(sent, 'lev', split_axis=0, concat_axis=0, tiled=True)]
    pallas_call x2, Pallas kernels: 11.4 us -> 12.8 us  [embed_call(): pl.pallas_call(kernel, in_specs=specs, out_specs=[ANY, *out_specs], out_s...]
  transfers between devices with their start and end apart: 4 -> 4, of which waited for: 2 -> 1; matrix products, arithmetic and copies ran while one was open for 0% -> 0% of each run, Pallas kernels for 34% -> 44%
where the time goes in v10:
time: 67.5 us; the launch traced here: 67.1 us
  Pallas kernels  39.4 us (58%)
  starting transfers between devices  17.7 us (26%)
  waiting for transfers between devices  8.62 us (13%)
  between operations  1.05 us (2%)
    pallas_call x1, Pallas kernels, count_edges(): pl.pallas_call(functools.partial(count_kernel, chans=chans), in_specs=[VM...  16.8 us
    pallas_call x2, Pallas kernels, embed_call(): pl.pallas_call(kernel, in_specs=specs, out_specs=[ANY, *out_specs], out_s...  12.8 us
    all_to_all x1, waiting for transfers between devices, shards(): got = lax.all_to_all(sent, 'lev', split_axis=0, concat_axis=0, tiled=True)  8.61 us
    all_to_all x1, starting transfers between devices, shards(): got = lax.all_to_all(sent, 'lev', split_axis=0, concat_axis=0, tiled=True)  8.59 us
    all_to_all x1, starting transfers between devices, shards(): lax.all_to_all(rows.reshape(levels, slot_count, wide), 'lev', split_axis=...  5.25 us
    pallas_call x1, Pallas kernels, pack(): pl.pallas_call(functools.partial(pack_kernel, parts=parts), in_specs=[sme...  4.05 us
    pallas_call x1, Pallas kernels, node_update(): pl.pallas_call(functools.partial(node_kernel, pad=pad), in_specs=[VM] * l...  3.12 us
    ppermute x1, starting transfers between devices, shards(): from_up = lax.ppermute(low, 'tile', back)  2.2 us
  transfers between devices with their start and end apart: 4, of which 1 were waited for; matrix products, arithmetic and copies ran while one was open for 0% of the time, Pallas kernels for 44%

profile of v10, /device:TPU:1, one launch (start us, length us, event | category | flops | bytes accessed | tf_op | source)
XLA Modules:
  0.0 67.1 jit_solution(1554799933157534077)
XLA Ops:
  0.6 0.0 copy-start.8
  0.6 0.0 copy-start.9
  0.7 0.0 copy-start.10
  0.7 0.0 copy-start.1
  0.7 0.0 copy-start.2
  0.7 0.0 copy-start.3
  0.7 0.0 copy-start.4
  0.7 0.0 copy-start.5
  0.7 0.0 copy-start.6
  0.7 0.0 copy-start.7
  0.7 4.1 %pack.1 = bf16[32,8,3584]{2,1,0:T(8,128)(2,1)} custom-call(s32[1]{0:T(128)} %bitcast.me_ref, f32[224]{0:T(256)} %mean_ref.1, f32[224]{0:T(256)} %scale_ref.1, f32[7,131072]{1,0:T(8,128)} %x_ref.1), custom_call_target="tpu_custom_call" | custom-call | flops 2097152 | bytes 6291456 | tf_op jit(solution)/shard_map/pack/pallas_call | solution.py:92
  4.8 8.6 %all-to-all-start = ((bf16[32,8,3584]{2,1,0:T(8,128)(2,1)}), bf16[32,8,3584]{2,1,0:T(8,128)(2,1)S(1)}, u32[]{:S(2)}, u32[]{:S(2)}) async-start(bf16[32,8,3584]{2,1,0:T(8,128)(2,1)} %pack.1), calls=%async_computation | async-start | bytes 3670016 | tf_op jit(solution)/shard_map/all_to_all | solution.py:476
  13.4 0.0 copy-done.8
  13.4 0.1 copy.23
  13.5 0.1 reshape.27.src_ref
  13.6 0.0 copy-done.9
  13.6 0.1 copy.24
  13.6 0.1 reshape.28.dst_ref
  13.7 0.0 copy-done.10
  13.7 0.0 copy-done.1
  13.8 0.0 copy-done.2
  13.8 0.0 copy-done.3
  13.8 0.0 copy-done.4
  13.8 0.0 copy-done.5
  13.8 0.0 copy-done.6
  13.8 0.0 copy-done.7
  13.8 16.8 %count.1 = (bf16[320,4608]{1,0:T(8,128)(2,1)}, bf16[256,512]{1,0:T(8,128)(2,1)S(1)}, f32[320,512]{1,0:T(8,128)}, bf16[512,512]{1,0:T(8,128)(2,1)}, bf16[512,512]...) custom-call(s32[1,4096]{1,0:T(1,128)S(1)} %copy-done.3, ...), custom_call_target="tpu_custom_call" | custom-call | flops 12079595520 | bytes 2949120 | tf_op jit(solution)/shard_map/count/pallas_call | solution.py:159
  30.6 8.6 %all-to-all-done = bf16[32,8,3584]{2,1,0:T(8,128)(2,1)S(1)} async-done(((bf16[32,8,3584]{2,1,0:T(8,128)(2,1)}), bf16[32,8,3584]{2,1,0:T(8,128)(2,1)S(1)}, u32[]{:S(2)}, u32[]{:S(2)}) %all-to-all-start) | async-done | bytes 1835040 | tf_op jit(solution)/shard_map/all_to_all | solution.py:476
  39.2 0.0 copy-start
  39.2 1.5 %select.1 = (bf16[256,256]{1,0:T(8,128)(2,1)S(1)}, bf16[256,256]{1,0:T(8,128)(2,1)S(1)}, bf16[256,512]{1,0:T(8,128)(2,1)S(1)}) custom-call(bf16[256,3584]{1,0:T(8,128)(2,1)S(1)} %bitcast.9, s32[1,512]{1,0:T(1,128)S(1)} %bitcast.13), custom_call_target="tpu_custom_call" | custom-call | flops 1073741824 | bytes 2097152 | tf_op jit(solution)/shard_map/select/pallas_call | solution.py:217
  40.7 1.7 %collective-permute-start = (bf16[256,256]{1,0:T(8,128)(2,1)S(1)}, bf16[256,256]{1,0:T(8,128)(2,1)S(1)}, u32[]{:S(2)}, u32[]{:S(2)}) collective-permute-start(bf16[256,256]{1,0:T(8,128)(2,1)S(1)} %get-tuple-element.23), channel_id=1, source_target_pairs={{0,32},{32,64},{64,96},{96,0},{1,33},{33,65},{65,97},{97,1},{2,34}... | collective-permute-start | bytes 393224 | tf_op jit(solution)/shard_map/ppermute | solution.py:505
  42.4 2.2 %collective-permute-start.1 = (bf16[256,256]{1,0:T(8,128)(2,1)S(1)}, bf16[256,256]{1,0:T(8,128)(2,1)S(1)}, u32[]{:S(2)}, u32[]{:S(2)}) collective-permute-start(bf16[256,256]{1,0:T(8,128)(2,1)S(1)} %get-tuple-element.24), channel_id=1, source_target_pairs={{32,0},{64,32},{96,64},{0,96},{33,1},{65,33},{97,65},{1,97},{34,2}... | collective-permute-start | bytes 393224 | tf_op jit(solution)/shard_map/ppermute | solution.py:506
  44.6 3.0 %embed.2 = (bf16[4096,512]{1,0:T(8,128)(2,1)}, bf16[512,512]{1,0:T(8,128)(2,1)}, bf16[256,512]{1,0:T(8,128)(2,1)S(1)}) custom-call(bf16[256,3584]{1,0:T(8,128)(2,1)S(1)} %bitcast.10, bf16[256,512]{1,0:T(8,128)(2,1)S(1)} %get-tuple-element.32.tail_ref, s32[1,512]{1,0:T(1,128)S(1)} %reshape.27.src_ref, bf16[256,512]{1,0:T(8,128)(2,1)S(1)} %get-tuple-element.27.w_in, ...), custom_call_target="tpu_custom_call" | custom-call | flops 1744830464 | bytes 1048576 | tf_op jit(solution)/shard_map/embed/pallas_call | solution.py:335
  47.7 0.0 copy-done
  47.7 0.0 collective-permute-done.low_ref
  47.7 0.0 collective-permute-done.1.up_ref
  47.7 1.1 %slots.1 = bf16[512,256]{1,0:T(8,128)(2,1)} custom-call(bf16[256,512]{1,0:T(8,128)(2,1)S(1)} %get-tuple-element.37.own_ref, bf16[256,256]{1,0:T(8,128)(2,1)S(1)} %collective-permute-done.low_ref, bf16[256,256]{1,0:T(8,128)(2,1)S(1)} %collective-permute-done.1.up_ref, s32[1,512]{1,0:T(1,128)S(1)} %reshape.27.src_ref, s32[1,512]{1,0:T(1,128)S(1)} %reshape.28.dst_ref), custom_call_target="tpu_custom_call" | custom-call | flops 134217728 | bytes 524288 | tf_op jit(solution)/shard_map/slots/pallas_call | solution.py:245
  48.8 5.2 %all-to-all-start.1 = ((bf16[32,16,256]{2,1,0:T(8,128)(2,1)}), bf16[32,16,256]{2,1,0:T(8,128)(2,1)S(1)}, u32[]{:S(2)}, u32[]{:S(2)}) async-start(bf16[32,16,256]{2,1,0:T(8,128)(2,1)} %bitcast.5), calls=%async_computation.1 | async-start | bytes 524288 | tf_op jit(solution)/shard_map/all_to_all | solution.py:511
  54.0 9.8 %embed.3 = (bf16[4096,512]{1,0:T(8,128)(2,1)}, f32[320,512]{1,0:T(8,128)S(1)}) custom-call(bf16[256,256]{1,0:T(8,128)(2,1)S(1)} %collective-permute-done.low_ref, bf16[256,256]{1,0:T(8,128)(2,1)S(1)} %collective-permute-done.1.up_ref, bf16[512,512]{1,0:T(8,128)(2,1)S(1)} %get-tuple-element.26.w_both, ...), custom_call_target="tpu_custom_call", output_to_operand_aliasing={{0}: (11, {})} | custom-call | flops 6207569920 | bytes 7340032 | tf_op jit(solution)/shard_map/embed/pallas_call | solution.py:335
  63.9 0.0 all-to-all-done.1
  63.9 3.1 %node.1 = bf16[320,512]{1,0:T(8,128)(2,1)} custom-call(bf16[512,256]{1,0:T(8,128)(2,1)S(1)} %bitcast.12, bf16[256,512]{1,0:T(8,128)(2,1)S(1)} %get-tuple-element.27.w_in, f32[1,512]{1,0:T(1,128)S(1)} %get-tuple-element.28.b_in, bf16[512,512]{1,0:T(8,128)(2,1)S(1)} %get-tuple-element.26.w_both, f32[1,512]{1,0:T(1,128)S(1)} %get-tuple-element.29.b_msg, ...), custom_call_target="tpu_custom_call" | custom-call | flops 805306368 | bytes 3145728 | tf_op jit(solution)/shard_map/node/pallas_call | solution.py:432
  (1 shorter events, 0.0 us)
Async XLA Ops:
  0.6 12.8 %copy-start.8 = (s32[1,32,16]{1,2,0:T(8,128)S(1)}, s32[1,32,16]{1,2,0:T(8,128)}, u32[]{:S(2)}) copy-start(s32[1,32,16]{1,2,0:T(8,128)} %param.27) | copy-start | bytes 6148
  0.6 12.9 %copy-start.9 = (s32[1,32,16]{1,2,0:T(8,128)S(1)}, s32[1,32,16]{1,2,0:T(8,128)}, u32[]{:S(2)}) copy-start(s32[1,32,16]{1,2,0:T(8,128)} %param.28) | copy-start | bytes 6148
  0.7 13.1 %copy-start.10 = (s32[1,2,256]{2,1,0:T(2,128)S(1)}, s32[1,2,256]{2,1,0:T(2,128)}, u32[]{:S(2)}) copy-start(s32[1,2,256]{2,1,0:T(2,128)} %param.24) | copy-start | bytes 6148
  0.7 13.1 %copy-start.1 = (bf16[320,512]{1,0:T(8,128)(2,1)S(1)}, bf16[320,512]{1,0:T(8,128)(2,1)}, u32[]{:S(2)}) copy-start(bf16[320,512]{1,0:T(8,128)(2,1)} %rest_4_.1) | copy-start | bytes 983044
  0.7 13.1 %copy-start.2 = (bf16[224,512]{1,0:T(8,128)(2,1)S(1)}, bf16[224,512]{1,0:T(8,128)(2,1)}, u32[]{:S(2)}) copy-start(bf16[224,512]{1,0:T(8,128)(2,1)} %w_ref.1) | copy-start | bytes 688132
  0.7 13.1 %copy-start.3 = (s32[1,4096]{1,0:T(1,128)S(1)}, s32[1,4096]{1,0:T(1,128)}, u32[]{:S(2)}) copy-start(s32[1,4096]{1,0:T(1,128)} %src_ref) | copy-start | bytes 49156
  0.7 13.1 %copy-start.4 = (s32[1,4096]{1,0:T(1,128)S(1)}, s32[1,4096]{1,0:T(1,128)}, u32[]{:S(2)}) copy-start(s32[1,4096]{1,0:T(1,128)} %dst_ref.1) | copy-start | bytes 49156
  0.7 13.1 %copy-start.5 = (f32[512]{0:T(512)S(1)}, f32[512]{0:T(512)}, u32[]{:S(2)}) copy-start(f32[512]{0:T(512)} %param.22) | copy-start | bytes 6148
  0.7 13.1 %copy-start.6 = (f32[512]{0:T(512)S(1)}, f32[512]{0:T(512)}, u32[]{:S(2)}) copy-start(f32[512]{0:T(512)} %param.34) | copy-start | bytes 6148
  0.7 13.1 %copy-start.7 = (f32[512]{0:T(512)S(1)}, f32[512]{0:T(512)}, u32[]{:S(2)}) copy-start(f32[512]{0:T(512)} %param.30) | copy-start | bytes 6148
  4.8 34.4 %all-to-all-start = ((bf16[32,8,3584]{2,1,0:T(8,128)(2,1)}), bf16[32,8,3584]{2,1,0:T(8,128)(2,1)S(1)}, u32[]{:S(2)}, u32[]{:S(2)}) async-start(bf16[32,8,3584]{2,1,0:T(8,128)(2,1)} %pack.1), calls=%async_computation | async-start | bytes 3670016 | tf_op jit(solution)/shard_map/all_to_all | solution.py:476
  39.2 8.4 %copy-start = (bf16[32,8,3584]{2,1,0:T(8,128)(2,1)}, bf16[32,8,3584]{2,1,0:T(8,128)(2,1)S(1)}, u32[]{:S(2)}) copy-start(bf16[32,8,3584]{2,1,0:T(8,128)(2,1)S(1)} %all-to-all-done) | copy-start | bytes 5505028
  40.7 6.9 %collective-permute-start = (bf16[256,256]{1,0:T(8,128)(2,1)S(1)}, bf16[256,256]{1,0:T(8,128)(2,1)S(1)}, u32[]{:S(2)}, u32[]{:S(2)}) collective-permute-start(bf16[256,256]{1,0:T(8,128)(2,1)S(1)} %get-tuple-element.23), channel_id=1, source_target_pairs={{0,32},{32,64},{64,96},{96,0},{1,33},{33,65},{65,97},{97,1},{2,34}... | collective-permute-start | bytes 393224 | tf_op jit(solution)/shard_map/ppermute | solution.py:505
  42.4 5.2 %collective-permute-start.1 = (bf16[256,256]{1,0:T(8,128)(2,1)S(1)}, bf16[256,256]{1,0:T(8,128)(2,1)S(1)}, u32[]{:S(2)}, u32[]{:S(2)}) collective-permute-start(bf16[256,256]{1,0:T(8,128)(2,1)S(1)} %get-tuple-element.24), channel_id=1, source_target_pairs={{32,0},{64,32},{96,64},{0,96},{33,1},{65,33},{97,65},{1,97},{34,2}... | collective-permute-start | bytes 393224 | tf_op jit(solution)/shard_map/ppermute | solution.py:506
  48.8 15.1 %all-to-all-start.1 = ((bf16[32,16,256]{2,1,0:T(8,128)(2,1)}), bf16[32,16,256]{2,1,0:T(8,128)(2,1)S(1)}, u32[]{:S(2)}, u32[]{:S(2)}) async-start(bf16[32,16,256]{2,1,0:T(8,128)(2,1)} %bitcast.5), calls=%async_computation.1 | async-start | bytes 524288 | tf_op jit(solution)/shard_map/all_to_all | solution.py:511
